TPU v7x, 256 devices: a whole 4x4x8 slice. The times are simulated.
256 devices in a mesh: hid: 32 (over x, z), tok: 8 (over y, core).
Axes of the slice: x: 4, y: 4, z: 8, core: 2. Of those that a mesh axis runs over, the one named last changes fastest.
Arguments:
- tokens: bfloat16 [2048, 12288], P('tok', 'hid'), may hold values from -6 to 6
- cotangent: bfloat16 [2048, 12288], P('tok', 'hid'), may hold values from -0.75 to 0.75
- up_tiles: bfloat16 [6, 256, 24576], P(None, None, 'hid'), may hold values from -0.15625 to 0.15625
- down_tiles: bfloat16 [6, 24576, 256], P(None, 'hid'), may hold values from -0.109375 to 0.109375
- block_index: int32 [6, 96, 2], P(None, 'hid'), may hold values from 0 to 2, as said below
- up_left: bfloat16 [12288, 256], P('hid'), may hold values from -0.0546875 to 0.0546875
- up_right: bfloat16 [256, 24576], P(None, 'hid'), may hold values from -0.375 to 0.375
- down_left: bfloat16 [24576, 256], P('hid'), may hold values from -0.0390625 to 0.0390625
- down_right: bfloat16 [256, 12288], P(None, 'hid'), may hold values from -0.375 to 0.375
Outputs:
- layer_out: bfloat16 [2048, 12288], P('tok', 'hid')
- grad_tokens: bfloat16 [2048, 12288], P('tok', 'hid')
- grad_up_tiles: bfloat16 [6, 256, 24576], P(None, 'tok', 'hid')
- grad_down_tiles: bfloat16 [6, 24576, 256], P(None, ('hid', 'tok'))
- grad_up_left: bfloat16 [12288, 256], P(('hid', 'tok'))
- grad_up_right: bfloat16 [256, 24576], P('tok', 'hid')
- grad_down_left: bfloat16 [24576, 256], P(('hid', 'tok'))
- grad_down_right: bfloat16 [256, 12288], P('tok', 'hid')
Inputs may be any that keep to these rules, and one draw needn't show every extreme that they name: `block_index`: each row names two different sub-blocks.
All inputs are finite; a program needn't handle non-finite values.
Results may differ from a plain program's by a relative error of at most 0.03.
Values may be sent and summed in bfloat16 or wider, within the bound.
No kernel may reach another device: no remote copies, remote signals or barrier semaphores. Data moves between devices by JAX's collectives and lax.ppermute only.
A program may use at most 128 MiB of HBM per device.

v0:
```python
import jax
import jax.numpy as jnp
from jax import lax
from jax.sharding import PartitionSpec as P

GELU_SCALE = 0.7978845608028654
GELU_CUBIC = 0.044715


def partner(block, axis, distance):
    count = lax.axis_size(axis)
    route = []
    for low in range(count):
        high = low | 1 << distance
        if high != low and high < count:
            route += [(low, high), (high, low)]
    return lax.ppermute(block, axis, route)


def gelu_parts(pre_act):
    inner = GELU_SCALE * (pre_act + GELU_CUBIC * pre_act * pre_act * pre_act)
    tanh_value = jnp.tanh(inner)
    value = 0.5 * pre_act * (1.0 + tanh_value)
    slope = 0.5 * (1.0 + tanh_value) + 0.5 * pre_act * (
        1.0 - tanh_value * tanh_value
    ) * GELU_SCALE * (1.0 + 3.0 * GELU_CUBIC * pre_act * pre_act)
    return (value, slope)


def on_device(
    tokens, cotangent, up_tiles, down_tiles, block_index, up_left, up_right, down_left, down_right
):
    hid_count = lax.axis_size("hid")
    level_count = hid_count.bit_length()
    position = lax.axis_index("hid")
    token_rows, feat_width = tokens.shape
    sub_width = feat_width // 3
    block_count = block_index.shape[1]
    hidden_width = up_tiles.shape[2]
    block_width = hidden_width // block_count
    select_float_values = (block_index[..., None] == jnp.arange(3, dtype=jnp.int32)).astype(
        jnp.float32
    )
    select_half_values = select_float_values.astype(jnp.bfloat16)
    up_blocks = [
        up_tiles[partition_key].reshape(2, sub_width, block_count, block_width)
        for partition_key in range(level_count)
    ]
    down_blocks = [
        down_tiles[partition_key].reshape(block_count, block_width, 2, sub_width)
        for partition_key in range(level_count)
    ]

    def partner_of(partition_key):
        if partition_key == 0:
            return position
        return jnp.bitwise_xor(position, jnp.int32(1 << partition_key - 1))

    def choose(field, partition_key):
        reshaped_tiles = field.reshape(token_rows, 3, sub_width)
        return jnp.einsum(
            "rfg,hyf->rhyg",
            reshaped_tiles,
            select_half_values[partition_key],
            preferred_element_type=jnp.float32,
        ).astype(jnp.bfloat16)

    def place(partner_pairs, partition_key):
        placed_blocks = jnp.einsum(
            "kdow,dog->kgw",
            partner_pairs,
            select_float_values[partition_key],
            precision=lax.Precision.HIGHEST,
        )
        return placed_blocks.reshape(token_rows, feat_width).astype(jnp.bfloat16)

    gathered = lax.all_gather(tokens, "hid", axis=1, tiled=True)
    feature_copies = [
        lax.dynamic_slice_in_dim(gathered, partner_of(partition_key) * feat_width, feat_width, 1)
        for partition_key in range(level_count)
    ]
    low_up = lax.psum(
        jnp.dot(tokens, up_left, preferred_element_type=jnp.float32).astype(jnp.bfloat16), "hid"
    )
    chosen_inputs = [
        choose(feature_copies[partition_key], partition_key) for partition_key in range(level_count)
    ]
    pre_act = jnp.dot(low_up, up_right, preferred_element_type=jnp.float32).reshape(
        token_rows, block_count, block_width
    )
    for partition_key in range(level_count):
        pre_act = pre_act + jnp.einsum(
            "tbjs,jsbh->tbh",
            chosen_inputs[partition_key],
            up_blocks[partition_key],
            preferred_element_type=jnp.float32,
        )
    hidden_value, slope = gelu_parts(pre_act)
    hidden_act = hidden_value.astype(jnp.bfloat16)
    hidden_flat = hidden_act.reshape(token_rows, hidden_width)
    low_down = lax.psum(
        jnp.dot(hidden_flat, down_left, preferred_element_type=jnp.float32).astype(jnp.bfloat16),
        "hid",
    )
    out_parts = [
        place(
            jnp.einsum(
                "tbh,bhjs->tbjs",
                hidden_act,
                down_blocks[partition_key],
                preferred_element_type=jnp.float32,
            ),
            partition_key,
        )
        for partition_key in range(level_count)
    ]
    output_acc = out_parts[0].astype(jnp.float32)
    for partition_key in range(1, level_count):
        output_acc = output_acc + partner(
            out_parts[partition_key], "hid", partition_key - 1
        ).astype(jnp.float32)
    layer_out = (
        output_acc + jnp.dot(low_down, down_right, preferred_element_type=jnp.float32)
    ).astype(jnp.bfloat16)
    back_down = lax.psum(
        jnp.dot(cotangent, down_right.T, preferred_element_type=jnp.float32).astype(jnp.bfloat16),
        "hid",
    )
    grad_gathered = lax.all_gather(cotangent, "hid", axis=1, tiled=True)
    grad_copies = [
        lax.dynamic_slice_in_dim(
            grad_gathered, partner_of(partition_key) * feat_width, feat_width, 1
        )
        for partition_key in range(level_count)
    ]
    chosen_grads = [
        choose(grad_copies[partition_key], partition_key) for partition_key in range(level_count)
    ]
    grad_hidden = jnp.dot(back_down, down_left.T, preferred_element_type=jnp.float32).reshape(
        token_rows, block_count, block_width
    )
    for partition_key in range(level_count):
        grad_hidden = grad_hidden + jnp.einsum(
            "tbjs,bhjs->tbh",
            chosen_grads[partition_key],
            down_blocks[partition_key],
            preferred_element_type=jnp.float32,
        )
    down_terms = jnp.stack(
        [
            jnp.einsum(
                "tbh,tbjs->bhjs",
                hidden_act,
                chosen_grads[partition_key],
                preferred_element_type=jnp.float32,
            ).reshape(hidden_width, 2 * sub_width)
            for partition_key in range(level_count)
        ]
    )
    down_left_term = jnp.dot(hidden_flat.T, back_down, preferred_element_type=jnp.float32)
    down_right_term = jnp.dot(low_down.T, cotangent, preferred_element_type=jnp.float32)
    grad_down_tiles, grad_down_left, grad_down_right = (
        lax.psum_scatter(
            down_terms.astype(jnp.bfloat16), "tok", scatter_dimension=1, tiled=True
        ).astype(jnp.float32),
        lax.psum_scatter(
            down_left_term.astype(jnp.bfloat16), "tok", scatter_dimension=0, tiled=True
        ).astype(jnp.float32),
        lax.psum_scatter(
            down_right_term.astype(jnp.bfloat16), "tok", scatter_dimension=0, tiled=True
        ).astype(jnp.float32),
    )
    grad_pre = (grad_hidden * slope).astype(jnp.bfloat16)
    grad_flat = grad_pre.reshape(token_rows, hidden_width)
    back_up = lax.psum(
        jnp.dot(grad_flat, up_right.T, preferred_element_type=jnp.float32).astype(jnp.bfloat16),
        "hid",
    )
    in_parts = [
        place(
            jnp.einsum(
                "tbh,jsbh->tbjs",
                grad_pre,
                up_blocks[partition_key],
                preferred_element_type=jnp.float32,
            ),
            partition_key,
        )
        for partition_key in range(level_count)
    ]
    input_acc = in_parts[0].astype(jnp.float32)
    for partition_key in range(1, level_count):
        input_acc = input_acc + partner(in_parts[partition_key], "hid", partition_key - 1).astype(
            jnp.float32
        )
    grad_tokens = (
        input_acc + jnp.dot(back_up, up_left.T, preferred_element_type=jnp.float32)
    ).astype(jnp.bfloat16)
    up_terms = jnp.stack(
        [
            jnp.einsum(
                "tbjs,tbh->jsbh",
                chosen_inputs[partition_key],
                grad_pre,
                preferred_element_type=jnp.float32,
            ).reshape(2 * sub_width, hidden_width)
            for partition_key in range(level_count)
        ]
    )
    up_right_term = jnp.dot(low_up.T, grad_flat, preferred_element_type=jnp.float32)
    up_left_term = jnp.dot(tokens.T, back_up, preferred_element_type=jnp.float32)
    grad_up_tiles, grad_up_right, grad_up_left = (
        lax.psum_scatter(
            up_terms.astype(jnp.bfloat16), "tok", scatter_dimension=1, tiled=True
        ).astype(jnp.float32),
        lax.psum_scatter(
            up_right_term.astype(jnp.bfloat16), "tok", scatter_dimension=0, tiled=True
        ).astype(jnp.float32),
        lax.psum_scatter(
            up_left_term.astype(jnp.bfloat16), "tok", scatter_dimension=0, tiled=True
        ).astype(jnp.float32),
    )
    return (
        layer_out,
        grad_tokens,
        grad_up_tiles.astype(jnp.bfloat16),
        grad_down_tiles.astype(jnp.bfloat16),
        grad_up_left.astype(jnp.bfloat16),
        grad_up_right.astype(jnp.bfloat16),
        grad_down_left.astype(jnp.bfloat16),
        grad_down_right.astype(jnp.bfloat16),
    )


def solution(mesh):
    return jax.shard_map(
        on_device,
        mesh=mesh,
        in_specs=(
            P("tok", "hid"),
            P("tok", "hid"),
            P(None, None, "hid"),
            P(None, "hid", None),
            P(None, "hid", None),
            P("hid", None),
            P(None, "hid"),
            P("hid", None),
            P(None, "hid"),
        ),
        out_specs=(
            P("tok", "hid"),
            P("tok", "hid"),
            P(None, "tok", "hid"),
            P(None, ("hid", "tok"), None),
            P(("hid", "tok"), None),
            P("tok", "hid"),
            P(("hid", "tok"), None),
            P("tok", "hid"),
        ),
        check_vma=False,
    )
```

profile of v0, /device:TPU:1, one launch (start us, length us, event | category | flops | bytes accessed | tf_op | source)
XLA Modules:
  0.0 774.3 jit_solution(9446525643140161980)
XLA Ops:
  16.3 2.2 reshape.191
  20.6 2.3 reshape.189
  25.1 2.5 fusion.172
  30.7 125.0 %all-reduce.7.cloned.1.call-done = (bf16[256,256]{1,0:T(8,128)(2,1)}, bf16[256,256]{1,0:T(8,128)(2,1)}) async-done(((bf16[256,256]{1,0:T(8,128)(2,1)}, bf16[256,256]{1,0:T(8,128)(2,1)}), (bf16[256,256]{1,0:T(8,128)(2,1)}, bf16[256,256]{1,0:T(8,128)(2,1)})) %all-reduce.7.cloned.1.call-update) | async-done | bytes 262160 | tf_op jit(solution)/shard_map/psum | solution.py:82
  157.8 2.3 fusion.176
  160.0 88.6 %all-gather.3.cloned.1.call-done = bf16[256,12288]{0,1:T(8,128)(2,1)} async-done(((bf16[256,384]{0,1:T(8,128)(2,1)}), bf16[256,12288]{0,1:T(8,128)(2,1)}) %all-gather.3.cloned.1.call-update) | async-done | bytes 6291472 | tf_op jit(solution)/shard_map/all_gather | solution.py:77
  248.6 88.8 %all-gather.5.cloned.1.call-done = bf16[256,12288]{0,1:T(8,128)(2,1)} async-done(((bf16[256,384]{0,1:T(8,128)(2,1)}), bf16[256,12288]{0,1:T(8,128)(2,1)}) %all-gather.5.cloned.1.call-update) | async-done | bytes 6291472 | tf_op jit(solution)/shard_map/all_gather | solution.py:129
  337.4 3.0 constant_dynamic-slice_fusion.5
  401.9 2.1 copy.346
  415.6 4.9 copy.351
  427.9 120.2 %all-reduce.5.cloned.1.call-done = (bf16[256,256]{1,0:T(8,128)(2,1)}, bf16[256,256]{1,0:T(8,128)(2,1)}) async-done(((bf16[256,256]{1,0:T(8,128)(2,1)}, bf16[256,256]{1,0:T(8,128)(2,1)}), (bf16[256,256]{1,0:T(8,128)(2,1)}, bf16[256,256]{1,0:T(8,128)(2,1)})) %all-reduce.5.cloned.1.call-update) | async-done | bytes 262160 | tf_op jit(solution)/shard_map/psum | solution.py:101
  557.8 2.2 fusion.36
  566.9 2.2 copy.359
  571.1 2.2 copy.361
  575.4 2.2 copy.363
  587.6 2.2 collective-permute-start.6
  609.3 2.8 collective-permute-start.9
  629.9 2.7 collective-permute-start.2
  632.6 2.7 collective-permute-start.4
  637.3 4.4 collective-permute-done.1
  644.5 13.8 %reduce-scatter.17.cloned.1.call-done = bf16[32,384]{1,0:T(8,128)(2,1)} async-done(((bf16[256,384]{1,0:T(8,128)(2,1)}), bf16[32,384]{1,0:T(8,128)(2,1)}) %reduce-scatter.17.cloned.1.call-update) | async-done | bytes 24592 | tf_op jit(solution)/shard_map/reduce_scatter | solution.py:169
  658.3 35.2 %reduce-scatter.13.cloned.1.call-done = bf16[32,768]{1,0:T(8,128)(2,1)} async-done(((bf16[256,768]{1,0:T(8,128)(2,1)}), bf16[32,768]{1,0:T(8,128)(2,1)}) %reduce-scatter.13.cloned.1.call-update) | async-done | bytes 49168 | tf_op jit(solution)/shard_map/reduce_scatter | solution.py:216
  693.5 35.5 %reduce-scatter.15.cloned.1.call-done = bf16[96,256]{1,0:T(8,128)(2,1)} async-done(((bf16[768,256]{1,0:T(8,128)(2,1)}), bf16[96,256]{1,0:T(8,128)(2,1)}) %reduce-scatter.15.cloned.1.call-update) | async-done | bytes 49168 | tf_op jit(solution)/shard_map/reduce_scatter | solution.py:166
  728.9 38.3 %reduce-scatter.11.cloned.1.call-done = bf16[6,96,256]{2,1,0:T(8,128)(2,1)} async-done(((bf16[6,768,256]{2,1,0:T(8,128)(2,1)}), bf16[6,96,256]{2,1,0:T(8,128)(2,1)}) %reduce-scatter.11.cloned.1.call-update) | async-done | bytes 294928 | tf_op jit(solution)/shard_map/reduce_scatter | solution.py:163
  (313 shorter events, 170.6 us)
Async XLA Ops:
  7.2 148.4 %all-reduce.7.cloned.1.call-start = ((), (), s32[]{:S(2)}) async-start(), calls=%async_computation.15 | async-start | bytes 524288 | tf_op jit(solution)/shard_map/psum | solution.py:82
  11.3 237.3 %all-gather.3.cloned.1.call-start = ((), (), s32[]{:S(2)}) async-start(), calls=%async_computation.6 | async-start | bytes 6488064 | tf_op jit(solution)/shard_map/all_gather | solution.py:77
  13.1 324.3 %all-gather.5.cloned.1.call-start = ((), (), s32[]{:S(2)}) async-start(), calls=%async_computation.7 | async-start | bytes 6488064 | tf_op jit(solution)/shard_map/all_gather | solution.py:129
  14.9 533.2 %all-reduce.5.cloned.1.call-start = ((), (), s32[]{:S(2)}) async-start(), calls=%async_computation.14 | async-start | bytes 524288 | tf_op jit(solution)/shard_map/psum | solution.py:101
  23.1 362.2 %copy-start.10 = (bf16[2,128,3,256]{3,2,1,0:T(4,128)(2,1)}, bf16[2,128,3,256]{3,2,1,0:T(4,128)(2,1)S(1)}, u32[]{:S(2)}) copy-start(bf16[2,128,3,256]{3,2,1,0:T(4,128)(2,1)S(1)} %reshape.192) | copy-start | bytes 1179652
  28.0 358.9 %copy-start.4 = (bf16[3,256,2,128]{3,2,1,0:T(2,128)(2,1)}, bf16[3,256,2,128]{3,2,1,0:T(2,128)(2,1)S(1)}, u32[]{:S(2)}) copy-start(bf16[3,256,2,128]{3,2,1,0:T(2,128)(2,1)S(1)} %reshape_squeeze.45) | copy-start | bytes 1179652
  28.1 359.2 %copy-start.6 = (bf16[3,256,2,128]{3,2,1,0:T(2,128)(2,1)}, bf16[3,256,2,128]{3,2,1,0:T(2,128)(2,1)S(1)}, u32[]{:S(2)}) copy-start(bf16[3,256,2,128]{3,2,1,0:T(2,128)(2,1)S(1)} %reshape_squeeze.44) | copy-start | bytes 1179652
  28.2 359.4 %copy-start.8 = (bf16[3,256,2,128]{3,2,1,0:T(2,128)(2,1)}, bf16[3,256,2,128]{3,2,1,0:T(2,128)(2,1)S(1)}, u32[]{:S(2)}) copy-start(bf16[3,256,2,128]{3,2,1,0:T(2,128)(2,1)S(1)} %reshape_squeeze.43) | copy-start | bytes 1179652
  410.9 231.9 %reduce-scatter.9.cloned.1.call-start = ((), (), s32[]{:S(2)}) async-start(), calls=%async_computation.8 | async-start | bytes 3538944 | tf_op jit(solution)/shard_map/reduce_scatter | solution.py:213
  420.5 224.0 %reduce-scatter.19.cloned.1.call-start = ((), (), s32[]{:S(2)}) async-start(), calls=%async_computation.13 | async-start | bytes 221184
  551.7 106.6 %reduce-scatter.17.cloned.1.call-start = ((), (), s32[]{:S(2)}) async-start(), calls=%async_computation.12 | async-start | bytes 221184 | tf_op jit(solution)/shard_map/reduce_scatter | solution.py:169
  555.7 137.7 %reduce-scatter.13.cloned.1.call-start = ((), (), s32[]{:S(2)}) async-start(), calls=%async_computation.10 | async-start | bytes 442368 | tf_op jit(solution)/shard_map/reduce_scatter | solution.py:216
  560.1 168.9 %reduce-scatter.15.cloned.1.call-start = ((), (), s32[]{:S(2)}) async-start(), calls=%async_computation.11 | async-start | bytes 442368 | tf_op jit(solution)/shard_map/reduce_scatter | solution.py:166
  585.1 43.0 %collective-permute-start.5 = (bf16[256,384]{1,0:T(8,128)(2,1)}, bf16[256,384]{1,0:T(8,128)(2,1)}, u32[]{:S(2)}, u32[]{:S(2)}) collective-permute-start(bf16[256,384]{1,0:T(8,128)(2,1)} %copy.313), channel_id=1, source_target_pairs={{0,8},{8,0},{16,24},{24,16},{32,40},{40,32},{48,56},{56,48},{64,72... | collective-permute-start | bytes 589832 | tf_op jit(solution)/shard_map/ppermute | solution.py:17
  587.6 41.2 %collective-permute-start.6 = (bf16[256,384]{1,0:T(8,128)(2,1)}, bf16[256,384]{1,0:T(8,128)(2,1)}, u32[]{:S(2)}, u32[]{:S(2)}) collective-permute-start(bf16[256,384]{1,0:T(8,128)(2,1)} %copy.320), channel_id=1, source_target_pairs={{0,16},{16,0},{8,24},{24,8},{32,48},{48,32},{40,56},{56,40},{64,80... | collective-permute-start | bytes 589832 | tf_op jit(solution)/shard_map/ppermute | solution.py:17
  592.1 175.2 %reduce-scatter.11.cloned.1.call-start = ((), (), s32[]{:S(2)}) async-start(), calls=%async_computation.9 | async-start | bytes 2654208 | tf_op jit(solution)/shard_map/reduce_scatter | solution.py:163
  596.3 33.6 %collective-permute-start.7 = (bf16[256,384]{1,0:T(8,128)(2,1)}, bf16[256,384]{1,0:T(8,128)(2,1)}, u32[]{:S(2)}, u32[]{:S(2)}) collective-permute-start(bf16[256,384]{1,0:T(8,128)(2,1)} %copy.326), channel_id=1, source_target_pairs={{0,32},{32,0},{8,40},{40,8},{16,48},{48,16},{24,56},{56,24},{64,96... | collective-permute-start | bytes 589832 | tf_op jit(solution)/shard_map/ppermute | solution.py:17
  606.2 26.4 %collective-permute-start.8 = (bf16[256,384]{1,0:T(8,128)(2,1)S(1)}, bf16[256,384]{1,0:T(8,128)(2,1)S(1)}, u32[]{:S(2)}, u32[]{:S(2)}) collective-permute-start(bf16[256,384]{1,0:T(8,128)(2,1)S(1)} %copy.332), channel_id=1, source_target_pairs={{0,64},{64,0},{8,72},{72,8},{16,80},{80,16},{24,88},{88,24},{32,96... | collective-permute-start | bytes 589832 | tf_op jit(solution)/shard_map/ppermute | solution.py:17
  609.3 23.3 %collective-permute-start.9 = (bf16[256,384]{1,0:T(8,128)(2,1)}, bf16[256,384]{1,0:T(8,128)(2,1)S(1)}, u32[]{:S(2)}, u32[]{:S(2)}) collective-permute-start(bf16[256,384]{1,0:T(8,128)(2,1)} %copy.338), channel_id=1, source_target_pairs={{0,128},{128,0},{8,136},{136,8},{16,144},{144,16},{24,152},{152,24... | collective-permute-start | bytes 589832 | tf_op jit(solution)/shard_map/ppermute | solution.py:17
  628.1 9.2 %collective-permute-start = (bf16[256,384]{1,0:T(8,128)(2,1)}, bf16[256,384]{1,0:T(8,128)(2,1)S(1)}, u32[]{:S(2)}, u32[]{:S(2)}) collective-permute-start(bf16[256,384]{1,0:T(8,128)(2,1)} %copy.251), channel_id=1, source_target_pairs={{0,8},{8,0},{16,24},{24,16},{32,40},{40,32},{48,56},{56,48},{64,72... | collective-permute-start | bytes 589832 | tf_op jit(solution)/shard_map/ppermute | solution.py:17
  628.8 13.0 %collective-permute-start.1 = (bf16[256,384]{1,0:T(8,128)(2,1)}, bf16[256,384]{1,0:T(8,128)(2,1)S(1)}, u32[]{:S(2)}, u32[]{:S(2)}) collective-permute-start(bf16[256,384]{1,0:T(8,128)(2,1)} %copy.258), channel_id=1, source_target_pairs={{0,16},{16,0},{8,24},{24,8},{32,48},{48,32},{40,56},{56,40},{64,80... | collective-permute-start | bytes 589832 | tf_op jit(solution)/shard_map/ppermute | solution.py:17
  629.9 11.9 %collective-permute-start.2 = (bf16[256,384]{1,0:T(8,128)(2,1)}, bf16[256,384]{1,0:T(8,128)(2,1)S(1)}, u32[]{:S(2)}, u32[]{:S(2)}) collective-permute-start(bf16[256,384]{1,0:T(8,128)(2,1)} %copy.264), channel_id=1, source_target_pairs={{0,32},{32,0},{8,40},{40,8},{16,48},{48,16},{24,56},{56,24},{64,96... | collective-permute-start | bytes 589832 | tf_op jit(solution)/shard_map/ppermute | solution.py:17
  632.6 9.2 %collective-permute-start.3 = (bf16[256,384]{1,0:T(8,128)(2,1)}, bf16[256,384]{1,0:T(8,128)(2,1)S(1)}, u32[]{:S(2)}, u32[]{:S(2)}) collective-permute-start(bf16[256,384]{1,0:T(8,128)(2,1)} %copy.270), channel_id=1, source_target_pairs={{0,64},{64,0},{8,72},{72,8},{16,80},{80,16},{24,88},{88,24},{32,96... | collective-permute-start | bytes 589832 | tf_op jit(solution)/shard_map/ppermute | solution.py:17
  632.6 9.2 %collective-permute-start.4 = (bf16[256,384]{1,0:T(8,128)(2,1)}, bf16[256,384]{1,0:T(8,128)(2,1)S(1)}, u32[]{:S(2)}, u32[]{:S(2)}) collective-permute-start(bf16[256,384]{1,0:T(8,128)(2,1)} %copy.276), channel_id=1, source_target_pairs={{0,128},{128,0},{8,136},{136,8},{16,144},{144,16},{24,152},{152,24... | collective-permute-start | bytes 589832 | tf_op jit(solution)/shard_map/ppermute | solution.py:17
  (54 other events, 1162.3 us)
Sparse Core Ops, SparseCore 0:
  12.1 143.4 all-reduce.6
  158.8 89.7 all-gather.2
  251.7 85.6 all-gather.4
  411.0 137.0 all-reduce.4
  550.5 36.9 reduce-scatter.8
  590.4 32.5 reduce-scatter.18
  626.2 32.0 reduce-scatter.16
  661.4 32.0 reduce-scatter.12
  696.7 32.1 reduce-scatter.14
  731.9 35.3 reduce-scatter.10
where the time goes:
time: 781 us; the launch traced here: 774 us
  waiting for transfers between devices  550 us (70%)
  local copies, waits for them, and re-layouts  106 us (14%)
  matrix products  87.5 us (11%)
  between operations  15.4 us (2%)
  starting transfers between devices  15.1 us (2%)
    psum x1, waiting for transfers between devices, on_device(): lax.psum(jnp.dot(tokens, up_left, preferred_element_type=jnp.float32).ast...  125 us
    psum x1, waiting for transfers between devices, on_device(): lax.psum(jnp.dot(hidden_flat, down_left, preferred_element_type=jnp.float...  120 us
    all_gather x1, waiting for transfers between devices, on_device(): grad_gathered = lax.all_gather(cotangent, 'hid', axis=1, tiled=True)  88.8 us
    all_gather x1, waiting for transfers between devices, on_device(): gathered = lax.all_gather(tokens, 'hid', axis=1, tiled=True)  88.6 us
    reduce_scatter x1, waiting for transfers between devices, on_device(): lax.psum_scatter(down_terms.astype(jnp.bfloat16), 'tok', scatter_dimensio...  38.3 us
    reduce_scatter x1, waiting for transfers between devices, on_device(): lax.psum_scatter(down_left_term.astype(jnp.bfloat16), 'tok', scatter_dime...  35.5 us
    reduce_scatter x1, waiting for transfers between devices, on_device(): lax.psum_scatter(up_right_term.astype(jnp.bfloat16), 'tok', scatter_dimen...  35.2 us
    dot_general x12, matrix products, choose(): jnp.einsum('rfg,hyf->rhyg', reshaped_tiles, select_half_values[partition_...  22.3 us
  transfers between devices with their start and end apart: 20, of which 9 were waited for; matrix products, arithmetic and copies ran while one was open for 15% of the time, Pallas kernels for 0%

commit v1 on v0

v1 whole, which is shorter than its diff:
```python
import functools

import jax
import jax.numpy as jnp
from jax import lax
from jax.experimental import pallas as pl
from jax.experimental.pallas import tpu as pltpu
from jax.sharding import PartitionSpec as P

GELU_SCALE = 0.7978845608028654
GELU_CUBIC = 0.044715
BF = jnp.bfloat16
F32 = jnp.float32
VMEM_LIMIT = 56 * 1024 * 1024


def gelu_parts(pre_act):
    inner = GELU_SCALE * (pre_act + GELU_CUBIC * pre_act * pre_act * pre_act)
    tanh_value = jnp.tanh(inner)
    value = 0.5 * pre_act * (1.0 + tanh_value)
    slope = 0.5 * (1.0 + tanh_value) + 0.5 * pre_act * (
        1.0 - tanh_value * tanh_value
    ) * GELU_SCALE * (1.0 + 3.0 * GELU_CUBIC * pre_act * pre_act)
    return (value, slope)


def dot(a, b):
    return jnp.dot(a, b, preferred_element_type=F32)


def dot_nt(a, b):
    return lax.dot_general(a, b, (((1,), (1,)), ((), ())), preferred_element_type=F32)


def dot_tn(a, b):
    return lax.dot_general(a, b, (((0,), (0,)), ((), ())), preferred_element_type=F32)


def vmem_spec():
    return pl.BlockSpec(memory_space=pltpu.VMEM)


def head_kernel(tok_ref, cot_ref, up_left_ref, down_right_ref, both_ref, low_ref):
    rows = tok_ref.shape[0]
    tok, cot = tok_ref[...], cot_ref[...]
    both_ref[:rows] = tok
    both_ref[rows:] = cot
    low_ref[:rows] = dot(tok, up_left_ref[...]).astype(BF)
    low_ref[rows:] = dot_nt(cot, down_right_ref[...]).astype(BF)


def chosen(ref, index_ref, level, block, first_row, rows, sub):
    pieces = []
    for j in range(2):
        column = pl.multiple_of(index_ref[level, block, j] * sub, sub)
        pieces.append(ref[pl.ds(first_row, rows), pl.ds(column, sub)])
    return jnp.concatenate(pieces, axis=1)


def middle_kernel(levels, index_ref, *refs):
    fields = refs[:levels]
    low_ref, up_ref, down_ref, up_right_ref, down_left_ref = refs[levels : levels + 5]
    act_ref, grad_ref, lowp_ref = refs[levels + 5 : levels + 8]
    parts = refs[levels + 8 : 2 * levels + 8]
    out_acc, in_acc, low_acc = refs[2 * levels + 8 :]
    block = pl.program_id(0)
    rows = low_ref.shape[0] // 2
    sub = fields[0].shape[1] // 3

    @pl.when(block == 0)
    def _():
        out_acc[...] = jnp.zeros_like(out_acc)
        in_acc[...] = jnp.zeros_like(in_acc)
        low_acc[...] = jnp.zeros_like(low_acc)

    pre_act = dot(low_ref[:rows], up_right_ref[...])
    grad_hidden = dot_nt(low_ref[rows:], down_left_ref[...])
    for k in range(levels):
        pre_act += dot(chosen(fields[k], index_ref, k, block, 0, rows, sub), up_ref[k])
        grad_hidden += dot_nt(chosen(fields[k], index_ref, k, block, rows, rows, sub), down_ref[k])
    value, slope = gelu_parts(pre_act)
    act = value.astype(BF)
    grad = (grad_hidden * slope).astype(BF)
    act_ref[...] = act
    grad_ref[...] = grad
    low_acc[:rows] += dot(act, down_left_ref[...])
    low_acc[rows:] += dot_nt(grad, up_right_ref[...])
    for k in range(levels):
        out_pair = dot(act, down_ref[k])
        in_pair = dot_nt(grad, up_ref[k])
        for j in range(2):
            where = 3 * k + index_ref[k, block, j]
            out_acc[where] += out_pair[:, j * sub : (j + 1) * sub]
            in_acc[where] += in_pair[:, j * sub : (j + 1) * sub]

    @pl.when(block == pl.num_programs(0) - 1)
    def _():
        lowp_ref[...] = low_acc[...].astype(BF)
        for k in range(levels):
            for c in range(3):
                cols = slice(c * sub, (c + 1) * sub)
                parts[k][:rows, cols] = out_acc[3 * k + c].astype(BF)
                parts[k][rows:, cols] = in_acc[3 * k + c].astype(BF)


def grads_kernel(levels, groups, index_ref, *refs):
    fields = refs[:levels]
    low_ref, act_ref, grad_ref, out_ref = refs[levels:]
    block = pl.program_id(0)
    rows = low_ref.shape[0] // 2
    sub = fields[0].shape[1] // 3
    width = act_ref.shape[1]
    piece = width // groups
    per = 3 * piece
    up_base = (levels + 1) * per
    act_t = act_ref[...].T
    grad = grad_ref[...]
    for k in range(levels + 1):
        if k < levels:
            field = chosen(fields[k], index_ref, k, block, 0, rows, sub)
            grad_field = chosen(fields[k], index_ref, k, block, rows, rows, sub)
        else:
            field = low_ref[:rows]
            grad_field = low_ref[rows:]
        down = dot(act_t, grad_field).astype(BF)
        up = dot_tn(field, grad).astype(BF)
        for m in range(groups):
            slot = block * groups + m
            group = slot // 3
            row = pl.multiple_of(k * per + (slot - 3 * group) * piece, piece)
            out_ref[group, pl.ds(row, piece), :] = down[m * piece : (m + 1) * piece]
            row = pl.multiple_of(up_base + (block * (levels + 1) + k) * piece, piece)
            out_ref[m, pl.ds(row, piece), :] = up[m * piece : (m + 1) * piece]


def late_kernel(groups, both_ref, low_ref, out_ref):
    rows = low_ref.shape[0] // 2
    right = dot_tn(low_ref[:rows], both_ref[rows:]).astype(BF)
    left = dot_tn(both_ref[:rows], low_ref[rows:]).astype(BF)
    hr = right.shape[0] // groups
    hl = left.shape[0] // groups
    for m in range(groups):
        for c in range(right.shape[1] // 128):
            out_ref[m, c * hr : (c + 1) * hr] = right[m * hr : (m + 1) * hr, c * 128 : (c + 1) * 128]
        base = hr * (right.shape[1] // 128)
        for c in range(left.shape[1] // 128):
            out_ref[m, base + c * hl : base + (c + 1) * hl] = left[
                m * hl : (m + 1) * hl, c * 128 : (c + 1) * 128
            ]


def final_kernel(levels, *refs):
    parts = refs[:levels]
    low_ref, down_right_ref, up_left_ref, late_ref = refs[levels : levels + 4]
    layer_ref, tokens_ref, right_ref, left_ref = refs[levels + 4 :]
    rows = low_ref.shape[0] // 2
    out = parts[0][:rows].astype(F32)
    back = parts[0][rows:].astype(F32)
    for k in range(1, levels):
        out += parts[k][:rows].astype(F32)
        back += parts[k][rows:].astype(F32)
    layer_ref[...] = (out + dot(low_ref[:rows], down_right_ref[...])).astype(BF)
    tokens_ref[...] = (back + dot_nt(low_ref[rows:], up_left_ref[...])).astype(BF)
    late = late_ref[0].astype(F32)
    for m in range(1, late_ref.shape[0]):
        late += late_ref[m].astype(F32)
    late = late.astype(BF)
    hr, hl = right_ref.shape[0], left_ref.shape[0]
    for c in range(right_ref.shape[1] // 128):
        right_ref[:, c * 128 : (c + 1) * 128] = late[c * hr : (c + 1) * hr]
    base = hr * (right_ref.shape[1] // 128)
    for c in range(left_ref.shape[1] // 128):
        left_ref[:, c * 128 : (c + 1) * 128] = late[base + c * hl : base + (c + 1) * hl]


def params():
    return pltpu.CompilerParams(vmem_limit_bytes=VMEM_LIMIT)


def cost(flops, size):
    return pl.CostEstimate(flops=flops, bytes_accessed=size, transcendentals=0)


def hid_sum(value):
    count = lax.axis_size("hid")
    pieces = value.reshape(count, value.shape[0] // count, value.shape[1])
    pieces = lax.all_to_all(pieces, "hid", 0, 0, tiled=True)
    total = jnp.sum(pieces.astype(F32), axis=0).astype(BF)
    pieces = jnp.broadcast_to(total[None], pieces.shape)
    return lax.all_to_all(pieces, "hid", 0, 0, tiled=True).reshape(value.shape)


def on_device(
    tokens, cotangent, up_tiles, down_tiles, block_index, up_left, up_right, down_left, down_right
):
    hid_count = lax.axis_size("hid")
    groups = lax.axis_size("tok")
    levels = hid_count.bit_length()
    rows, feat = tokens.shape
    blocks = block_index.shape[1]
    hidden = up_tiles.shape[2]
    width = hidden // blocks
    rank = up_left.shape[1]
    sub = feat // 3
    sds = jax.ShapeDtypeStruct

    def partner(value, level):
        distance = 1 << (level - 1)
        return lax.ppermute(value, "hid", [(i, i ^ distance) for i in range(hid_count)])

    both, low_part = pl.pallas_call(
        head_kernel,
        out_shape=(sds((2 * rows, feat), BF), sds((2 * rows, rank), BF)),
        in_specs=[vmem_spec()] * 4,
        out_specs=(vmem_spec(), vmem_spec()),
        compiler_params=params(),
        cost_estimate=cost(4 * rows * feat * rank, 4 * rows * feat * 2),
        name="head",
    )(tokens, cotangent, up_left, down_right)
    order = [3, 2, 1, 5, 4]
    fields = [both] + [None] * (levels - 1)
    for level in order:
        fields[level] = partner(both, level)
    low = hid_sum(low_part)

    def whole(shape):
        return pl.BlockSpec(shape, lambda b, *_: (0,) * len(shape))

    grid_params = pltpu.CompilerParams(
        dimension_semantics=("arbitrary",), vmem_limit_bytes=VMEM_LIMIT
    )
    flops = 2 * rows * (levels + 1) * 2 * sub * hidden
    middle = pl.pallas_call(
        functools.partial(middle_kernel, levels),
        grid_spec=pltpu.PrefetchScalarGridSpec(
            num_scalar_prefetch=1,
            grid=(blocks,),
            in_specs=[whole((2 * rows, feat))] * levels
            + [
                whole((2 * rows, rank)),
                pl.BlockSpec((levels, 2 * sub, width), lambda b, *_: (0, 0, b)),
                pl.BlockSpec((levels, width, 2 * sub), lambda b, *_: (0, b, 0)),
                pl.BlockSpec((rank, width), lambda b, *_: (0, b)),
                pl.BlockSpec((width, rank), lambda b, *_: (b, 0)),
            ],
            out_specs=[
                pl.BlockSpec((rows, width), lambda b, *_: (0, b)),
                pl.BlockSpec((rows, width), lambda b, *_: (0, b)),
                whole((2 * rows, rank)),
            ]
            + [whole((2 * rows, feat))] * levels,
            scratch_shapes=[
                pltpu.VMEM((3 * levels, rows, sub), F32),
                pltpu.VMEM((3 * levels, rows, sub), F32),
                pltpu.VMEM((2 * rows, rank), F32),
            ],
        ),
        out_shape=[
            sds((rows, hidden), BF),
            sds((rows, hidden), BF),
            sds((2 * rows, rank), BF),
        ]
        + [sds((2 * rows, feat), BF)] * levels,
        compiler_params=grid_params,
        cost_estimate=cost(4 * flops, 10 * 1024 * 1024),
        name="middle",
    )(block_index, *fields, low, up_tiles, down_tiles, up_right, down_left)
    act, grad_pre, lowp = middle[:3]
    parts = list(middle[3:])

    piece = width // groups
    chunk = 2 * (levels + 1) * 3 * piece
    packed = pl.pallas_call(
        functools.partial(grads_kernel, levels, groups),
        grid_spec=pltpu.PrefetchScalarGridSpec(
            num_scalar_prefetch=1,
            grid=(blocks,),
            in_specs=[whole((2 * rows, feat))] * levels
            + [
                whole((2 * rows, rank)),
                pl.BlockSpec((rows, width), lambda b, *_: (0, b)),
                pl.BlockSpec((rows, width), lambda b, *_: (0, b)),
            ],
            out_specs=whole((groups, chunk, width)),
        ),
        out_shape=sds((groups, chunk, width), BF),
        compiler_params=grid_params,
        cost_estimate=cost(2 * flops, 10 * 1024 * 1024),
        name="grads",
    )(block_index, *fields, low, act, grad_pre)

    for level in order:
        parts[level] = partner(parts[level], level)
    low2 = hid_sum(lowp)
    summed = lax.psum_scatter(
        packed.reshape(groups * chunk, width), "tok", scatter_dimension=0, tiled=True
    )
    half = (levels + 1) * 3 * piece
    down_sum = summed[:half].reshape(levels + 1, 3 * piece, width)
    up_sum = summed[half:].reshape(blocks, levels + 1, piece, width)
    grad_down_tiles = down_sum[:levels]
    grad_down_left = down_sum[levels]
    up_sum = up_sum.transpose(1, 2, 0, 3).reshape(levels + 1, piece, hidden)
    grad_up_tiles = up_sum[:levels]
    grad_up_right = up_sum[levels]

    late_rows = (rank // groups) * (feat // 128) + (feat // groups) * (rank // 128)
    late = pl.pallas_call(
        functools.partial(late_kernel, groups),
        out_shape=sds((groups, late_rows, 128), BF),
        in_specs=[vmem_spec()] * 2,
        out_specs=vmem_spec(),
        compiler_params=params(),
        cost_estimate=cost(4 * rows * feat * rank, 4 * rows * feat * 2),
        name="late",
    )(both, low2)
    late = lax.all_to_all(late, "tok", 0, 0, tiled=True)
    layer_out, grad_tokens, grad_down_right, grad_up_left = pl.pallas_call(
        functools.partial(final_kernel, levels),
        out_shape=(
            sds((rows, feat), BF),
            sds((rows, feat), BF),
            sds((rank // groups, feat), BF),
            sds((feat // groups, rank), BF),
        ),
        in_specs=[vmem_spec()] * (levels + 4),
        out_specs=(vmem_spec(),) * 4,
        compiler_params=params(),
        cost_estimate=cost(4 * rows * feat * rank, 16 * rows * feat * 2),
        name="final",
    )(*parts, low2, down_right, up_left, late)
    return (
        layer_out,
        grad_tokens,
        grad_up_tiles,
        grad_down_tiles,
        grad_up_left,
        grad_up_right,
        grad_down_left,
        grad_down_right,
    )


def solution(mesh):
    return jax.shard_map(
        on_device,
        mesh=mesh,
        in_specs=(
            P("tok", "hid"),
            P("tok", "hid"),
            P(None, None, "hid"),
            P(None, "hid", None),
            P(None, "hid", None),
            P("hid", None),
            P(None, "hid"),
            P("hid", None),
            P(None, "hid"),
        ),
        out_specs=(
            P("tok", "hid"),
            P("tok", "hid"),
            P(None, "tok", "hid"),
            P(None, ("hid", "tok"), None),
            P(("hid", "tok"), None),
            P("tok", "hid"),
            P(("hid", "tok"), None),
            P("tok", "hid"),
        ),
        check_vma=False,
    )
```

time: 781 us -> 185 us (0.24)
  the two profiles are of different devices: /device:TPU:1 before, /device:TPU:16 now
where the time goes in v1:
time: 185 us; the launch traced here: 184 us
  waiting for transfers between devices  57.4 us (31%)
  blocking collectives  41.9 us (23%)
  starting transfers between devices  35.3 us (19%)
  Pallas kernels  24.5 us (13%)
  between operations  14.2 us (8%)
  local copies, waits for them, and re-layouts  10.4 us (6%)
    ppermute x10, waiting for transfers between devices, partner(): lax.ppermute(value, 'hid', [(i, i ^ distance) for i in range(hid_count)])  49.2 us
    all_to_all x2, blocking collectives, hid_sum(): pieces = lax.all_to_all(pieces, 'hid', 0, 0, tiled=True)  41.9 us
    ppermute x10, starting transfers between devices, partner(): lax.ppermute(value, 'hid', [(i, i ^ distance) for i in range(hid_count)])  21.7 us
    pallas_call x1, Pallas kernels, on_device(): pl.pallas_call(functools.partial(middle_kernel, levels), grid_spec=pltpu....  9.6 us
    all_to_all x2, starting transfers between devices, hid_sum(): return lax.all_to_all(pieces, 'hid', 0, 0, tiled=True).reshape(value.shape)  8.79 us
    all_to_all x2, waiting for transfers between devices, hid_sum(): return lax.all_to_all(pieces, 'hid', 0, 0, tiled=True).reshape(value.shape)  8.1 us
    pallas_call x1, Pallas kernels, on_device(): pl.pallas_call(functools.partial(grads_kernel, levels, groups), grid_spec...  7.52 us
    unnamed x40, local copies, waits for them, and re-layouts  5.06 us
  transfers between devices with their start and end apart: 14, of which 6 were waited for; matrix products, arithmetic and copies ran while one was open for 1% of the time, Pallas kernels for 3%

profile of v1, /device:TPU:16, one launch (start us, length us, event | category | flops | bytes accessed | tf_op | source)
XLA Modules:
  0.0 183.9 jit_solution(15356884463379709999)
XLA Ops:
  7.2 2.2 %head.1 = (bf16[512,384]{1,0:T(8,128)(2,1)}, bf16[512,256]{1,0:T(8,128)(2,1)}) custom-call(bf16[256,384]{1,0:T(8,128)(2,1)} %tok_ref.1, bf16[256,384]{1,0:T(8,128)(2,1)} %cot_ref.1, bf16[384,256]{1,0:T(8,128)(2,1)} %refs_8_.3, bf16[256,384]{1,0:T(8,128)(2,1)} %refs_7_.3), custom_call_target="tpu_custom_call" | custom-call | flops 100663296 | bytes 786432 | tf_op jit(solution)/shard_map/head/pallas_call | solution.py:211
  9.4 23.8 %all_to_all.25 = bf16[32,16,256]{2,1,0:T(8,128)(2,1)S(1)} all-to-all(bf16[32,16,256]{2,1,0:T(8,128)(2,1)} %bitcast.24), channel_id=1, replica_groups=mesh['hid'=32,'tok'=8] {'hid'}, dimensions={0} | all-to-all | bytes 524288 | tf_op jit(solution)/shard_map/all_to_all | solution.py:187
  34.0 4.4 %all-to-all-start.1 = ((bf16[32,16,256]{2,1,0:T(8,128)(2,1)}), bf16[32,16,256]{2,1,0:T(8,128)(2,1)S(1)}, u32[]{:S(2)}, u32[]{:S(2)}) async-start(bf16[32,16,256]{2,1,0:T(8,128)(2,1)} %broadcast_in_dim.4), calls=%async_computation.1 | async-start | bytes 524288 | tf_op jit(solution)/shard_map/all_to_all | solution.py:190
  38.4 3.4 %collective-permute-start.4 = (bf16[512,384]{1,0:T(8,128)(2,1)}, bf16[512,384]{1,0:T(8,128)(2,1)S(1)}, u32[]{:S(2)}, u32[]{:S(2)}) collective-permute-start(bf16[512,384]{1,0:T(8,128)(2,1)} %get-tuple-element.23.refs_0_.both_ref), channel_id=1, source_target_pairs={{0,128},{8,136},{16,144},{24,152},{32,160},{40,168},{48,176},{56,1... | collective-permute-start | bytes 1179656 | tf_op jit(solution)/shard_map/ppermute | solution.py:209
  42.4 5.4 %collective-permute-start.2 = (bf16[512,384]{1,0:T(8,128)(2,1)}, bf16[512,384]{1,0:T(8,128)(2,1)S(1)}, u32[]{:S(2)}, u32[]{:S(2)}) collective-permute-start(bf16[512,384]{1,0:T(8,128)(2,1)} %get-tuple-element.23.refs_0_.both_ref), channel_id=1, source_target_pairs={{0,32},{8,40},{16,48},{24,56},{32,0},{40,8},{48,16},{56,24},{64,96... | collective-permute-start | bytes 1179656 | tf_op jit(solution)/shard_map/ppermute | solution.py:209
  49.6 4.6 %collective-permute-done.4.refs_5_ = bf16[512,384]{1,0:T(8,128)(2,1)S(1)} collective-permute-done((bf16[512,384]{1,0:T(8,128)(2,1)}, bf16[512,384]{1,0:T(8,128)(2,1)S(1)}, u32[]{:S(2)}, u32[]{:S(2)}) %collective-permute-start.4) | collective-permute-done | bytes 393248 | tf_op jit(solution)/shard_map/ppermute | solution.py:209
  54.3 6.8 %collective-permute-done.3.refs_4_ = bf16[512,384]{1,0:T(8,128)(2,1)S(1)} collective-permute-done((bf16[512,384]{1,0:T(8,128)(2,1)}, bf16[512,384]{1,0:T(8,128)(2,1)S(1)}, u32[]{:S(2)}, u32[]{:S(2)}) %collective-permute-start.3) | collective-permute-done | bytes 393248 | tf_op jit(solution)/shard_map/ppermute | solution.py:209
  61.0 5.3 %collective-permute-done.2.refs_3_ = bf16[512,384]{1,0:T(8,128)(2,1)S(1)} collective-permute-done((bf16[512,384]{1,0:T(8,128)(2,1)}, bf16[512,384]{1,0:T(8,128)(2,1)S(1)}, u32[]{:S(2)}, u32[]{:S(2)}) %collective-permute-start.2) | collective-permute-done | bytes 393248 | tf_op jit(solution)/shard_map/ppermute | solution.py:209
  66.3 15.2 %collective-permute-done.1.refs_2_ = bf16[512,384]{1,0:T(8,128)(2,1)S(1)} collective-permute-done((bf16[512,384]{1,0:T(8,128)(2,1)}, bf16[512,384]{1,0:T(8,128)(2,1)S(1)}, u32[]{:S(2)}, u32[]{:S(2)}) %collective-permute-start.1) | collective-permute-done | bytes 393248 | tf_op jit(solution)/shard_map/ppermute | solution.py:209
  82.4 9.6 %middle.1 = (bf16[256,768]{1,0:T(8,128)(2,1)}, bf16[256,768]{1,0:T(8,128)(2,1)}, bf16[512,256]{1,0:T(8,128)(2,1)}, bf16[512,384]{1,0:T(8,128)(2,1)}, bf16[512,38...) custom-call(s32[6,3,2]{2,1,0:T(4,128)} %copy.21.index_ref, ...), custom_call_target="tpu_custom_call" | custom-call | flops 2818572288 | bytes 10485760 | tf_op jit(solution)/shard_map/middle/pallas_call | solution.py:233
  92.0 7.5 %grads.1 = bf16[8,1344,256]{2,1,0:T(8,128)(2,1)} custom-call(s32[6,3,2]{2,1,0:T(4,128)} %copy.21.index_ref, bf16[512,384]{1,0:T(8,128)(2,1)} %get-tuple-element.23.refs_0_.both_ref, bf16[512,384]{1,0:T(8,128)(2,1)} %copy-done.8, bf16[512,384]{1,0:T(8,128)(2,1)} %copy-done.7, bf16[512,384]{1,0:T(8,128)(2,1)} %copy-done.6, bf16[512,384]{1,0:T(8,128)(2,1)} %copy-done.5, ...), custom_call_target="tpu_custom_call" | custom-call | flops 1409286144 | bytes 10485760 | tf_op jit(solution)/shard_map/grads/pallas_call | solution.py:273
  100.5 18.1 %all_to_all.26 = bf16[32,16,256]{2,1,0:T(8,128)(2,1)S(1)} all-to-all(bf16[32,16,256]{2,1,0:T(8,128)(2,1)S(1)} %bitcast.23), channel_id=1, replica_groups=mesh['hid'=32,'tok'=8] {'hid'}, dimensions={0} | all-to-all | bytes 524288 | tf_op jit(solution)/shard_map/all_to_all | solution.py:187
  119.4 4.4 %all-to-all-start.3 = ((bf16[32,16,256]{2,1,0:T(8,128)(2,1)}), bf16[32,16,256]{2,1,0:T(8,128)(2,1)S(1)}, u32[]{:S(2)}, u32[]{:S(2)}) async-start(bf16[32,16,256]{2,1,0:T(8,128)(2,1)} %broadcast_in_dim.5), calls=%async_computation.3 | async-start | bytes 524288 | tf_op jit(solution)/shard_map/all_to_all | solution.py:190
  123.8 1.9 %collective-permute-start.5 = (bf16[512,384]{1,0:T(8,128)(2,1)}, bf16[512,384]{1,0:T(8,128)(2,1)S(1)}, u32[]{:S(2)}, u32[]{:S(2)}) collective-permute-start(bf16[512,384]{1,0:T(8,128)(2,1)} %get-tuple-element.26), channel_id=1, source_target_pairs={{0,8},{8,0},{16,24},{24,16},{32,40},{40,32},{48,56},{56,48},{64,72... | collective-permute-start | bytes 1179656 | tf_op jit(solution)/shard_map/ppermute | solution.py:209
  125.7 2.4 %collective-permute-start.6 = (bf16[512,384]{1,0:T(8,128)(2,1)}, bf16[512,384]{1,0:T(8,128)(2,1)S(1)}, u32[]{:S(2)}, u32[]{:S(2)}) collective-permute-start(bf16[512,384]{1,0:T(8,128)(2,1)} %get-tuple-element.27), channel_id=1, source_target_pairs={{0,16},{8,24},{16,0},{24,8},{32,48},{40,56},{48,32},{56,40},{64,80... | collective-permute-start | bytes 1179656 | tf_op jit(solution)/shard_map/ppermute | solution.py:209
  128.1 2.7 %collective-permute-start.7 = (bf16[512,384]{1,0:T(8,128)(2,1)S(1)}, bf16[512,384]{1,0:T(8,128)(2,1)S(1)}, u32[]{:S(2)}, u32[]{:S(2)}) collective-permute-start(bf16[512,384]{1,0:T(8,128)(2,1)S(1)} %copy-done.18), channel_id=1, source_target_pairs={{0,32},{8,40},{16,48},{24,56},{32,0},{40,8},{48,16},{56,24},{64,96... | collective-permute-start | bytes 1179656 | tf_op jit(solution)/shard_map/ppermute | solution.py:209
  130.7 1.5 collective-permute-start.8
  132.2 2.8 %collective-permute-start.9 = (bf16[512,384]{1,0:T(8,128)(2,1)S(1)}, bf16[512,384]{1,0:T(8,128)(2,1)S(1)}, u32[]{:S(2)}, u32[]{:S(2)}) collective-permute-start(bf16[512,384]{1,0:T(8,128)(2,1)S(1)} %copy-done.16), channel_id=1, source_target_pairs={{0,128},{8,136},{16,144},{24,152},{32,160},{40,168},{48,176},{56,1... | collective-permute-start | bytes 1179656 | tf_op jit(solution)/shard_map/ppermute | solution.py:209
  135.0 8.1 %all-to-all-done.3 = bf16[32,16,256]{2,1,0:T(8,128)(2,1)S(1)} async-done(((bf16[32,16,256]{2,1,0:T(8,128)(2,1)}), bf16[32,16,256]{2,1,0:T(8,128)(2,1)S(1)}, u32[]{:S(2)}, u32[]{:S(2)}) %all-to-all-start.3) | async-done | bytes 262176 | tf_op jit(solution)/shard_map/all_to_all | solution.py:190
  143.8 2.2 %late.1 = bf16[8,192,128]{2,1,0:T(8,128)(2,1)} custom-call(bf16[512,384]{1,0:T(8,128)(2,1)} %get-tuple-element.23.refs_0_.both_ref, bf16[512,256]{1,0:T(8,128)(2,1)} %bitcast.14), custom_call_target="tpu_custom_call" | custom-call | flops 100663296 | bytes 786432 | tf_op jit(solution)/shard_map/late/pallas_call | solution.py:308
  145.9 4.8 %all-to-all-start.4 = ((bf16[8,192,128]{2,1,0:T(8,128)(2,1)}), bf16[8,192,128]{2,1,0:T(8,128)(2,1)S(1)}, u32[]{:S(2)}, u32[]{:S(2)}) async-start(bf16[8,192,128]{2,1,0:T(8,128)(2,1)} %late.1), calls=%async_computation.4 | async-start | bytes 786432 | tf_op jit(solution)/shard_map/all_to_all | solution.py:317
  150.8 17.4 %collective-permute-done.7.refs_3_ = bf16[512,384]{1,0:T(8,128)(2,1)S(1)} collective-permute-done((bf16[512,384]{1,0:T(8,128)(2,1)S(1)}, bf16[512,384]{1,0:T(8,128)(2,1)S(1)}, u32[]{:S(2)}, u32[]{:S(2)}) %collective-permute-start.7) | collective-permute-done | bytes 393248 | tf_op jit(solution)/shard_map/ppermute | solution.py:209
  169.4 3.0 %final.1 = (bf16[256,384]{1,0:T(8,128)(2,1)}, bf16[256,384]{1,0:T(8,128)(2,1)}, bf16[32,384]{1,0:T(8,128)(2,1)}, bf16[48,256]{1,0:T(8,128)(2,1)}) custom-call(bf16[512,384]{1,0:T(8,128)(2,1)} %get-tuple-element.25.refs_0_, bf16[512,384]{1,0:T(8,128)(2,1)} %copy-done.9, bf16[512,384]{1,0:T(8,128)(2,1)} %copy-done.10, bf16[512,384]{1,0:T(8,128)(2,1)} %copy-done.11, ...), custom_call_target="tpu_custom_call" | custom-call | flops 100663296 | bytes 3145728 | tf_op jit(solution)/shard_map/final/pallas_call | solution.py:318
  172.4 1.1 slice.33
  (63 shorter events, 11.3 us)
Async XLA Ops:
  7.2 41.8 %copy-start.15 = (s32[6,3,2]{0,2,1:T(2,128)S(1)}, s32[6,3,2]{0,2,1:T(2,128)}, u32[]{:S(2)}) copy-start(s32[6,3,2]{0,2,1:T(2,128)} %param.13) | copy-start | bytes 436
  34.0 47.5 %all-to-all-start.1 = ((bf16[32,16,256]{2,1,0:T(8,128)(2,1)}), bf16[32,16,256]{2,1,0:T(8,128)(2,1)S(1)}, u32[]{:S(2)}, u32[]{:S(2)}) async-start(bf16[32,16,256]{2,1,0:T(8,128)(2,1)} %broadcast_in_dim.4), calls=%async_computation.1 | async-start | bytes 524288 | tf_op jit(solution)/shard_map/all_to_all | solution.py:190
  38.4 134.1 %reduce-scatter.2.cloned.1.call-start = ((), (), s32[]{:S(2)}) async-start(), calls=%async_computation.6 | async-start | bytes 6193152 | tf_op jit(solution)/shard_map/reduce_scatter | solution.py:295
  38.4 15.9 %collective-permute-start.4 = (bf16[512,384]{1,0:T(8,128)(2,1)}, bf16[512,384]{1,0:T(8,128)(2,1)S(1)}, u32[]{:S(2)}, u32[]{:S(2)}) collective-permute-start(bf16[512,384]{1,0:T(8,128)(2,1)} %get-tuple-element.23.refs_0_.both_ref), channel_id=1, source_target_pairs={{0,128},{8,136},{16,144},{24,152},{32,160},{40,168},{48,176},{56,1... | collective-permute-start | bytes 1179656 | tf_op jit(solution)/shard_map/ppermute | solution.py:209
  41.8 19.2 %collective-permute-start.3 = (bf16[512,384]{1,0:T(8,128)(2,1)}, bf16[512,384]{1,0:T(8,128)(2,1)S(1)}, u32[]{:S(2)}, u32[]{:S(2)}) collective-permute-start(bf16[512,384]{1,0:T(8,128)(2,1)} %get-tuple-element.23.refs_0_.both_ref), channel_id=1, source_target_pairs={{0,64},{8,72},{16,80},{24,88},{32,96},{40,104},{48,112},{56,120},{... | collective-permute-start | bytes 1179656 | tf_op jit(solution)/shard_map/ppermute | solution.py:209
  42.4 23.9 %collective-permute-start.2 = (bf16[512,384]{1,0:T(8,128)(2,1)}, bf16[512,384]{1,0:T(8,128)(2,1)S(1)}, u32[]{:S(2)}, u32[]{:S(2)}) collective-permute-start(bf16[512,384]{1,0:T(8,128)(2,1)} %get-tuple-element.23.refs_0_.both_ref), channel_id=1, source_target_pairs={{0,32},{8,40},{16,48},{24,56},{32,0},{40,8},{48,16},{56,24},{64,96... | collective-permute-start | bytes 1179656 | tf_op jit(solution)/shard_map/ppermute | solution.py:209
  47.8 33.7 %collective-permute-start.1 = (bf16[512,384]{1,0:T(8,128)(2,1)}, bf16[512,384]{1,0:T(8,128)(2,1)S(1)}, u32[]{:S(2)}, u32[]{:S(2)}) collective-permute-start(bf16[512,384]{1,0:T(8,128)(2,1)} %get-tuple-element.23.refs_0_.both_ref), channel_id=1, source_target_pairs={{0,16},{8,24},{16,0},{24,8},{32,48},{40,56},{48,32},{56,40},{64,80... | collective-permute-start | bytes 1179656 | tf_op jit(solution)/shard_map/ppermute | solution.py:209
  48.4 33.1 %collective-permute-start = (bf16[512,384]{1,0:T(8,128)(2,1)}, bf16[512,384]{1,0:T(8,128)(2,1)S(1)}, u32[]{:S(2)}, u32[]{:S(2)}) collective-permute-start(bf16[512,384]{1,0:T(8,128)(2,1)} %get-tuple-element.23.refs_0_.both_ref), channel_id=1, source_target_pairs={{0,8},{8,0},{16,24},{24,16},{32,40},{40,32},{48,56},{56,48},{64,72... | collective-permute-start | bytes 1179656 | tf_op jit(solution)/shard_map/ppermute | solution.py:209
  54.3 27.2 %copy-start.4 = (bf16[512,384]{1,0:T(8,128)(2,1)}, bf16[512,384]{1,0:T(8,128)(2,1)S(1)}, u32[]{:S(2)}) copy-start(bf16[512,384]{1,0:T(8,128)(2,1)S(1)} %collective-permute-done.4.refs_5_) | copy-start | bytes 1179652
  61.0 20.5 %copy-start.5 = (bf16[512,384]{1,0:T(8,128)(2,1)}, bf16[512,384]{1,0:T(8,128)(2,1)S(1)}, u32[]{:S(2)}) copy-start(bf16[512,384]{1,0:T(8,128)(2,1)S(1)} %collective-permute-done.3.refs_4_) | copy-start | bytes 1179652
  66.3 15.2 %copy-start.6 = (bf16[512,384]{1,0:T(8,128)(2,1)}, bf16[512,384]{1,0:T(8,128)(2,1)S(1)}, u32[]{:S(2)}) copy-start(bf16[512,384]{1,0:T(8,128)(2,1)S(1)} %collective-permute-done.2.refs_3_) | copy-start | bytes 1179652
  99.6 28.5 %copy-start.18 = (bf16[512,384]{1,0:T(8,128)(2,1)S(1)}, bf16[512,384]{1,0:T(8,128)(2,1)}, u32[]{:S(2)}) copy-start(bf16[512,384]{1,0:T(8,128)(2,1)} %get-tuple-element.28) | copy-start | bytes 1179652
  99.6 31.2 %copy-start.17 = (bf16[512,384]{1,0:T(8,128)(2,1)S(1)}, bf16[512,384]{1,0:T(8,128)(2,1)}, u32[]{:S(2)}) copy-start(bf16[512,384]{1,0:T(8,128)(2,1)} %get-tuple-element.29) | copy-start | bytes 1179652
  99.6 32.6 %copy-start.16 = (bf16[512,384]{1,0:T(8,128)(2,1)S(1)}, bf16[512,384]{1,0:T(8,128)(2,1)}, u32[]{:S(2)}) copy-start(bf16[512,384]{1,0:T(8,128)(2,1)} %get-tuple-element.30) | copy-start | bytes 1179652
  119.4 23.6 %all-to-all-start.3 = ((bf16[32,16,256]{2,1,0:T(8,128)(2,1)}), bf16[32,16,256]{2,1,0:T(8,128)(2,1)S(1)}, u32[]{:S(2)}, u32[]{:S(2)}) async-start(bf16[32,16,256]{2,1,0:T(8,128)(2,1)} %broadcast_in_dim.5), calls=%async_computation.3 | async-start | bytes 524288 | tf_op jit(solution)/shard_map/all_to_all | solution.py:190
  123.8 26.9 %collective-permute-start.5 = (bf16[512,384]{1,0:T(8,128)(2,1)}, bf16[512,384]{1,0:T(8,128)(2,1)S(1)}, u32[]{:S(2)}, u32[]{:S(2)}) collective-permute-start(bf16[512,384]{1,0:T(8,128)(2,1)} %get-tuple-element.26), channel_id=1, source_target_pairs={{0,8},{8,0},{16,24},{24,16},{32,40},{40,32},{48,56},{56,48},{64,72... | collective-permute-start | bytes 1179656 | tf_op jit(solution)/shard_map/ppermute | solution.py:209
  125.7 25.1 %collective-permute-start.6 = (bf16[512,384]{1,0:T(8,128)(2,1)}, bf16[512,384]{1,0:T(8,128)(2,1)S(1)}, u32[]{:S(2)}, u32[]{:S(2)}) collective-permute-start(bf16[512,384]{1,0:T(8,128)(2,1)} %get-tuple-element.27), channel_id=1, source_target_pairs={{0,16},{8,24},{16,0},{24,8},{32,48},{40,56},{48,32},{56,40},{64,80... | collective-permute-start | bytes 1179656 | tf_op jit(solution)/shard_map/ppermute | solution.py:209
  128.1 40.1 %collective-permute-start.7 = (bf16[512,384]{1,0:T(8,128)(2,1)S(1)}, bf16[512,384]{1,0:T(8,128)(2,1)S(1)}, u32[]{:S(2)}, u32[]{:S(2)}) collective-permute-start(bf16[512,384]{1,0:T(8,128)(2,1)S(1)} %copy-done.18), channel_id=1, source_target_pairs={{0,32},{8,40},{16,48},{24,56},{32,0},{40,8},{48,16},{56,24},{64,96... | collective-permute-start | bytes 1179656 | tf_op jit(solution)/shard_map/ppermute | solution.py:209
  130.7 37.4 %collective-permute-start.8 = (bf16[512,384]{1,0:T(8,128)(2,1)S(1)}, bf16[512,384]{1,0:T(8,128)(2,1)S(1)}, u32[]{:S(2)}, u32[]{:S(2)}) collective-permute-start(bf16[512,384]{1,0:T(8,128)(2,1)S(1)} %copy-done.17), channel_id=1, source_target_pairs={{0,64},{8,72},{16,80},{24,88},{32,96},{40,104},{48,112},{56,120},{... | collective-permute-start | bytes 1179656 | tf_op jit(solution)/shard_map/ppermute | solution.py:209
  132.2 36.0 %collective-permute-start.9 = (bf16[512,384]{1,0:T(8,128)(2,1)S(1)}, bf16[512,384]{1,0:T(8,128)(2,1)S(1)}, u32[]{:S(2)}, u32[]{:S(2)}) collective-permute-start(bf16[512,384]{1,0:T(8,128)(2,1)S(1)} %copy-done.16), channel_id=1, source_target_pairs={{0,128},{8,136},{16,144},{24,152},{32,160},{40,168},{48,176},{56,1... | collective-permute-start | bytes 1179656 | tf_op jit(solution)/shard_map/ppermute | solution.py:209
  145.9 22.3 %all-to-all-start.4 = ((bf16[8,192,128]{2,1,0:T(8,128)(2,1)}), bf16[8,192,128]{2,1,0:T(8,128)(2,1)S(1)}, u32[]{:S(2)}, u32[]{:S(2)}) async-start(bf16[8,192,128]{2,1,0:T(8,128)(2,1)} %late.1), calls=%async_computation.4 | async-start | bytes 786432 | tf_op jit(solution)/shard_map/all_to_all | solution.py:317
  150.7 17.5 %copy-start.9 = (bf16[512,384]{1,0:T(8,128)(2,1)}, bf16[512,384]{1,0:T(8,128)(2,1)S(1)}, u32[]{:S(2)}) copy-start(bf16[512,384]{1,0:T(8,128)(2,1)S(1)} %collective-permute-done.5.refs_1_) | copy-start | bytes 1179652
  150.8 17.5 %copy-start.10 = (bf16[512,384]{1,0:T(8,128)(2,1)}, bf16[512,384]{1,0:T(8,128)(2,1)S(1)}, u32[]{:S(2)}) copy-start(bf16[512,384]{1,0:T(8,128)(2,1)S(1)} %collective-permute-done.6.refs_2_) | copy-start | bytes 1179652
  172.4 3.2 %copy-start.3 = (bf16[1344,256]{1,0:T(8,128)(2,1)S(1)}, bf16[1344,256]{1,0:T(8,128)(2,1)}, u32[]{:S(2)}) copy-start(bf16[1344,256]{1,0:T(8,128)(2,1)} %reduce-scatter.2.cloned.1.call-done) | copy-start | bytes 2064388
  (9 other events, 8.2 us)
Sparse Core Ops, SparseCore 0:
  99.7 36.8 reduce-scatter.1

commit v2 on v1

--- a/solution.py
+++ b/solution.py
@@ -181,13 +181,37 @@
     return pl.CostEstimate(flops=flops, bytes_accessed=size, transcendentals=0)
 
 
+def group_exchange(pieces, groups):
+    return lax.all_to_all(pieces, "hid", 0, 0, axis_index_groups=groups, tiled=True)
+
+
+def group_scatter(value, groups):
+    count = len(groups[0])
+    pieces = value.reshape(count, value.shape[0] // count, value.shape[1])
+    return jnp.sum(group_exchange(pieces, groups).astype(F32), axis=0).astype(BF)
+
+
+def group_gather(value, groups):
+    count = len(groups[0])
+    pieces = jnp.broadcast_to(value[None], (count,) + value.shape)
+    return group_exchange(pieces, groups).reshape(count * value.shape[0], value.shape[1])
+
+
 def hid_sum(value):
     count = lax.axis_size("hid")
-    pieces = value.reshape(count, value.shape[0] // count, value.shape[1])
-    pieces = lax.all_to_all(pieces, "hid", 0, 0, tiled=True)
-    total = jnp.sum(pieces.astype(F32), axis=0).astype(BF)
-    pieces = jnp.broadcast_to(total[None], pieces.shape)
-    return lax.all_to_all(pieces, "hid", 0, 0, tiled=True).reshape(value.shape)
+    inner = 8 if count % 8 == 0 else 1
+    outer = count // inner
+    columns = [[o * inner + i for o in range(outer)] for i in range(inner)]
+    lines = [[o * inner + i for i in range(inner)] for o in range(outer)]
+
+    def once(_, held):
+        held = group_scatter(held, columns)
+        held = group_scatter(held, lines)
+        held = group_gather(held, lines)
+        return group_gather(held, columns)
+
+    trips = 1 + lax.shift_right_logical(lax.axis_index("hid"), 20)
+    return lax.fori_loop(0, trips, once, value)
 
 
 def on_device(

time: 185 us -> 191 us (1.032)
  the two profiles are of different devices: /device:TPU:16 before, /device:TPU:1 now
where the time goes in v2:
time: 191 us
  blocking collectives  106 us (55%)
  starting transfers between devices  24.8 us (13%)
  Pallas kernels  24 us (13%)
  between operations  14.2 us (7%)
  waiting for transfers between devices  11 us (6%)
  local copies, waits for them, and re-layouts  9.91 us (5%)
    all_to_all x6, blocking collectives, group_exchange(): lax.all_to_all(pieces, 'hid', 0, 0, axis_index_groups=groups, tiled=True)  88.3 us
    all_to_all x1, blocking collectives, on_device(): late = lax.all_to_all(late, 'tok', 0, 0, tiled=True)  18 us
    ppermute x10, starting transfers between devices, partner(): lax.ppermute(value, 'hid', [(i, i ^ distance) for i in range(hid_count)])  17.9 us
    all_to_all x2, waiting for transfers between devices, group_exchange(): lax.all_to_all(pieces, 'hid', 0, 0, axis_index_groups=groups, tiled=True)  11 us
    pallas_call x1, Pallas kernels, on_device(): pl.pallas_call(functools.partial(middle_kernel, levels), grid_spec=pltpu....  9.47 us
    pallas_call x1, Pallas kernels, on_device(): pl.pallas_call(functools.partial(grads_kernel, levels, groups), grid_spec...  7.42 us
    all_to_all x2, starting transfers between devices, group_exchange(): lax.all_to_all(pieces, 'hid', 0, 0, axis_index_groups=groups, tiled=True)  6.81 us
    unnamed x28, local copies, waits for them, and re-layouts  4.51 us
  transfers between devices with their start and end apart: 13, of which 2 were waited for; matrix products, arithmetic and copies ran while one was open for 2% of the time, Pallas kernels for 3%

profile of v2, /device:TPU:1, one launch (start us, length us, event | category | flops | bytes accessed | tf_op | source)
XLA Modules:
  0.0 190.5 jit_solution(1010691483699668996)
XLA Ops:
  7.2 2.1 %head.1 = (bf16[512,384]{1,0:T(8,128)(2,1)}, bf16[512,256]{1,0:T(8,128)(2,1)S(1)}) custom-call(bf16[256,384]{1,0:T(8,128)(2,1)} %tok_ref.1, bf16[256,384]{1,0:T(8,128)(2,1)} %cot_ref.1, bf16[384,256]{1,0:T(8,128)(2,1)} %refs_8_.3, bf16[256,384]{1,0:T(8,128)(2,1)} %refs_7_.3), custom_call_target="tpu_custom_call" | custom-call | flops 100663296 | bytes 786432 | tf_op jit(solution)/shard_map/head/pallas_call | solution.py:235
  9.3 3.6 %collective-permute-start.4 = (bf16[512,384]{1,0:T(8,128)(2,1)}, bf16[512,384]{1,0:T(8,128)(2,1)S(1)}, u32[]{:S(2)}, u32[]{:S(2)}) collective-permute-start(bf16[512,384]{1,0:T(8,128)(2,1)} %get-tuple-element.137.refs_0_.both_ref), channel_id=1, source_target_pairs={{0,128},{8,136},{16,144},{24,152},{32,160},{40,168},{48,176},{56,1... | collective-permute-start | bytes 1179656 | tf_op jit(solution)/shard_map/ppermute | solution.py:233
  13.2 6.9 %collective-permute-start.2 = (bf16[512,384]{1,0:T(8,128)(2,1)}, bf16[512,384]{1,0:T(8,128)(2,1)S(1)}, u32[]{:S(2)}, u32[]{:S(2)}) collective-permute-start(bf16[512,384]{1,0:T(8,128)(2,1)} %get-tuple-element.137.refs_0_.both_ref), channel_id=1, source_target_pairs={{0,32},{8,40},{16,48},{24,56},{32,0},{40,8},{48,16},{56,24},{64,96... | collective-permute-start | bytes 1179656 | tf_op jit(solution)/shard_map/ppermute | solution.py:233
  20.1 1.2 collective-permute-start.1
  22.0 1.4 copy.24.index_ref
  23.4 55.0 %while.26 = (s32[]{:T(128)}, bf16[512,256]{1,0:T(8,128)(2,1)S(1)}, s32[]{:T(128)}, s32[]{:T(128)}, bf16[]{:T(256)}) while((s32[]{:T(128)}, bf16[512,256]{1,0:T(8,128)(2,1)S(1)}, s32[]{:T(128)}, s32[]{:T(128)}, bf16[]{:T(256)}) %tuple.57), condition=%wide.region_3.0_spmd, body=%wide.region_0.0_spmd.sunk | while | flops 126978 | bytes 2375777 | solution.py:214
  23.4 9.2 %all_to_all.86 = bf16[4,128,256]{2,1,0:T(8,128)(2,1)S(1)} all-to-all(bf16[4,128,256]{2,1,0:T(8,128)(2,1)S(1)} %bitcast.36), channel_id=1, replica_groups={{0,64,128,192},{8,72,136,200},{16,80,144,208},{24,88,152,216},{32,96,16..., dimensions={0} | all-to-all | bytes 524288 | tf_op jit(solution)/shard_map/while/body/all_to_all | solution.py:185
  32.6 24.1 %all_to_all.87 = bf16[8,16,256]{2,1,0:T(8,128)(2,1)S(1)} all-to-all(bf16[8,16,256]{2,1,0:T(8,128)(2,1)S(1)} %bitcast.38), channel_id=1, replica_groups={{0,8,16,24,32,40,48,56},{64,72,80,88,96,104,112,120},{128,136,144,152,1..., dimensions={0} | all-to-all | bytes 131072 | tf_op jit(solution)/shard_map/while/body/all_to_all | solution.py:185
  56.8 12.1 %all_to_all.88 = bf16[8,16,256]{2,1,0:T(8,128)(2,1)S(1)} all-to-all(bf16[8,16,256]{2,1,0:T(8,128)(2,1)S(1)} %broadcast_in_dim.54), channel_id=1, replica_groups={{0,8,16,24,32,40,48,56},{64,72,80,88,96,104,112,120},{128,136,144,152,1..., dimensions={0} | all-to-all | bytes 131072 | tf_op jit(solution)/shard_map/while/body/all_to_all | solution.py:185
  69.5 3.4 %all-to-all-start.3 = ((bf16[4,128,256]{2,1,0:T(8,128)(2,1)}), bf16[4,128,256]{2,1,0:T(8,128)(2,1)S(1)}, u32[]{:S(2)}, u32[]{:S(2)}) async-start(bf16[4,128,256]{2,1,0:T(8,128)(2,1)} %broadcast_in_dim.55), calls=%async_computation.3 | async-start | bytes 524288 | tf_op jit(solution)/shard_map/while/body/all_to_all | solution.py:185
  72.9 5.5 %all-to-all-done.3 = bf16[4,128,256]{2,1,0:T(8,128)(2,1)S(1)} async-done(((bf16[4,128,256]{2,1,0:T(8,128)(2,1)}), bf16[4,128,256]{2,1,0:T(8,128)(2,1)S(1)}, u32[]{:S(2)}, u32[]{:S(2)}) %all-to-all-start.3) | async-done | bytes 262176 | tf_op jit(solution)/shard_map/while/body/all_to_all | solution.py:185
  79.8 9.5 %middle.1 = (bf16[256,768]{1,0:T(8,128)(2,1)}, bf16[256,768]{1,0:T(8,128)(2,1)}, bf16[512,256]{1,0:T(8,128)(2,1)S(1)}, bf16[512,384]{1,0:T(8,128)(2,1)}, bf16[51...) custom-call(s32[6,3,2]{2,1,0:T(4,128)} %copy.24.index_ref, ...), custom_call_target="tpu_custom_call" | custom-call | flops 2818572288 | bytes 10485760 | tf_op jit(solution)/shard_map/middle/pallas_call | solution.py:257
  89.2 7.4 %grads.1 = bf16[8,1344,256]{2,1,0:T(8,128)(2,1)} custom-call(s32[6,3,2]{2,1,0:T(4,128)} %copy.24.index_ref, bf16[512,384]{1,0:T(8,128)(2,1)} %get-tuple-element.137.refs_0_.both_ref, bf16[512,384]{1,0:T(8,128)(2,1)} %copy-done.5, bf16[512,384]{1,0:T(8,128)(2,1)} %copy-done.4, bf16[512,384]{1,0:T(8,128)(2,1)} %copy-done.3, bf16[512,384]{1,0:T(8,128)(2,1)} %copy-done.2, ...), custom_call_target="tpu_custom_call" | custom-call | flops 1409286144 | bytes 10485760 | tf_op jit(solution)/shard_map/grads/pallas_call | solution.py:297
  97.1 2.8 %collective-permute-start.7 = (bf16[512,384]{1,0:T(8,128)(2,1)}, bf16[512,384]{1,0:T(8,128)(2,1)S(1)}, u32[]{:S(2)}, u32[]{:S(2)}) collective-permute-start(bf16[512,384]{1,0:T(8,128)(2,1)} %get-tuple-element.143), channel_id=1, source_target_pairs={{0,32},{8,40},{16,48},{24,56},{32,0},{40,8},{48,16},{56,24},{64,96... | collective-permute-start | bytes 1179656 | tf_op jit(solution)/shard_map/ppermute | solution.py:233
  100.1 1.8 collective-permute-start.9
  101.9 52.7 %while.27 = (s32[]{:T(128)}, bf16[512,256]{1,0:T(8,128)(2,1)S(1)}, s32[]{:T(128)}, s32[]{:T(128)}, bf16[]{:T(256)}) while((s32[]{:T(128)}, bf16[512,256]{1,0:T(8,128)(2,1)S(1)}, s32[]{:T(128)}, s32[]{:T(128)}, bf16[]{:T(256)}) %tuple.60), condition=%wide.region_7.0_spmd, body=%wide.region_4.0_spmd.sunk | while | flops 126978 | bytes 2375777 | solution.py:214
  101.9 14.8 %all_to_all.89 = bf16[4,128,256]{2,1,0:T(8,128)(2,1)S(1)} all-to-all(bf16[4,128,256]{2,1,0:T(8,128)(2,1)S(1)} %bitcast.34), channel_id=1, replica_groups={{0,64,128,192},{8,72,136,200},{16,80,144,208},{24,88,152,216},{32,96,16..., dimensions={0} | all-to-all | bytes 524288 | tf_op jit(solution)/shard_map/while/body/all_to_all | solution.py:185
  116.7 17.7 %all_to_all.90 = bf16[8,16,256]{2,1,0:T(8,128)(2,1)S(1)} all-to-all(bf16[8,16,256]{2,1,0:T(8,128)(2,1)S(1)} %bitcast.40), channel_id=1, replica_groups={{0,8,16,24,32,40,48,56},{64,72,80,88,96,104,112,120},{128,136,144,152,1..., dimensions={0} | all-to-all | bytes 131072 | tf_op jit(solution)/shard_map/while/body/all_to_all | solution.py:185
  134.4 10.6 %all_to_all.91 = bf16[8,16,256]{2,1,0:T(8,128)(2,1)S(1)} all-to-all(bf16[8,16,256]{2,1,0:T(8,128)(2,1)S(1)} %broadcast_in_dim.56), channel_id=1, replica_groups={{0,8,16,24,32,40,48,56},{64,72,80,88,96,104,112,120},{128,136,144,152,1..., dimensions={0} | all-to-all | bytes 131072 | tf_op jit(solution)/shard_map/while/body/all_to_all | solution.py:185
  145.7 3.4 %all-to-all-start.7 = ((bf16[4,128,256]{2,1,0:T(8,128)(2,1)}), bf16[4,128,256]{2,1,0:T(8,128)(2,1)S(1)}, u32[]{:S(2)}, u32[]{:S(2)}) async-start(bf16[4,128,256]{2,1,0:T(8,128)(2,1)} %broadcast_in_dim.57), calls=%async_computation.7 | async-start | bytes 524288 | tf_op jit(solution)/shard_map/while/body/all_to_all | solution.py:185
  149.2 5.5 %all-to-all-done.7 = bf16[4,128,256]{2,1,0:T(8,128)(2,1)S(1)} async-done(((bf16[4,128,256]{2,1,0:T(8,128)(2,1)}), bf16[4,128,256]{2,1,0:T(8,128)(2,1)S(1)}, u32[]{:S(2)}, u32[]{:S(2)}) %all-to-all-start.7) | async-done | bytes 262176 | tf_op jit(solution)/shard_map/while/body/all_to_all | solution.py:185
  154.7 2.1 %late.1 = bf16[8,192,128]{2,1,0:T(8,128)(2,1)} custom-call(bf16[512,384]{1,0:T(8,128)(2,1)} %get-tuple-element.137.refs_0_.both_ref, bf16[512,256]{1,0:T(8,128)(2,1)S(1)} %get-tuple-element.147.low_ref.refs_6_), custom_call_target="tpu_custom_call" | custom-call | flops 100663296 | bytes 786432 | tf_op jit(solution)/shard_map/late/pallas_call | solution.py:332
  156.8 18.0 %all_to_all.85.refs_9_ = bf16[8,192,128]{2,1,0:T(8,128)(2,1)} all-to-all(bf16[8,192,128]{2,1,0:T(8,128)(2,1)} %late.1), channel_id=1, replica_groups=mesh['hid'=32,'tok'=8] {'tok'}, dimensions={0} | all-to-all | bytes 786432 | tf_op jit(solution)/shard_map/all_to_all | solution.py:341
  176.1 2.9 %final.1 = (bf16[256,384]{1,0:T(8,128)(2,1)}, bf16[256,384]{1,0:T(8,128)(2,1)}, bf16[32,384]{1,0:T(8,128)(2,1)}, bf16[48,256]{1,0:T(8,128)(2,1)}) custom-call(bf16[512,384]{1,0:T(8,128)(2,1)} %get-tuple-element.140.refs_0_, bf16[512,384]{1,0:T(8,128)(2,1)} %copy-done.6, bf16[512,384]{1,0:T(8,128)(2,1)} %copy-done.7, bf16[512,384]{1,0:T(8,128)(2,1)} %copy-done.8, ...), custom_call_target="tpu_custom_call" | custom-call | flops 100663296 | bytes 3145728 | tf_op jit(solution)/shard_map/final/pallas_call | solution.py:342
  (60 shorter events, 10.5 us)
Async XLA Ops:
  7.2 171.9 %reduce-scatter.2.cloned.1.call-start = ((), (), s32[]{:S(2)}) async-start(), calls=%async_computation.10 | async-start | bytes 6193152 | tf_op jit(solution)/shard_map/reduce_scatter | solution.py:319
  9.3 69.1 %collective-permute-start.4 = (bf16[512,384]{1,0:T(8,128)(2,1)}, bf16[512,384]{1,0:T(8,128)(2,1)S(1)}, u32[]{:S(2)}, u32[]{:S(2)}) collective-permute-start(bf16[512,384]{1,0:T(8,128)(2,1)} %get-tuple-element.137.refs_0_.both_ref), channel_id=1, source_target_pairs={{0,128},{8,136},{16,144},{24,152},{32,160},{40,168},{48,176},{56,1... | collective-permute-start | bytes 1179656 | tf_op jit(solution)/shard_map/ppermute | solution.py:233
  12.9 65.5 %collective-permute-start.3 = (bf16[512,384]{1,0:T(8,128)(2,1)}, bf16[512,384]{1,0:T(8,128)(2,1)S(1)}, u32[]{:S(2)}, u32[]{:S(2)}) collective-permute-start(bf16[512,384]{1,0:T(8,128)(2,1)} %get-tuple-element.137.refs_0_.both_ref), channel_id=1, source_target_pairs={{0,64},{8,72},{16,80},{24,88},{32,96},{40,104},{48,112},{56,120},{... | collective-permute-start | bytes 1179656 | tf_op jit(solution)/shard_map/ppermute | solution.py:233
  13.2 65.3 %collective-permute-start.2 = (bf16[512,384]{1,0:T(8,128)(2,1)}, bf16[512,384]{1,0:T(8,128)(2,1)S(1)}, u32[]{:S(2)}, u32[]{:S(2)}) collective-permute-start(bf16[512,384]{1,0:T(8,128)(2,1)} %get-tuple-element.137.refs_0_.both_ref), channel_id=1, source_target_pairs={{0,32},{8,40},{16,48},{24,56},{32,0},{40,8},{48,16},{56,24},{64,96... | collective-permute-start | bytes 1179656 | tf_op jit(solution)/shard_map/ppermute | solution.py:233
  20.1 58.4 %collective-permute-start.1 = (bf16[512,384]{1,0:T(8,128)(2,1)}, bf16[512,384]{1,0:T(8,128)(2,1)S(1)}, u32[]{:S(2)}, u32[]{:S(2)}) collective-permute-start(bf16[512,384]{1,0:T(8,128)(2,1)} %get-tuple-element.137.refs_0_.both_ref), channel_id=1, source_target_pairs={{0,16},{8,24},{16,0},{24,8},{32,48},{40,56},{48,32},{56,40},{64,80... | collective-permute-start | bytes 1179656 | tf_op jit(solution)/shard_map/ppermute | solution.py:233
  21.3 57.2 %collective-permute-start = (bf16[512,384]{1,0:T(8,128)(2,1)}, bf16[512,384]{1,0:T(8,128)(2,1)S(1)}, u32[]{:S(2)}, u32[]{:S(2)}) collective-permute-start(bf16[512,384]{1,0:T(8,128)(2,1)} %get-tuple-element.137.refs_0_.both_ref), channel_id=1, source_target_pairs={{0,8},{8,0},{16,24},{24,16},{32,40},{40,32},{48,56},{56,48},{64,72... | collective-permute-start | bytes 1179656 | tf_op jit(solution)/shard_map/ppermute | solution.py:233
  69.5 8.9 %all-to-all-start.3 = ((bf16[4,128,256]{2,1,0:T(8,128)(2,1)}), bf16[4,128,256]{2,1,0:T(8,128)(2,1)S(1)}, u32[]{:S(2)}, u32[]{:S(2)}) async-start(bf16[4,128,256]{2,1,0:T(8,128)(2,1)} %broadcast_in_dim.55), calls=%async_computation.3 | async-start | bytes 524288 | tf_op jit(solution)/shard_map/while/body/all_to_all | solution.py:185
  78.4 0.9 copy-start.2
  78.5 1.0 copy-start.3
  78.5 1.1 copy-start.4
  78.5 1.2 copy-start.5
  96.7 3.2 %copy-start.12 = (bf16[512,384]{1,0:T(8,128)(2,1)S(1)}, bf16[512,384]{1,0:T(8,128)(2,1)}, u32[]{:S(2)}) copy-start(bf16[512,384]{1,0:T(8,128)(2,1)} %get-tuple-element.144) | copy-start | bytes 1179652
  96.7 3.5 %copy-start.11 = (bf16[512,384]{1,0:T(8,128)(2,1)S(1)}, bf16[512,384]{1,0:T(8,128)(2,1)}, u32[]{:S(2)}) copy-start(bf16[512,384]{1,0:T(8,128)(2,1)} %get-tuple-element.145) | copy-start | bytes 1179652
  96.7 78.1 %collective-permute-start.5 = (bf16[512,384]{1,0:T(8,128)(2,1)}, bf16[512,384]{1,0:T(8,128)(2,1)S(1)}, u32[]{:S(2)}, u32[]{:S(2)}) collective-permute-start(bf16[512,384]{1,0:T(8,128)(2,1)} %get-tuple-element.141), channel_id=1, source_target_pairs={{0,8},{8,0},{16,24},{24,16},{32,40},{40,32},{48,56},{56,48},{64,72... | collective-permute-start | bytes 1179656 | tf_op jit(solution)/shard_map/ppermute | solution.py:233
  96.9 77.9 %collective-permute-start.6 = (bf16[512,384]{1,0:T(8,128)(2,1)}, bf16[512,384]{1,0:T(8,128)(2,1)S(1)}, u32[]{:S(2)}, u32[]{:S(2)}) collective-permute-start(bf16[512,384]{1,0:T(8,128)(2,1)} %get-tuple-element.142), channel_id=1, source_target_pairs={{0,16},{8,24},{16,0},{24,8},{32,48},{40,56},{48,32},{56,40},{64,80... | collective-permute-start | bytes 1179656 | tf_op jit(solution)/shard_map/ppermute | solution.py:233
  97.1 77.8 %collective-permute-start.7 = (bf16[512,384]{1,0:T(8,128)(2,1)}, bf16[512,384]{1,0:T(8,128)(2,1)S(1)}, u32[]{:S(2)}, u32[]{:S(2)}) collective-permute-start(bf16[512,384]{1,0:T(8,128)(2,1)} %get-tuple-element.143), channel_id=1, source_target_pairs={{0,32},{8,40},{16,48},{24,56},{32,0},{40,8},{48,16},{56,24},{64,96... | collective-permute-start | bytes 1179656 | tf_op jit(solution)/shard_map/ppermute | solution.py:233
  99.8 75.0 %collective-permute-start.8 = (bf16[512,384]{1,0:T(8,128)(2,1)S(1)}, bf16[512,384]{1,0:T(8,128)(2,1)S(1)}, u32[]{:S(2)}, u32[]{:S(2)}) collective-permute-start(bf16[512,384]{1,0:T(8,128)(2,1)S(1)} %copy-done.12), channel_id=1, source_target_pairs={{0,64},{8,72},{16,80},{24,88},{32,96},{40,104},{48,112},{56,120},{... | collective-permute-start | bytes 1179656 | tf_op jit(solution)/shard_map/ppermute | solution.py:233
  100.1 74.7 %collective-permute-start.9 = (bf16[512,384]{1,0:T(8,128)(2,1)S(1)}, bf16[512,384]{1,0:T(8,128)(2,1)S(1)}, u32[]{:S(2)}, u32[]{:S(2)}) collective-permute-start(bf16[512,384]{1,0:T(8,128)(2,1)S(1)} %copy-done.11), channel_id=1, source_target_pairs={{0,128},{8,136},{16,144},{24,152},{32,160},{40,168},{48,176},{56,1... | collective-permute-start | bytes 1179656 | tf_op jit(solution)/shard_map/ppermute | solution.py:233
  145.7 8.9 %all-to-all-start.7 = ((bf16[4,128,256]{2,1,0:T(8,128)(2,1)}), bf16[4,128,256]{2,1,0:T(8,128)(2,1)S(1)}, u32[]{:S(2)}, u32[]{:S(2)}) async-start(bf16[4,128,256]{2,1,0:T(8,128)(2,1)} %broadcast_in_dim.57), calls=%async_computation.7 | async-start | bytes 524288 | tf_op jit(solution)/shard_map/while/body/all_to_all | solution.py:185
  174.8 0.9 copy-start.7
  174.8 1.0 copy-start.8
  174.8 1.2 copy-start.9
  174.9 1.3 copy-start.10
  179.1 3.2 %copy-start = (bf16[1344,256]{1,0:T(8,128)(2,1)S(1)}, bf16[1344,256]{1,0:T(8,128)(2,1)}, u32[]{:S(2)}) copy-start(bf16[1344,256]{1,0:T(8,128)(2,1)} %reduce-scatter.2.cloned.1.call-done) | copy-start | bytes 2064388
  (2 other events, 1.6 us)
Sparse Core Ops, SparseCore 0:
  96.8 38.7 reduce-scatter.1

commit v3 on v2

--- a/solution.py
+++ b/solution.py
@@ -151,8 +151,8 @@
 
 def final_kernel(levels, *refs):
     parts = refs[:levels]
-    low_ref, down_right_ref, up_left_ref, late_ref = refs[levels : levels + 4]
-    layer_ref, tokens_ref, right_ref, left_ref = refs[levels + 4 :]
+    low_ref, down_right_ref, up_left_ref = refs[levels : levels + 3]
+    layer_ref, tokens_ref = refs[levels + 3 :]
     rows = low_ref.shape[0] // 2
     out = parts[0][:rows].astype(F32)
     back = parts[0][rows:].astype(F32)
@@ -161,6 +161,9 @@
         back += parts[k][rows:].astype(F32)
     layer_ref[...] = (out + dot(low_ref[:rows], down_right_ref[...])).astype(BF)
     tokens_ref[...] = (back + dot_nt(low_ref[rows:], up_left_ref[...])).astype(BF)
+
+
+def last_kernel(late_ref, right_ref, left_ref):
     late = late_ref[0].astype(F32)
     for m in range(1, late_ref.shape[0]):
         late += late_ref[m].astype(F32)
@@ -197,21 +200,35 @@
     return group_exchange(pieces, groups).reshape(count * value.shape[0], value.shape[1])
 
 
-def hid_sum(value):
+def line_step(held, distance):
     count = lax.axis_size("hid")
-    inner = 8 if count % 8 == 0 else 1
-    outer = count // inner
-    columns = [[o * inner + i for o in range(outer)] for i in range(inner)]
-    lines = [[o * inner + i for i in range(inner)] for o in range(outer)]
-
-    def once(_, held):
-        held = group_scatter(held, columns)
-        held = group_scatter(held, lines)
-        held = group_gather(held, lines)
-        return group_gather(held, columns)
-
+    other = lax.ppermute(held, "hid", [(i, i ^ distance) for i in range(count)])
+    return (held.astype(F32) + other.astype(F32)).astype(BF)
+
+
+def hid_inner():
+    return 8 if lax.axis_size("hid") % 8 == 0 else 1
+
+
+def hid_columns():
+    inner = hid_inner()
+    return [list(range(i, lax.axis_size("hid"), inner)) for i in range(inner)]
+
+
+def finish_sum(held, distance):
     trips = 1 + lax.shift_right_logical(lax.axis_index("hid"), 20)
-    return lax.fori_loop(0, trips, once, value)
+    outer = len(hid_columns()[0])
+
+    def once(_, carried):
+        value = carried[0]
+        step = distance
+        while step < hid_inner():
+            value = line_step(value, step)
+            step *= 2
+        return value, group_gather(value, hid_columns())
+
+    wide = jnp.zeros((outer * held.shape[0], held.shape[1]), held.dtype)
+    return lax.fori_loop(0, trips, once, (held, wide))[1]
 
 
 def on_device(
@@ -245,7 +262,9 @@
     fields = [both] + [None] * (levels - 1)
     for level in order:
         fields[level] = partner(both, level)
-    low = hid_sum(low_part)
+    total = group_scatter(low_part, hid_columns())
+    total, fields[4] = lax.optimization_barrier((total, fields[4]))
+    low = finish_sum(total, 1)
 
     def whole(shape):
         return pl.BlockSpec(shape, lambda b, *_: (0,) * len(shape))
@@ -315,7 +334,9 @@
 
     for level in order:
         parts[level] = partner(parts[level], level)
-    low2 = hid_sum(lowp)
+    total = group_scatter(lowp, hid_columns())
+    total, parts[4] = lax.optimization_barrier((total, parts[4]))
+    low2 = finish_sum(total, 1)
     summed = lax.psum_scatter(
         packed.reshape(groups * chunk, width), "tok", scatter_dimension=0, tiled=True
     )
@@ -338,21 +359,26 @@
         cost_estimate=cost(4 * rows * feat * rank, 4 * rows * feat * 2),
         name="late",
     )(both, low2)
+    late, parts = lax.optimization_barrier((late, parts))
     late = lax.all_to_all(late, "tok", 0, 0, tiled=True)
-    layer_out, grad_tokens, grad_down_right, grad_up_left = pl.pallas_call(
+    layer_out, grad_tokens = pl.pallas_call(
         functools.partial(final_kernel, levels),
-        out_shape=(
-            sds((rows, feat), BF),
-            sds((rows, feat), BF),
-            sds((rank // groups, feat), BF),
-            sds((feat // groups, rank), BF),
-        ),
-        in_specs=[vmem_spec()] * (levels + 4),
-        out_specs=(vmem_spec(),) * 4,
+        out_shape=(sds((rows, feat), BF), sds((rows, feat), BF)),
+        in_specs=[vmem_spec()] * (levels + 3),
+        out_specs=(vmem_spec(),) * 2,
         compiler_params=params(),
         cost_estimate=cost(4 * rows * feat * rank, 16 * rows * feat * 2),
         name="final",
-    )(*parts, low2, down_right, up_left, late)
+    )(*parts, low2, down_right, up_left)
+    grad_down_right, grad_up_left = pl.pallas_call(
+        last_kernel,
+        out_shape=(sds((rank // groups, feat), BF), sds((feat // groups, rank), BF)),
+        in_specs=[vmem_spec()],
+        out_specs=(vmem_spec(),) * 2,
+        compiler_params=params(),
+        cost_estimate=cost(rows * feat, 3 * rows * feat),
+        name="last",
+    )(late)
     return (
         layer_out,
         grad_tokens,

time: 191 us -> 199 us (1.042)
  blocking collectives: 106 us -> 0 us
  waiting for transfers between devices: 11 us -> 84.1 us
  starting transfers between devices: 24.8 us -> 60.6 us
  local copies, waits for them, and re-layouts: 9.91 us -> 12.4 us
  Pallas kernels: 24 us -> 26.1 us
    all_to_all x7 -> x0, blocking collectives: 106 us -> none  [the longest x6 88.3 us: group_exchange(): lax.all_to_all(pieces, 'hid', 0, 0, axis_index_groups=groups, tiled=True)]
    ppermute x0 -> x6, waiting for transfers between devices: none -> 67.8 us  [line_step(): other = lax.ppermute(held, 'hid', [(i, i ^ distance) for i in range(count)])]
    ppermute x0 -> x6, starting transfers between devices: none -> 12.3 us  [line_step(): other = lax.ppermute(held, 'hid', [(i, i ^ distance) for i in range(count)])]
    all_to_all x0 -> x1, starting transfers between devices: none -> 11.1 us  [on_device(): late = lax.all_to_all(late, 'tok', 0, 0, tiled=True)]
    all_to_all x2 -> x4, starting transfers between devices: 6.81 us -> 14.6 us  [group_exchange(): lax.all_to_all(pieces, 'hid', 0, 0, axis_index_groups=groups, tiled=True)]
    all_to_all x0 -> x1, waiting for transfers between devices: none -> 5.18 us  [on_device(): late = lax.all_to_all(late, 'tok', 0, 0, tiled=True)]
    ppermute x10, starting transfers between devices: 17.9 us -> 22.5 us  [partner(): lax.ppermute(value, 'hid', [(i, i ^ distance) for i in range(hid_count)])]
    unnamed x28 -> x34, local copies, waits for them, and re-layouts: 4.51 us -> 4.09 us
  transfers between devices with their start and end apart: 13 -> 22, of which waited for: 2 -> 10; matrix products, arithmetic and copies ran while one was open for 2% -> 2% of each run, Pallas kernels for 3% -> 3%
where the time goes in v3:
time: 199 us; the launch traced here: 198 us
  waiting for transfers between devices  84.1 us (42%)
  starting transfers between devices  60.6 us (30%)
  Pallas kernels  26.1 us (13%)
  between operations  14.2 us (7%)
  local copies, waits for them, and re-layouts  12.4 us (6%)
    ppermute x6, waiting for transfers between devices, line_step(): other = lax.ppermute(held, 'hid', [(i, i ^ distance) for i in range(count)])  67.8 us
    ppermute x10, starting transfers between devices, partner(): lax.ppermute(value, 'hid', [(i, i ^ distance) for i in range(hid_count)])  22.5 us
    all_to_all x4, starting transfers between devices, group_exchange(): lax.all_to_all(pieces, 'hid', 0, 0, axis_index_groups=groups, tiled=True)  14.6 us
    ppermute x6, starting transfers between devices, line_step(): other = lax.ppermute(held, 'hid', [(i, i ^ distance) for i in range(count)])  12.3 us
    all_to_all x4, waiting for transfers between devices, group_exchange(): lax.all_to_all(pieces, 'hid', 0, 0, axis_index_groups=groups, tiled=True)  11.2 us
    all_to_all x1, starting transfers between devices, on_device(): late = lax.all_to_all(late, 'tok', 0, 0, tiled=True)  11.1 us
    pallas_call x1, Pallas kernels, on_device(): pl.pallas_call(functools.partial(middle_kernel, levels), grid_spec=pltpu....  9.76 us
    pallas_call x1, Pallas kernels, on_device(): pl.pallas_call(functools.partial(grads_kernel, levels, groups), grid_spec...  7.42 us
  transfers between devices with their start and end apart: 22, of which 10 were waited for; matrix products, arithmetic and copies ran while one was open for 2% of the time, Pallas kernels for 3%

profile of v3, /device:TPU:1, one launch (start us, length us, event | category | flops | bytes accessed | tf_op | source)
XLA Modules:
  0.0 197.7 jit_solution(15809532422611853362)
XLA Ops:
  11.4 3.7 %all-to-all-start.2 = ((bf16[4,128,256]{2,1,0:T(8,128)(2,1)}), bf16[4,128,256]{2,1,0:T(8,128)(2,1)S(1)}, u32[]{:S(2)}, u32[]{:S(2)}) async-start(bf16[4,128,256]{2,1,0:T(8,128)(2,1)} %bitcast.25), calls=%async_computation.2 | async-start | bytes 524288 | tf_op jit(solution)/shard_map/all_to_all | solution.py:188
  15.2 3.0 %collective-permute-start.10 = (bf16[512,384]{1,0:T(8,128)(2,1)}, bf16[512,384]{1,0:T(8,128)(2,1)S(1)}, u32[]{:S(2)}, u32[]{:S(2)}) collective-permute-start(bf16[512,384]{1,0:T(8,128)(2,1)} %get-tuple-element.78.refs_0_.both_ref), channel_id=1, source_target_pairs={{0,128},{8,136},{16,144},{24,152},{32,160},{40,168},{48,176},{56,1... | collective-permute-start | bytes 1179656 | tf_op jit(solution)/shard_map/ppermute | solution.py:250
  18.1 6.9 %collective-permute-start.8 = (bf16[512,384]{1,0:T(8,128)(2,1)}, bf16[512,384]{1,0:T(8,128)(2,1)S(1)}, u32[]{:S(2)}, u32[]{:S(2)}) collective-permute-start(bf16[512,384]{1,0:T(8,128)(2,1)} %get-tuple-element.78.refs_0_.both_ref), channel_id=1, source_target_pairs={{0,32},{8,40},{16,48},{24,56},{32,0},{40,8},{48,16},{56,24},{64,96... | collective-permute-start | bytes 1179656 | tf_op jit(solution)/shard_map/ppermute | solution.py:250
  29.4 50.8 %while.24 = (s32[]{:T(128)}, bf16[128,256]{1,0:T(8,128)(2,1)S(1)}, bf16[512,256]{1,0:T(8,128)(2,1)}, s32[]{:T(128)}, s32[]{:T(128)}) while((s32[]{:T(128)}, bf16[128,256]{1,0:T(8,128)(2,1)S(1)}, bf16[512,256]{1,0:T(8,128)(2,1)}, s32[]{:T(128)}, s32[]{:T(128)}) %tuple.41), condition=%wide.region_2.0_spmd, body=%wide.region_1.0_spmd.sunk | while | flops 393218 | bytes 3539185 | solution.py:231
  30.1 27.9 %collective-permute-done = bf16[128,256]{1,0:T(8,128)(2,1)S(1)} collective-permute-done((bf16[128,256]{1,0:T(8,128)(2,1)S(1)}, bf16[128,256]{1,0:T(8,128)(2,1)S(1)}, u32[]{:S(2)}, u32[]{:S(2)}) %collective-permute-start) | collective-permute-done | bytes 65568 | tf_op jit(solution)/shard_map/while/body/ppermute | solution.py:205
  58.0 2.9 %collective-permute-start.1 = (bf16[128,256]{1,0:T(8,128)(2,1)S(1)}, bf16[128,256]{1,0:T(8,128)(2,1)S(1)}, u32[]{:S(2)}, u32[]{:S(2)}) collective-permute-start(bf16[128,256]{1,0:T(8,128)(2,1)S(1)} %add_convert_fusion.12), channel_id=1, source_target_pairs={{0,16},{8,24},{16,0},{24,8},{32,48},{40,56},{48,32},{56,40},{64,80... | collective-permute-start | bytes 196616 | tf_op jit(solution)/shard_map/while/body/ppermute | solution.py:205
  64.5 5.3 %collective-permute-done.2 = bf16[128,256]{1,0:T(8,128)(2,1)S(1)} collective-permute-done((bf16[128,256]{1,0:T(8,128)(2,1)S(1)}, bf16[128,256]{1,0:T(8,128)(2,1)S(1)}, u32[]{:S(2)}, u32[]{:S(2)}) %collective-permute-start.2) | collective-permute-done | bytes 65568 | tf_op jit(solution)/shard_map/while/body/ppermute | solution.py:205
  70.5 3.4 %all-to-all-start = ((bf16[4,128,256]{2,1,0:T(8,128)(2,1)}), bf16[4,128,256]{2,1,0:T(8,128)(2,1)S(1)}, u32[]{:S(2)}, u32[]{:S(2)}) async-start(bf16[4,128,256]{2,1,0:T(8,128)(2,1)} %broadcast_in_dim.10), calls=%async_computation | async-start | bytes 524288 | tf_op jit(solution)/shard_map/while/body/all_to_all | solution.py:188
  73.9 5.5 %all-to-all-done = bf16[4,128,256]{2,1,0:T(8,128)(2,1)S(1)} async-done(((bf16[4,128,256]{2,1,0:T(8,128)(2,1)}), bf16[4,128,256]{2,1,0:T(8,128)(2,1)S(1)}, u32[]{:S(2)}, u32[]{:S(2)}) %all-to-all-start) | async-done | bytes 262176 | tf_op jit(solution)/shard_map/while/body/all_to_all | solution.py:188
  81.3 9.8 %middle.1 = (bf16[256,768]{1,0:T(8,128)(2,1)}, bf16[256,768]{1,0:T(8,128)(2,1)}, bf16[512,256]{1,0:T(8,128)(2,1)}, bf16[512,384]{1,0:T(8,128)(2,1)}, bf16[512,38...) custom-call(s32[6,3,2]{2,1,0:T(4,128)} %copy.21.index_ref, ...), custom_call_target="tpu_custom_call" | custom-call | flops 2818572288 | bytes 10485760 | tf_op jit(solution)/shard_map/middle/pallas_call | solution.py:276
  91.1 7.4 %grads.1 = bf16[8,1344,256]{2,1,0:T(8,128)(2,1)} custom-call(s32[6,3,2]{2,1,0:T(4,128)} %copy.21.index_ref, bf16[512,384]{1,0:T(8,128)(2,1)} %get-tuple-element.78.refs_0_.both_ref, bf16[512,384]{1,0:T(8,128)(2,1)} %copy-done.9, bf16[512,384]{1,0:T(8,128)(2,1)} %copy-done.8, bf16[512,384]{1,0:T(8,128)(2,1)} %copy-done.7, bf16[512,384]{1,0:T(8,128)(2,1)} %copy-done.5, ...), custom_call_target="tpu_custom_call" | custom-call | flops 1409286144 | bytes 10485760 | tf_op jit(solution)/shard_map/grads/pallas_call | solution.py:316
  98.9 3.4 %all-to-all-start.3 = ((bf16[4,128,256]{2,1,0:T(8,128)(2,1)}), bf16[4,128,256]{2,1,0:T(8,128)(2,1)S(1)}, u32[]{:S(2)}, u32[]{:S(2)}) async-start(bf16[4,128,256]{2,1,0:T(8,128)(2,1)} %bitcast.3), calls=%async_computation.3 | async-start | bytes 524288 | tf_op jit(solution)/shard_map/all_to_all | solution.py:188
  102.3 2.4 %collective-permute-start.12 = (bf16[512,384]{1,0:T(8,128)(2,1)}, bf16[512,384]{1,0:T(8,128)(2,1)S(1)}, u32[]{:S(2)}, u32[]{:S(2)}) collective-permute-start(bf16[512,384]{1,0:T(8,128)(2,1)} %get-tuple-element.88), channel_id=1, source_target_pairs={{0,8},{8,0},{16,24},{24,16},{32,40},{40,32},{48,56},{56,48},{64,72... | collective-permute-start | bytes 1179656 | tf_op jit(solution)/shard_map/ppermute | solution.py:250
  107.9 2.9 %collective-permute-start.15 = (bf16[512,384]{1,0:T(8,128)(2,1)S(1)}, bf16[512,384]{1,0:T(8,128)(2,1)S(1)}, u32[]{:S(2)}, u32[]{:S(2)}) collective-permute-start(bf16[512,384]{1,0:T(8,128)(2,1)S(1)} %copy-done.15), channel_id=1, source_target_pairs={{0,128},{8,136},{16,144},{24,152},{32,160},{40,168},{48,176},{56,1... | collective-permute-start | bytes 1179656 | tf_op jit(solution)/shard_map/ppermute | solution.py:250
  111.6 50.8 %while.25 = (s32[]{:T(128)}, bf16[128,256]{1,0:T(8,128)(2,1)S(1)}, bf16[512,256]{1,0:T(8,128)(2,1)}, s32[]{:T(128)}, s32[]{:T(128)}) while((s32[]{:T(128)}, bf16[128,256]{1,0:T(8,128)(2,1)S(1)}, bf16[512,256]{1,0:T(8,128)(2,1)}, s32[]{:T(128)}, s32[]{:T(128)}) %tuple.44), condition=%wide.region_5.0_spmd, body=%wide.region_4.0_spmd.sunk | while | flops 393218 | bytes 3539185 | solution.py:231
  113.1 19.6 %collective-permute-done.3 = bf16[128,256]{1,0:T(8,128)(2,1)S(1)} collective-permute-done((bf16[128,256]{1,0:T(8,128)(2,1)S(1)}, bf16[128,256]{1,0:T(8,128)(2,1)S(1)}, u32[]{:S(2)}, u32[]{:S(2)}) %collective-permute-start.3) | collective-permute-done | bytes 65568 | tf_op jit(solution)/shard_map/while/body/ppermute | solution.py:205
  132.7 3.4 %collective-permute-start.4 = (bf16[128,256]{1,0:T(8,128)(2,1)S(1)}, bf16[128,256]{1,0:T(8,128)(2,1)S(1)}, u32[]{:S(2)}, u32[]{:S(2)}) collective-permute-start(bf16[128,256]{1,0:T(8,128)(2,1)S(1)} %add_convert_fusion.15), channel_id=1, source_target_pairs={{0,16},{8,24},{16,0},{24,8},{32,48},{40,56},{48,32},{56,40},{64,80... | collective-permute-start | bytes 196616 | tf_op jit(solution)/shard_map/while/body/ppermute | solution.py:205
  136.1 8.1 %collective-permute-done.4 = bf16[128,256]{1,0:T(8,128)(2,1)S(1)} collective-permute-done((bf16[128,256]{1,0:T(8,128)(2,1)S(1)}, bf16[128,256]{1,0:T(8,128)(2,1)S(1)}, u32[]{:S(2)}, u32[]{:S(2)}) %collective-permute-start.4) | collective-permute-done | bytes 65568 | tf_op jit(solution)/shard_map/while/body/ppermute | solution.py:205
  146.2 5.1 %collective-permute-done.5 = bf16[128,256]{1,0:T(8,128)(2,1)S(1)} collective-permute-done((bf16[128,256]{1,0:T(8,128)(2,1)S(1)}, bf16[128,256]{1,0:T(8,128)(2,1)S(1)}, u32[]{:S(2)}, u32[]{:S(2)}) %collective-permute-start.5) | collective-permute-done | bytes 65568 | tf_op jit(solution)/shard_map/while/body/ppermute | solution.py:205
  152.1 4.1 %all-to-all-start.1 = ((bf16[4,128,256]{2,1,0:T(8,128)(2,1)}), bf16[4,128,256]{2,1,0:T(8,128)(2,1)S(1)}, u32[]{:S(2)}, u32[]{:S(2)}) async-start(bf16[4,128,256]{2,1,0:T(8,128)(2,1)} %broadcast_in_dim.11), calls=%async_computation.1 | async-start | bytes 524288 | tf_op jit(solution)/shard_map/while/body/all_to_all | solution.py:188
  156.2 5.5 %all-to-all-done.1 = bf16[4,128,256]{2,1,0:T(8,128)(2,1)S(1)} async-done(((bf16[4,128,256]{2,1,0:T(8,128)(2,1)}), bf16[4,128,256]{2,1,0:T(8,128)(2,1)S(1)}, u32[]{:S(2)}, u32[]{:S(2)}) %all-to-all-start.1) | async-done | bytes 262176 | tf_op jit(solution)/shard_map/while/body/all_to_all | solution.py:188
  164.7 11.1 %all-to-all-start.4 = ((bf16[8,192,128]{2,1,0:T(8,128)(2,1)}), bf16[8,192,128]{2,1,0:T(8,128)(2,1)S(1)}, u32[]{:S(2)}, u32[]{:S(2)}) async-start(bf16[8,192,128]{2,1,0:T(8,128)(2,1)} %late.1), calls=%async_computation.5 | async-start | bytes 786432 | tf_op jit(solution)/shard_map/all_to_all | solution.py:363
  175.8 2.9 %final.1 = (bf16[256,384]{1,0:T(8,128)(2,1)}, bf16[256,384]{1,0:T(8,128)(2,1)}) custom-call(bf16[512,384]{1,0:T(8,128)(2,1)} %get-tuple-element.93.refs_0_, bf16[512,384]{1,0:T(8,128)(2,1)} %copy-done.11, bf16[512,384]{1,0:T(8,128)(2,1)} %copy-done.12, bf16[512,384]{1,0:T(8,128)(2,1)} %copy-done.13, bf16[512,384]{1,0:T(8,128)(2,1)} %copy-done.10, ...), custom_call_target="tpu_custom_call" | custom-call | flops 100663296 | bytes 3145728 | tf_op jit(solution)/shard_map/final/pallas_call | solution.py:364
  178.7 5.2 %all-to-all-done.4.late_ref = bf16[8,192,128]{2,1,0:T(8,128)(2,1)S(1)} async-done(((bf16[8,192,128]{2,1,0:T(8,128)(2,1)}), bf16[8,192,128]{2,1,0:T(8,128)(2,1)S(1)}, u32[]{:S(2)}, u32[]{:S(2)}) %all-to-all-start.4) | async-done | bytes 393248 | tf_op jit(solution)/shard_map/all_to_all | solution.py:363
  (86 shorter events, 34.1 us)
Async XLA Ops:
  9.4 19.1 %collective-permute-start.9 = (bf16[512,384]{1,0:T(8,128)(2,1)}, bf16[512,384]{1,0:T(8,128)(2,1)S(1)}, u32[]{:S(2)}, u32[]{:S(2)}) collective-permute-start(bf16[512,384]{1,0:T(8,128)(2,1)} %get-tuple-element.78.refs_0_.both_ref), channel_id=1, source_target_pairs={{0,64},{8,72},{16,80},{24,88},{32,96},{40,104},{48,112},{56,120},{... | collective-permute-start | bytes 1179656 | tf_op jit(solution)/shard_map/ppermute | solution.py:250
  11.4 16.2 %all-to-all-start.2 = ((bf16[4,128,256]{2,1,0:T(8,128)(2,1)}), bf16[4,128,256]{2,1,0:T(8,128)(2,1)S(1)}, u32[]{:S(2)}, u32[]{:S(2)}) async-start(bf16[4,128,256]{2,1,0:T(8,128)(2,1)} %bitcast.25), calls=%async_computation.2 | async-start | bytes 524288 | tf_op jit(solution)/shard_map/all_to_all | solution.py:188
  15.2 171.1 %reduce-scatter.2.cloned.1.call-start = ((), (), s32[]{:S(2)}) async-start(), calls=%async_computation.6 | async-start | bytes 6193152 | tf_op jit(solution)/shard_map/reduce_scatter | solution.py:340
  15.2 65.0 %collective-permute-start.10 = (bf16[512,384]{1,0:T(8,128)(2,1)}, bf16[512,384]{1,0:T(8,128)(2,1)S(1)}, u32[]{:S(2)}, u32[]{:S(2)}) collective-permute-start(bf16[512,384]{1,0:T(8,128)(2,1)} %get-tuple-element.78.refs_0_.both_ref), channel_id=1, source_target_pairs={{0,128},{8,136},{16,144},{24,152},{32,160},{40,168},{48,176},{56,1... | collective-permute-start | bytes 1179656 | tf_op jit(solution)/shard_map/ppermute | solution.py:250
  18.1 62.0 %collective-permute-start.8 = (bf16[512,384]{1,0:T(8,128)(2,1)}, bf16[512,384]{1,0:T(8,128)(2,1)S(1)}, u32[]{:S(2)}, u32[]{:S(2)}) collective-permute-start(bf16[512,384]{1,0:T(8,128)(2,1)} %get-tuple-element.78.refs_0_.both_ref), channel_id=1, source_target_pairs={{0,32},{8,40},{16,48},{24,56},{32,0},{40,8},{48,16},{56,24},{64,96... | collective-permute-start | bytes 1179656 | tf_op jit(solution)/shard_map/ppermute | solution.py:250
  25.0 55.1 %collective-permute-start.7 = (bf16[512,384]{1,0:T(8,128)(2,1)}, bf16[512,384]{1,0:T(8,128)(2,1)S(1)}, u32[]{:S(2)}, u32[]{:S(2)}) collective-permute-start(bf16[512,384]{1,0:T(8,128)(2,1)} %get-tuple-element.78.refs_0_.both_ref), channel_id=1, source_target_pairs={{0,16},{8,24},{16,0},{24,8},{32,48},{40,56},{48,32},{56,40},{64,80... | collective-permute-start | bytes 1179656 | tf_op jit(solution)/shard_map/ppermute | solution.py:250
  27.7 52.5 %collective-permute-start.6 = (bf16[512,384]{1,0:T(8,128)(2,1)}, bf16[512,384]{1,0:T(8,128)(2,1)S(1)}, u32[]{:S(2)}, u32[]{:S(2)}) collective-permute-start(bf16[512,384]{1,0:T(8,128)(2,1)} %get-tuple-element.78.refs_0_.both_ref), channel_id=1, source_target_pairs={{0,8},{8,0},{16,24},{24,16},{32,40},{40,32},{48,56},{56,48},{64,72... | collective-permute-start | bytes 1179656 | tf_op jit(solution)/shard_map/ppermute | solution.py:250
  29.4 28.6 %collective-permute-start = (bf16[128,256]{1,0:T(8,128)(2,1)S(1)}, bf16[128,256]{1,0:T(8,128)(2,1)S(1)}, u32[]{:S(2)}, u32[]{:S(2)}) collective-permute-start(bf16[128,256]{1,0:T(8,128)(2,1)S(1)} %get-tuple-element.176), channel_id=1, source_target_pairs={{0,8},{8,0},{16,24},{24,16},{32,40},{40,32},{48,56},{56,48},{64,72... | collective-permute-start | bytes 196616 | tf_op jit(solution)/shard_map/while/body/ppermute | solution.py:205
  58.0 4.6 %collective-permute-start.1 = (bf16[128,256]{1,0:T(8,128)(2,1)S(1)}, bf16[128,256]{1,0:T(8,128)(2,1)S(1)}, u32[]{:S(2)}, u32[]{:S(2)}) collective-permute-start(bf16[128,256]{1,0:T(8,128)(2,1)S(1)} %add_convert_fusion.12), channel_id=1, source_target_pairs={{0,16},{8,24},{16,0},{24,8},{32,48},{40,56},{48,32},{56,40},{64,80... | collective-permute-start | bytes 196616 | tf_op jit(solution)/shard_map/while/body/ppermute | solution.py:205
  62.6 7.2 %collective-permute-start.2 = (bf16[128,256]{1,0:T(8,128)(2,1)S(1)}, bf16[128,256]{1,0:T(8,128)(2,1)S(1)}, u32[]{:S(2)}, u32[]{:S(2)}) collective-permute-start(bf16[128,256]{1,0:T(8,128)(2,1)S(1)} %add_convert_fusion.13), channel_id=1, source_target_pairs={{0,32},{8,40},{16,48},{24,56},{32,0},{40,8},{48,16},{56,24},{64,96... | collective-permute-start | bytes 196616 | tf_op jit(solution)/shard_map/while/body/ppermute | solution.py:205
  70.5 8.9 %all-to-all-start = ((bf16[4,128,256]{2,1,0:T(8,128)(2,1)}), bf16[4,128,256]{2,1,0:T(8,128)(2,1)S(1)}, u32[]{:S(2)}, u32[]{:S(2)}) async-start(bf16[4,128,256]{2,1,0:T(8,128)(2,1)} %broadcast_in_dim.10), calls=%async_computation | async-start | bytes 524288 | tf_op jit(solution)/shard_map/while/body/all_to_all | solution.py:188
  98.5 12.2 %collective-permute-start.11 = (bf16[512,384]{1,0:T(8,128)(2,1)}, bf16[512,384]{1,0:T(8,128)(2,1)S(1)}, u32[]{:S(2)}, u32[]{:S(2)}) collective-permute-start(bf16[512,384]{1,0:T(8,128)(2,1)} %get-tuple-element.84), channel_id=1, source_target_pairs={{0,64},{8,72},{16,80},{24,88},{32,96},{40,104},{48,112},{56,120},{... | collective-permute-start | bytes 1179656 | tf_op jit(solution)/shard_map/ppermute | solution.py:250
  98.9 8.9 %all-to-all-start.3 = ((bf16[4,128,256]{2,1,0:T(8,128)(2,1)}), bf16[4,128,256]{2,1,0:T(8,128)(2,1)S(1)}, u32[]{:S(2)}, u32[]{:S(2)}) async-start(bf16[4,128,256]{2,1,0:T(8,128)(2,1)} %bitcast.3), calls=%async_computation.3 | async-start | bytes 524288 | tf_op jit(solution)/shard_map/all_to_all | solution.py:188
  102.3 62.3 %collective-permute-start.12 = (bf16[512,384]{1,0:T(8,128)(2,1)}, bf16[512,384]{1,0:T(8,128)(2,1)S(1)}, u32[]{:S(2)}, u32[]{:S(2)}) collective-permute-start(bf16[512,384]{1,0:T(8,128)(2,1)} %get-tuple-element.88), channel_id=1, source_target_pairs={{0,8},{8,0},{16,24},{24,16},{32,40},{40,32},{48,56},{56,48},{64,72... | collective-permute-start | bytes 1179656 | tf_op jit(solution)/shard_map/ppermute | solution.py:250
  104.7 59.9 %collective-permute-start.13 = (bf16[512,384]{1,0:T(8,128)(2,1)S(1)}, bf16[512,384]{1,0:T(8,128)(2,1)S(1)}, u32[]{:S(2)}, u32[]{:S(2)}) collective-permute-start(bf16[512,384]{1,0:T(8,128)(2,1)S(1)} %copy-done.17), channel_id=1, source_target_pairs={{0,16},{8,24},{16,0},{24,8},{32,48},{40,56},{48,32},{56,40},{64,80... | collective-permute-start | bytes 1179656 | tf_op jit(solution)/shard_map/ppermute | solution.py:250
  107.1 57.6 %collective-permute-start.14 = (bf16[512,384]{1,0:T(8,128)(2,1)S(1)}, bf16[512,384]{1,0:T(8,128)(2,1)S(1)}, u32[]{:S(2)}, u32[]{:S(2)}) collective-permute-start(bf16[512,384]{1,0:T(8,128)(2,1)S(1)} %copy-done.16), channel_id=1, source_target_pairs={{0,32},{8,40},{16,48},{24,56},{32,0},{40,8},{48,16},{56,24},{64,96... | collective-permute-start | bytes 1179656 | tf_op jit(solution)/shard_map/ppermute | solution.py:250
  107.9 56.8 %collective-permute-start.15 = (bf16[512,384]{1,0:T(8,128)(2,1)S(1)}, bf16[512,384]{1,0:T(8,128)(2,1)S(1)}, u32[]{:S(2)}, u32[]{:S(2)}) collective-permute-start(bf16[512,384]{1,0:T(8,128)(2,1)S(1)} %copy-done.15), channel_id=1, source_target_pairs={{0,128},{8,136},{16,144},{24,152},{32,160},{40,168},{48,176},{56,1... | collective-permute-start | bytes 1179656 | tf_op jit(solution)/shard_map/ppermute | solution.py:250
  111.6 21.0 %collective-permute-start.3 = (bf16[128,256]{1,0:T(8,128)(2,1)S(1)}, bf16[128,256]{1,0:T(8,128)(2,1)S(1)}, u32[]{:S(2)}, u32[]{:S(2)}) collective-permute-start(bf16[128,256]{1,0:T(8,128)(2,1)S(1)} %get-tuple-element.191), channel_id=1, source_target_pairs={{0,8},{8,0},{16,24},{24,16},{32,40},{40,32},{48,56},{56,48},{64,72... | collective-permute-start | bytes 196616 | tf_op jit(solution)/shard_map/while/body/ppermute | solution.py:205
  132.7 11.5 %collective-permute-start.4 = (bf16[128,256]{1,0:T(8,128)(2,1)S(1)}, bf16[128,256]{1,0:T(8,128)(2,1)S(1)}, u32[]{:S(2)}, u32[]{:S(2)}) collective-permute-start(bf16[128,256]{1,0:T(8,128)(2,1)S(1)} %add_convert_fusion.15), channel_id=1, source_target_pairs={{0,16},{8,24},{16,0},{24,8},{32,48},{40,56},{48,32},{56,40},{64,80... | collective-permute-start | bytes 196616 | tf_op jit(solution)/shard_map/while/body/ppermute | solution.py:205
  144.3 7.1 %collective-permute-start.5 = (bf16[128,256]{1,0:T(8,128)(2,1)S(1)}, bf16[128,256]{1,0:T(8,128)(2,1)S(1)}, u32[]{:S(2)}, u32[]{:S(2)}) collective-permute-start(bf16[128,256]{1,0:T(8,128)(2,1)S(1)} %add_convert_fusion.16), channel_id=1, source_target_pairs={{0,32},{8,40},{16,48},{24,56},{32,0},{40,8},{48,16},{56,24},{64,96... | collective-permute-start | bytes 196616 | tf_op jit(solution)/shard_map/while/body/ppermute | solution.py:205
  152.1 9.6 %all-to-all-start.1 = ((bf16[4,128,256]{2,1,0:T(8,128)(2,1)}), bf16[4,128,256]{2,1,0:T(8,128)(2,1)S(1)}, u32[]{:S(2)}, u32[]{:S(2)}) async-start(bf16[4,128,256]{2,1,0:T(8,128)(2,1)} %broadcast_in_dim.11), calls=%async_computation.1 | async-start | bytes 524288 | tf_op jit(solution)/shard_map/while/body/all_to_all | solution.py:188
  164.6 11.1 %copy-start.11 = (bf16[512,384]{1,0:T(8,128)(2,1)}, bf16[512,384]{1,0:T(8,128)(2,1)S(1)}, u32[]{:S(2)}) copy-start(bf16[512,384]{1,0:T(8,128)(2,1)S(1)} %collective-permute-done.12.refs_1_) | copy-start | bytes 1179652
  164.6 11.1 %copy-start.12 = (bf16[512,384]{1,0:T(8,128)(2,1)}, bf16[512,384]{1,0:T(8,128)(2,1)S(1)}, u32[]{:S(2)}) copy-start(bf16[512,384]{1,0:T(8,128)(2,1)S(1)} %collective-permute-done.13.refs_2_) | copy-start | bytes 1179652
  164.7 19.1 %all-to-all-start.4 = ((bf16[8,192,128]{2,1,0:T(8,128)(2,1)}), bf16[8,192,128]{2,1,0:T(8,128)(2,1)S(1)}, u32[]{:S(2)}, u32[]{:S(2)}) async-start(bf16[8,192,128]{2,1,0:T(8,128)(2,1)} %late.1), calls=%async_computation.5 | async-start | bytes 786432 | tf_op jit(solution)/shard_map/all_to_all | solution.py:363
  (16 other events, 67.1 us)
Sparse Core Ops, SparseCore 0:
  98.7 44.8 reduce-scatter.1

commit v4 on v3

--- a/solution.py
+++ b/solution.py
@@ -49,7 +49,8 @@
     low_ref[rows:] = dot_nt(cot, down_right_ref[...]).astype(BF)
 
 
-def chosen(ref, index_ref, level, block, first_row, rows, sub):
+def chosen(field, index_ref, level, block, rows, sub):
+    ref, first_row = field
     pieces = []
     for j in range(2):
         column = pl.multiple_of(index_ref[level, block, j] * sub, sub)
@@ -57,15 +58,29 @@
     return jnp.concatenate(pieces, axis=1)
 
 
-def middle_kernel(levels, index_ref, *refs):
-    fields = refs[:levels]
-    low_ref, up_ref, down_ref, up_right_ref, down_left_ref = refs[levels : levels + 5]
-    act_ref, grad_ref, lowp_ref = refs[levels + 5 : levels + 8]
-    parts = refs[levels + 8 : 2 * levels + 8]
-    out_acc, in_acc, low_acc = refs[2 * levels + 8 :]
+def spread(refs, rows):
+    halves = []
+    at = 0
+    while at < len(refs):
+        if refs[at].shape[0] == rows:
+            halves.append(((refs[at], 0), (refs[at + 1], 0)))
+            at += 2
+        else:
+            halves.append(((refs[at], 0), (refs[at], rows)))
+            at += 1
+    return halves
+
+
+def middle_kernel(levels, fields_count, index_ref, *refs):
+    rows = refs[0].shape[0]
+    fields = spread(refs[:fields_count], rows)
+    refs = refs[fields_count:]
+    low_ref, up_ref, down_ref, up_right_ref, down_left_ref = refs[:5]
+    act_ref, grad_ref, lowp_ref = refs[5:8]
+    parts = spread(refs[8 : 8 + fields_count - 1], rows)
+    out_acc, in_acc, low_acc = refs[8 + fields_count - 1 :]
     block = pl.program_id(0)
-    rows = low_ref.shape[0] // 2
-    sub = fields[0].shape[1] // 3
+    sub = refs[8].shape[1] // 3
 
     @pl.when(block == 0)
     def _():
@@ -76,8 +91,8 @@
     pre_act = dot(low_ref[:rows], up_right_ref[...])
     grad_hidden = dot_nt(low_ref[rows:], down_left_ref[...])
     for k in range(levels):
-        pre_act += dot(chosen(fields[k], index_ref, k, block, 0, rows, sub), up_ref[k])
-        grad_hidden += dot_nt(chosen(fields[k], index_ref, k, block, rows, rows, sub), down_ref[k])
+        pre_act += dot(chosen(fields[k][0], index_ref, k, block, rows, sub), up_ref[k])
+        grad_hidden += dot_nt(chosen(fields[k][1], index_ref, k, block, rows, sub), down_ref[k])
     value, slope = gelu_parts(pre_act)
     act = value.astype(BF)
     grad = (grad_hidden * slope).astype(BF)
@@ -97,18 +112,18 @@
     def _():
         lowp_ref[...] = low_acc[...].astype(BF)
         for k in range(levels):
-            for c in range(3):
-                cols = slice(c * sub, (c + 1) * sub)
-                parts[k][:rows, cols] = out_acc[3 * k + c].astype(BF)
-                parts[k][rows:, cols] = in_acc[3 * k + c].astype(BF)
-
-
-def grads_kernel(levels, groups, index_ref, *refs):
-    fields = refs[:levels]
-    low_ref, act_ref, grad_ref, out_ref = refs[levels:]
+            for half, acc in zip(parts[k], (out_acc, in_acc)):
+                ref, first = half
+                for c in range(3):
+                    ref[first : first + rows, c * sub : (c + 1) * sub] = acc[3 * k + c].astype(BF)
+
+
+def grads_kernel(levels, groups, fields_count, index_ref, *refs):
+    rows = refs[0].shape[0]
+    fields = spread(refs[:fields_count], rows)
+    low_ref, act_ref, grad_ref, out_ref = refs[fields_count:]
     block = pl.program_id(0)
-    rows = low_ref.shape[0] // 2
-    sub = fields[0].shape[1] // 3
+    sub = refs[0].shape[1] // 3
     width = act_ref.shape[1]
     piece = width // groups
     per = 3 * piece
@@ -117,8 +132,8 @@
     grad = grad_ref[...]
     for k in range(levels + 1):
         if k < levels:
-            field = chosen(fields[k], index_ref, k, block, 0, rows, sub)
-            grad_field = chosen(fields[k], index_ref, k, block, rows, rows, sub)
+            field = chosen(fields[k][0], index_ref, k, block, rows, sub)
+            grad_field = chosen(fields[k][1], index_ref, k, block, rows, sub)
         else:
             field = low_ref[:rows]
             grad_field = low_ref[rows:]
@@ -131,6 +146,24 @@
             out_ref[group, pl.ds(row, piece), :] = down[m * piece : (m + 1) * piece]
             row = pl.multiple_of(up_base + (block * (levels + 1) + k) * piece, piece)
             out_ref[m, pl.ds(row, piece), :] = up[m * piece : (m + 1) * piece]
+
+
+def unpack_kernel(levels, sum_ref, down_ref, left_ref, up_ref, right_ref):
+    per, width = left_ref.shape
+    piece = right_ref.shape[0]
+    for k in range(levels + 1):
+        rows = sum_ref[k * per : (k + 1) * per]
+        if k < levels:
+            down_ref[k] = rows
+        else:
+            left_ref[...] = rows
+        for block in range(right_ref.shape[1] // width):
+            first = (levels + 1) * per + (block * (levels + 1) + k) * piece
+            rows = sum_ref[first : first + piece]
+            if k < levels:
+                up_ref[k, :, block * width : (block + 1) * width] = rows
+            else:
+                right_ref[:, block * width : (block + 1) * width] = rows
 
 
 def late_kernel(groups, both_ref, low_ref, out_ref):
@@ -149,18 +182,19 @@
             ]
 
 
-def final_kernel(levels, *refs):
-    parts = refs[:levels]
-    low_ref, down_right_ref, up_left_ref = refs[levels : levels + 3]
-    layer_ref, tokens_ref = refs[levels + 3 :]
-    rows = low_ref.shape[0] // 2
-    out = parts[0][:rows].astype(F32)
-    back = parts[0][rows:].astype(F32)
-    for k in range(1, levels):
-        out += parts[k][:rows].astype(F32)
-        back += parts[k][rows:].astype(F32)
-    layer_ref[...] = (out + dot(low_ref[:rows], down_right_ref[...])).astype(BF)
-    tokens_ref[...] = (back + dot_nt(low_ref[rows:], up_left_ref[...])).astype(BF)
+def final_kernel(count, *refs):
+    rows = refs[count].shape[0] // 2
+    halves = spread(refs[:count], rows)
+    low_ref, down_right_ref, up_left_ref, layer_ref, tokens_ref = refs[count:]
+    for side, weight, out_ref in ((0, down_right_ref, layer_ref), (1, up_left_ref, tokens_ref)):
+        total = None
+        for half in halves:
+            ref, first = half[side]
+            value = ref[first : first + rows].astype(F32)
+            total = value if total is None else total + value
+        low = low_ref[side * rows : (side + 1) * rows]
+        product = dot(low, weight[...]) if side == 0 else dot_nt(low, weight[...])
+        out_ref[...] = (total + product).astype(BF)
 
 
 def last_kernel(late_ref, right_ref, left_ref):
@@ -215,20 +249,17 @@
     return [list(range(i, lax.axis_size("hid"), inner)) for i in range(inner)]
 
 
-def finish_sum(held, distance):
+def line_sum(held):
     trips = 1 + lax.shift_right_logical(lax.axis_index("hid"), 20)
-    outer = len(hid_columns()[0])
-
-    def once(_, carried):
-        value = carried[0]
-        step = distance
+
+    def once(_, value):
+        step = 1
         while step < hid_inner():
             value = line_step(value, step)
             step *= 2
-        return value, group_gather(value, hid_columns())
-
-    wide = jnp.zeros((outer * held.shape[0], held.shape[1]), held.dtype)
-    return lax.fori_loop(0, trips, once, (held, wide))[1]
+        return value
+
+    return lax.fori_loop(0, trips, once, held)
 
 
 def on_device(
@@ -245,10 +276,12 @@
     sub = feat // 3
     sds = jax.ShapeDtypeStruct
 
-    def partner(value, level):
-        distance = 1 << (level - 1)
+    def swap(value, distance):
         return lax.ppermute(value, "hid", [(i, i ^ distance) for i in range(hid_count)])
 
+    tie = lax.optimization_barrier
+    columns = hid_columns()
+    tok_two = swap(tokens, 2)
     both, low_part = pl.pallas_call(
         head_kernel,
         out_shape=(sds((2 * rows, feat), BF), sds((2 * rows, rank), BF)),
@@ -258,13 +291,20 @@
         cost_estimate=cost(4 * rows * feat * rank, 4 * rows * feat * 2),
         name="head",
     )(tokens, cotangent, up_left, down_right)
-    order = [3, 2, 1, 5, 4]
-    fields = [both] + [None] * (levels - 1)
-    for level in order:
-        fields[level] = partner(both, level)
-    total = group_scatter(low_part, hid_columns())
-    total, fields[4] = lax.optimization_barrier((total, fields[4]))
-    low = finish_sum(total, 1)
+    total, both_x = tie((group_scatter(low_part, columns), both))
+    x_one = swap(both_x, 8)
+    x_two = swap(both_x, 16)
+    total, x_one, x_two, tok_two, both_z, cot_z = tie(
+        (line_sum(total), x_one, x_two, tok_two, both, cotangent)
+    )
+    tok_four = swap(tok_two, 6)
+    cot_two = swap(cot_z, 2)
+    z_one = swap(both_z, 1)
+    low = group_gather(total, columns)
+    cot_four = swap(cot_two, 6)
+    fields = [tokens, cotangent, z_one, tok_two, cot_two, tok_four, cot_four, x_one, x_two]
+    part_shapes = [(2 * rows, feat), (2 * rows, feat)]
+    part_shapes += [(rows, feat)] * 4 + [(2 * rows, feat)] * 2
 
     def whole(shape):
         return pl.BlockSpec(shape, lambda b, *_: (0,) * len(shape))
@@ -274,11 +314,11 @@
     )
     flops = 2 * rows * (levels + 1) * 2 * sub * hidden
     middle = pl.pallas_call(
-        functools.partial(middle_kernel, levels),
+        functools.partial(middle_kernel, levels, len(fields)),
         grid_spec=pltpu.PrefetchScalarGridSpec(
             num_scalar_prefetch=1,
             grid=(blocks,),
-            in_specs=[whole((2 * rows, feat))] * levels
+            in_specs=[whole(field.shape) for field in fields]
             + [
                 whole((2 * rows, rank)),
                 pl.BlockSpec((levels, 2 * sub, width), lambda b, *_: (0, 0, b)),
@@ -291,7 +331,7 @@
                 pl.BlockSpec((rows, width), lambda b, *_: (0, b)),
                 whole((2 * rows, rank)),
             ]
-            + [whole((2 * rows, feat))] * levels,
+            + [whole(shape) for shape in part_shapes],
             scratch_shapes=[
                 pltpu.VMEM((3 * levels, rows, sub), F32),
                 pltpu.VMEM((3 * levels, rows, sub), F32),
@@ -303,7 +343,7 @@
             sds((rows, hidden), BF),
             sds((2 * rows, rank), BF),
         ]
-        + [sds((2 * rows, feat), BF)] * levels,
+        + [sds(shape, BF) for shape in part_shapes],
         compiler_params=grid_params,
         cost_estimate=cost(4 * flops, 10 * 1024 * 1024),
         name="middle",
@@ -314,11 +354,11 @@
     piece = width // groups
     chunk = 2 * (levels + 1) * 3 * piece
     packed = pl.pallas_call(
-        functools.partial(grads_kernel, levels, groups),
+        functools.partial(grads_kernel, levels, groups, len(fields)),
         grid_spec=pltpu.PrefetchScalarGridSpec(
             num_scalar_prefetch=1,
             grid=(blocks,),
-            in_specs=[whole((2 * rows, feat))] * levels
+            in_specs=[whole(field.shape) for field in fields]
             + [
                 whole((2 * rows, rank)),
                 pl.BlockSpec((rows, width), lambda b, *_: (0, b)),
@@ -332,22 +372,41 @@
         name="grads",
     )(block_index, *fields, low, act, grad_pre)
 
-    for level in order:
-        parts[level] = partner(parts[level], level)
-    total = group_scatter(lowp, hid_columns())
-    total, parts[4] = lax.optimization_barrier((total, parts[4]))
-    low2 = finish_sum(total, 1)
+    own, one, out_two, in_two, out_four, in_four, x_one, x_two = parts
+    out_four = swap(out_four, 6)
+    total, x_one, x_two = tie((group_scatter(lowp, columns), x_one, x_two))
+    x_one = swap(x_one, 8)
+    x_two = swap(x_two, 16)
+    total, x_one, x_two, out_four, in_four, one = tie(
+        (line_sum(total), x_one, x_two, out_four, in_four, one)
+    )
+
+    def joined(first, second):
+        return (first.astype(F32) + second.astype(F32)).astype(BF)
+
+    in_four = swap(in_four, 6)
+    out_two = swap(joined(out_two, out_four), 2)
+    one = swap(one, 1)
+    low2 = group_gather(total, columns)
+    in_two = swap(joined(in_two, in_four), 2)
+    parts = [own, one, out_two, in_two, x_one, x_two]
     summed = lax.psum_scatter(
         packed.reshape(groups * chunk, width), "tok", scatter_dimension=0, tiled=True
     )
-    half = (levels + 1) * 3 * piece
-    down_sum = summed[:half].reshape(levels + 1, 3 * piece, width)
-    up_sum = summed[half:].reshape(blocks, levels + 1, piece, width)
-    grad_down_tiles = down_sum[:levels]
-    grad_down_left = down_sum[levels]
-    up_sum = up_sum.transpose(1, 2, 0, 3).reshape(levels + 1, piece, hidden)
-    grad_up_tiles = up_sum[:levels]
-    grad_up_right = up_sum[levels]
+    grad_down_tiles, grad_down_left, grad_up_tiles, grad_up_right = pl.pallas_call(
+        functools.partial(unpack_kernel, levels),
+        out_shape=(
+            sds((levels, hidden // groups, 2 * sub), BF),
+            sds((hidden // groups, rank), BF),
+            sds((levels, 2 * sub // groups, hidden), BF),
+            sds((rank // groups, hidden), BF),
+        ),
+        in_specs=[vmem_spec()],
+        out_specs=(vmem_spec(),) * 4,
+        compiler_params=params(),
+        cost_estimate=cost(0, 4 * chunk * width),
+        name="unpack",
+    )(summed)
 
     late_rows = (rank // groups) * (feat // 128) + (feat // groups) * (rank // 128)
     late = pl.pallas_call(
@@ -359,12 +418,11 @@
         cost_estimate=cost(4 * rows * feat * rank, 4 * rows * feat * 2),
         name="late",
     )(both, low2)
-    late, parts = lax.optimization_barrier((late, parts))
     late = lax.all_to_all(late, "tok", 0, 0, tiled=True)
     layer_out, grad_tokens = pl.pallas_call(
-        functools.partial(final_kernel, levels),
+        functools.partial(final_kernel, len(parts)),
         out_shape=(sds((rows, feat), BF), sds((rows, feat), BF)),
-        in_specs=[vmem_spec()] * (levels + 3),
+        in_specs=[vmem_spec()] * (len(parts) + 3),
         out_specs=(vmem_spec(),) * 2,
         compiler_params=params(),
         cost_estimate=cost(4 * rows * feat * rank, 16 * rows * feat * 2),

time: 199 us -> 171 us (0.86)
  waiting for transfers between devices: 84.1 us -> 55.5 us
  local copies, waits for them, and re-layouts: 12.4 us -> 5.26 us
  starting transfers between devices: 60.6 us -> 66.7 us
    ppermute x6, waiting for transfers between devices: 67.8 us -> 22.5 us  [line_step(): other = lax.ppermute(held, 'hid', [(i, i ^ distance) for i in range(count)])]
    ppermute x10 -> x14, waiting for transfers between devices: 0.03 us -> 21.3 us  [swap(): lax.ppermute(value, 'hid', [(i, i ^ distance) for i in range(hid_count)])]
    all_to_all x4, starting transfers between devices: 14.6 us -> 20.9 us  [group_exchange(): lax.all_to_all(pieces, 'hid', 0, 0, axis_index_groups=groups, tiled=True)]
    all_to_all x1, waiting for transfers between devices: 5.18 us -> 0.01 us  [on_device(): late = lax.all_to_all(late, 'tok', 0, 0, tiled=True)]
    ppermute x10 -> x14, starting transfers between devices: 22.5 us -> 17.5 us  [swap(): lax.ppermute(value, 'hid', [(i, i ^ distance) for i in range(hid_count)])]
    all_to_all x1, starting transfers between devices: 11.1 us -> 15.9 us  [on_device(): late = lax.all_to_all(late, 'tok', 0, 0, tiled=True)]
    slice x6 -> x0, local copies, waits for them, and re-layouts: 3.64 us -> none  [the longest x2 1.19 us: on_device(): grad_up_tiles = up_sum[:levels]]
    pallas_call x3 -> x4, Pallas kernels: 20 us -> 21.9 us  [the longest x1 9.6 us: on_device(): pl.pallas_call(functools.partial(middle_kernel, levels, len(fields)), gri...]
  transfers between devices with their start and end apart: 22 -> 26, of which waited for: 10 -> 12; matrix products, arithmetic and copies ran while one was open for 2% -> 1% of each run, Pallas kernels for 3% -> 4%
where the time goes in v4:
time: 171 us; the launch traced here: 170 us
  starting transfers between devices  66.7 us (39%)
  waiting for transfers between devices  55.5 us (32%)
  Pallas kernels  27.9 us (16%)
  between operations  14.3 us (8%)
  local copies, waits for them, and re-layouts  5.26 us (3%)
    ppermute x6, waiting for transfers between devices, line_step(): other = lax.ppermute(held, 'hid', [(i, i ^ distance) for i in range(count)])  22.5 us
    ppermute x14, waiting for transfers between devices, swap(): lax.ppermute(value, 'hid', [(i, i ^ distance) for i in range(hid_count)])  21.3 us
    all_to_all x4, starting transfers between devices, group_exchange(): lax.all_to_all(pieces, 'hid', 0, 0, axis_index_groups=groups, tiled=True)  20.9 us
    ppermute x14, starting transfers between devices, swap(): lax.ppermute(value, 'hid', [(i, i ^ distance) for i in range(hid_count)])  17.5 us
    all_to_all x1, starting transfers between devices, on_device(): late = lax.all_to_all(late, 'tok', 0, 0, tiled=True)  15.9 us
    ppermute x6, starting transfers between devices, line_step(): other = lax.ppermute(held, 'hid', [(i, i ^ distance) for i in range(count)])  12.4 us
    all_to_all x4, waiting for transfers between devices, group_exchange(): lax.all_to_all(pieces, 'hid', 0, 0, axis_index_groups=groups, tiled=True)  11.7 us
    pallas_call x1, Pallas kernels, on_device(): pl.pallas_call(functools.partial(middle_kernel, levels, len(fields)), gri...  9.6 us
  transfers between devices with their start and end apart: 26, of which 12 were waited for; matrix products, arithmetic and copies ran while one was open for 1% of the time, Pallas kernels for 4%

profile of v4, /device:TPU:1, one launch (start us, length us, event | category | flops | bytes accessed | tf_op | source)
XLA Modules:
  0.0 170.0 jit_solution(17844208155512103618)
XLA Ops:
  9.4 5.0 %all-to-all-start = ((bf16[4,128,256]{2,1,0:T(8,128)(2,1)}), bf16[4,128,256]{2,1,0:T(8,128)(2,1)S(1)}, u32[]{:S(2)}, u32[]{:S(2)}) async-start(bf16[4,128,256]{2,1,0:T(8,128)(2,1)} %bitcast.10), calls=%async_computation | async-start | bytes 524288 | tf_op jit(solution)/shard_map/all_to_all | solution.py:222
  14.4 3.0 %collective-permute-start.8 = (bf16[256,384]{1,0:T(8,128)(2,1)}, bf16[256,384]{1,0:T(8,128)(2,1)S(1)}, u32[]{:S(2)}, u32[]{:S(2)}) collective-permute-start(bf16[256,384]{1,0:T(8,128)(2,1)} %refs_0_.3), channel_id=1, source_target_pairs={{0,16},{8,24},{16,0},{24,8},{32,48},{40,56},{48,32},{56,40},{64,80... | collective-permute-start | bytes 589832 | tf_op jit(solution)/shard_map/ppermute | solution.py:280
  21.6 18.9 %while.20 = (s32[]{:T(128)}, bf16[128,256]{1,0:T(8,128)(2,1)S(1)}, s32[]{:T(128)}, s32[]{:T(128)}) while((s32[]{:T(128)}, bf16[128,256]{1,0:T(8,128)(2,1)S(1)}, s32[]{:T(128)}, s32[]{:T(128)}) %tuple.43), condition=%wide.region_2.0_spmd, body=%wide.region_1.0_spmd.sunk | while | flops 393218 | bytes 1376429 | solution.py:262
  23.2 4.4 %collective-permute-done = bf16[128,256]{1,0:T(8,128)(2,1)S(1)} collective-permute-done((bf16[128,256]{1,0:T(8,128)(2,1)S(1)}, bf16[128,256]{1,0:T(8,128)(2,1)S(1)}, u32[]{:S(2)}, u32[]{:S(2)}) %collective-permute-start) | collective-permute-done | bytes 65568 | tf_op jit(solution)/shard_map/while/body/ppermute | solution.py:239
  29.4 2.6 %collective-permute-done.1 = bf16[128,256]{1,0:T(8,128)(2,1)S(1)} collective-permute-done((bf16[128,256]{1,0:T(8,128)(2,1)S(1)}, bf16[128,256]{1,0:T(8,128)(2,1)S(1)}, u32[]{:S(2)}, u32[]{:S(2)}) %collective-permute-start.1) | collective-permute-done | bytes 65568 | tf_op jit(solution)/shard_map/while/body/ppermute | solution.py:239
  32.0 6.8 %collective-permute-start.2 = (bf16[128,256]{1,0:T(8,128)(2,1)S(1)}, bf16[128,256]{1,0:T(8,128)(2,1)S(1)}, u32[]{:S(2)}, u32[]{:S(2)}) collective-permute-start(bf16[128,256]{1,0:T(8,128)(2,1)S(1)} %add_convert_fusion.15), channel_id=1, source_target_pairs={{0,32},{8,40},{16,48},{24,56},{32,0},{40,8},{48,16},{56,24},{64,96... | collective-permute-start | bytes 196616 | tf_op jit(solution)/shard_map/while/body/ppermute | solution.py:239
  43.0 3.3 %collective-permute-start.11 = (bf16[256,384]{1,0:T(8,128)(2,1)S(1)}, bf16[256,384]{1,0:T(8,128)(2,1)S(1)}, u32[]{:S(2)}, u32[]{:S(2)}) collective-permute-start(bf16[256,384]{1,0:T(8,128)(2,1)S(1)} %collective-permute-done.8.refs_3_), channel_id=1, source_target_pairs={{0,48},{8,56},{16,32},{24,40},{32,16},{40,24},{48,0},{56,8},{64,11... | collective-permute-start | bytes 589832 | tf_op jit(solution)/shard_map/ppermute | solution.py:280
  47.0 5.6 %all-to-all-start.1 = ((bf16[4,128,256]{2,1,0:T(8,128)(2,1)}), bf16[4,128,256]{2,1,0:T(8,128)(2,1)S(1)}, u32[]{:S(2)}, u32[]{:S(2)}) async-start(bf16[4,128,256]{2,1,0:T(8,128)(2,1)} %broadcast_in_dim.4), calls=%async_computation.1 | async-start | bytes 524288 | tf_op jit(solution)/shard_map/all_to_all | solution.py:222
  53.7 7.4 %collective-permute-done.11.refs_5_ = bf16[256,384]{1,0:T(8,128)(2,1)S(1)} collective-permute-done((bf16[256,384]{1,0:T(8,128)(2,1)S(1)}, bf16[256,384]{1,0:T(8,128)(2,1)S(1)}, u32[]{:S(2)}, u32[]{:S(2)}) %collective-permute-start.11) | collective-permute-done | bytes 196640 | tf_op jit(solution)/shard_map/ppermute | solution.py:280
  61.1 4.5 %collective-permute-done.12.refs_6_ = bf16[256,384]{1,0:T(8,128)(2,1)S(1)} collective-permute-done((bf16[256,384]{1,0:T(8,128)(2,1)S(1)}, bf16[256,384]{1,0:T(8,128)(2,1)S(1)}, u32[]{:S(2)}, u32[]{:S(2)}) %collective-permute-start.12) | collective-permute-done | bytes 196640 | tf_op jit(solution)/shard_map/ppermute | solution.py:280
  66.5 9.6 %middle.1 = (bf16[256,768]{1,0:T(8,128)(2,1)}, bf16[256,768]{1,0:T(8,128)(2,1)}, bf16[512,256]{1,0:T(8,128)(2,1)}, bf16[512,384]{1,0:T(8,128)(2,1)}, bf16[512,38...) custom-call(s32[6,3,2]{2,1,0:T(4,128)} %copy.17.index_ref, ...), custom_call_target="tpu_custom_call" | custom-call | flops 2818572288 | bytes 10485760 | tf_op jit(solution)/shard_map/middle/pallas_call | solution.py:316
  76.1 7.6 %grads.1 = bf16[8,1344,256]{2,1,0:T(8,128)(2,1)} custom-call(s32[6,3,2]{2,1,0:T(4,128)} %copy.17.index_ref, bf16[256,384]{1,0:T(8,128)(2,1)} %refs_0_.3, bf16[256,384]{1,0:T(8,128)(2,1)} %refs_1_.3, bf16[512,384]{1,0:T(8,128)(2,1)} %copy-done.6, bf16[256,384]{1,0:T(8,128)(2,1)} %copy-done.15, bf16[256,384]{1,0:T(8,128)(2,1)} %copy-done.16, ...), custom_call_target="tpu_custom_call" | custom-call | flops 1409286144 | bytes 10485760 | tf_op jit(solution)/shard_map/grads/pallas_call | solution.py:356
  83.7 6.6 %all-to-all-start.2 = ((bf16[4,128,256]{2,1,0:T(8,128)(2,1)}), bf16[4,128,256]{2,1,0:T(8,128)(2,1)S(1)}, u32[]{:S(2)}, u32[]{:S(2)}) async-start(bf16[4,128,256]{2,1,0:T(8,128)(2,1)} %bitcast.2), calls=%async_computation.2 | async-start | bytes 524288 | tf_op jit(solution)/shard_map/all_to_all | solution.py:222
  90.3 5.5 %all-to-all-done.2 = bf16[4,128,256]{2,1,0:T(8,128)(2,1)S(1)} async-done(((bf16[4,128,256]{2,1,0:T(8,128)(2,1)}), bf16[4,128,256]{2,1,0:T(8,128)(2,1)S(1)}, u32[]{:S(2)}, u32[]{:S(2)}) %all-to-all-start.2) | async-done | bytes 262176 | tf_op jit(solution)/shard_map/all_to_all | solution.py:222
  98.0 16.1 %while.21 = (s32[]{:T(128)}, bf16[128,256]{1,0:T(8,128)(2,1)S(1)}, s32[]{:T(128)}, s32[]{:T(128)}) while((s32[]{:T(128)}, bf16[128,256]{1,0:T(8,128)(2,1)S(1)}, s32[]{:T(128)}, s32[]{:T(128)}) %tuple.46), condition=%wide.region_5.0_spmd, body=%wide.region_4.0_spmd.sunk | while | flops 393218 | bytes 1376429 | solution.py:262
  98.0 3.2 %collective-permute-done.3 = bf16[128,256]{1,0:T(8,128)(2,1)S(1)} collective-permute-done((bf16[128,256]{1,0:T(8,128)(2,1)S(1)}, bf16[128,256]{1,0:T(8,128)(2,1)S(1)}, u32[]{:S(2)}, u32[]{:S(2)}) %collective-permute-start.3) | collective-permute-done | bytes 65568 | tf_op jit(solution)/shard_map/while/body/ppermute | solution.py:239
  102.3 4.2 %collective-permute-done.4 = bf16[128,256]{1,0:T(8,128)(2,1)S(1)} collective-permute-done((bf16[128,256]{1,0:T(8,128)(2,1)S(1)}, bf16[128,256]{1,0:T(8,128)(2,1)S(1)}, u32[]{:S(2)}, u32[]{:S(2)}) %collective-permute-start.4) | collective-permute-done | bytes 65568 | tf_op jit(solution)/shard_map/while/body/ppermute | solution.py:239
  107.7 6.4 %collective-permute-done.5 = bf16[128,256]{1,0:T(8,128)(2,1)S(1)} collective-permute-done((bf16[128,256]{1,0:T(8,128)(2,1)S(1)}, bf16[128,256]{1,0:T(8,128)(2,1)S(1)}, u32[]{:S(2)}, u32[]{:S(2)}) %collective-permute-start.5) | collective-permute-done | bytes 65568 | tf_op jit(solution)/shard_map/while/body/ppermute | solution.py:239
  115.1 3.8 %all-to-all-start.3 = ((bf16[4,128,256]{2,1,0:T(8,128)(2,1)}), bf16[4,128,256]{2,1,0:T(8,128)(2,1)S(1)}, u32[]{:S(2)}, u32[]{:S(2)}) async-start(bf16[4,128,256]{2,1,0:T(8,128)(2,1)} %broadcast_in_dim.5), calls=%async_computation.3 | async-start | bytes 524288 | tf_op jit(solution)/shard_map/all_to_all | solution.py:222
  120.8 3.6 %all-to-all-done.3 = bf16[4,128,256]{2,1,0:T(8,128)(2,1)S(1)} async-done(((bf16[4,128,256]{2,1,0:T(8,128)(2,1)}), bf16[4,128,256]{2,1,0:T(8,128)(2,1)S(1)}, u32[]{:S(2)}, u32[]{:S(2)}) %all-to-all-start.3) | async-done | bytes 262176 | tf_op jit(solution)/shard_map/all_to_all | solution.py:222
  127.3 15.9 %all-to-all-start.4 = ((bf16[8,192,128]{2,1,0:T(8,128)(2,1)}), bf16[8,192,128]{2,1,0:T(8,128)(2,1)S(1)}, u32[]{:S(2)}, u32[]{:S(2)}) async-start(bf16[8,192,128]{2,1,0:T(8,128)(2,1)} %late.1), calls=%async_computation.5 | async-start | bytes 786432 | tf_op jit(solution)/shard_map/all_to_all | solution.py:421
  143.3 2.6 %collective-permute-start.19 = (bf16[256,384]{1,0:T(8,128)(2,1)S(1)}, bf16[256,384]{1,0:T(8,128)(2,1)S(1)}, u32[]{:S(2)}, u32[]{:S(2)}) collective-permute-start(bf16[256,384]{1,0:T(8,128)(2,1)S(1)} %add_convert_fusion.6), channel_id=1, source_target_pairs={{0,16},{8,24},{16,0},{24,8},{32,48},{40,56},{48,32},{56,40},{64,80... | collective-permute-start | bytes 589832 | tf_op jit(solution)/shard_map/ppermute | solution.py:280
  145.9 9.4 %collective-permute-done.19.refs_3_ = bf16[256,384]{1,0:T(8,128)(2,1)S(1)} collective-permute-done((bf16[256,384]{1,0:T(8,128)(2,1)S(1)}, bf16[256,384]{1,0:T(8,128)(2,1)S(1)}, u32[]{:S(2)}, u32[]{:S(2)}) %collective-permute-start.19) | collective-permute-done | bytes 196640 | tf_op jit(solution)/shard_map/ppermute | solution.py:280
  156.1 2.7 %final.1 = (bf16[256,384]{1,0:T(8,128)(2,1)}, bf16[256,384]{1,0:T(8,128)(2,1)}) custom-call(bf16[512,384]{1,0:T(8,128)(2,1)} %get-tuple-element.93.refs_0_, bf16[512,384]{1,0:T(8,128)(2,1)} %copy-done.9, bf16[256,384]{1,0:T(8,128)(2,1)} %copy-done.11, bf16[256,384]{1,0:T(8,128)(2,1)} %copy-done.12, bf16[512,384]{1,0:T(8,128)(2,1)} %copy-done.7, ...), custom_call_target="tpu_custom_call" | custom-call | flops 100663296 | bytes 3145728 | tf_op jit(solution)/shard_map/final/pallas_call | solution.py:422
  (101 shorter events, 32.0 us)
Async XLA Ops:
  9.4 10.5 %all-to-all-start = ((bf16[4,128,256]{2,1,0:T(8,128)(2,1)}), bf16[4,128,256]{2,1,0:T(8,128)(2,1)S(1)}, u32[]{:S(2)}, u32[]{:S(2)}) async-start(bf16[4,128,256]{2,1,0:T(8,128)(2,1)} %bitcast.10), calls=%async_computation | async-start | bytes 524288 | tf_op jit(solution)/shard_map/all_to_all | solution.py:222
  14.4 26.1 %collective-permute-start.8 = (bf16[256,384]{1,0:T(8,128)(2,1)}, bf16[256,384]{1,0:T(8,128)(2,1)S(1)}, u32[]{:S(2)}, u32[]{:S(2)}) collective-permute-start(bf16[256,384]{1,0:T(8,128)(2,1)} %refs_0_.3), channel_id=1, source_target_pairs={{0,16},{8,24},{16,0},{24,8},{32,48},{40,56},{48,32},{56,40},{64,80... | collective-permute-start | bytes 589832 | tf_op jit(solution)/shard_map/ppermute | solution.py:280
  20.0 20.5 %collective-permute-start.7 = (bf16[512,384]{1,0:T(8,128)(2,1)}, bf16[512,384]{1,0:T(8,128)(2,1)S(1)}, u32[]{:S(2)}, u32[]{:S(2)}) collective-permute-start(bf16[512,384]{1,0:T(8,128)(2,1)} %get-tuple-element.87.both_ref), channel_id=1, source_target_pairs={{0,128},{8,136},{16,144},{24,152},{32,160},{40,168},{48,176},{56,1... | collective-permute-start | bytes 1179656 | tf_op jit(solution)/shard_map/ppermute | solution.py:280
  20.5 20.0 %collective-permute-start.6 = (bf16[512,384]{1,0:T(8,128)(2,1)}, bf16[512,384]{1,0:T(8,128)(2,1)S(1)}, u32[]{:S(2)}, u32[]{:S(2)}) collective-permute-start(bf16[512,384]{1,0:T(8,128)(2,1)} %get-tuple-element.87.both_ref), channel_id=1, source_target_pairs={{0,64},{8,72},{16,80},{24,88},{32,96},{40,104},{48,112},{56,120},{... | collective-permute-start | bytes 1179656 | tf_op jit(solution)/shard_map/ppermute | solution.py:280
  21.6 6.0 %collective-permute-start = (bf16[128,256]{1,0:T(8,128)(2,1)S(1)}, bf16[128,256]{1,0:T(8,128)(2,1)S(1)}, u32[]{:S(2)}, u32[]{:S(2)}) collective-permute-start(bf16[128,256]{1,0:T(8,128)(2,1)S(1)} %get-tuple-element.179), channel_id=1, source_target_pairs={{0,8},{8,0},{16,24},{24,16},{32,40},{40,32},{48,56},{56,48},{64,72... | collective-permute-start | bytes 196616 | tf_op jit(solution)/shard_map/while/body/ppermute | solution.py:239
  32.0 8.4 %collective-permute-start.2 = (bf16[128,256]{1,0:T(8,128)(2,1)S(1)}, bf16[128,256]{1,0:T(8,128)(2,1)S(1)}, u32[]{:S(2)}, u32[]{:S(2)}) collective-permute-start(bf16[128,256]{1,0:T(8,128)(2,1)S(1)} %add_convert_fusion.15), channel_id=1, source_target_pairs={{0,32},{8,40},{16,48},{24,56},{32,0},{40,8},{48,16},{56,24},{64,96... | collective-permute-start | bytes 196616 | tf_op jit(solution)/shard_map/while/body/ppermute | solution.py:239
  40.6 12.0 %collective-permute-start.10 = (bf16[256,384]{1,0:T(8,128)(2,1)S(1)}, bf16[256,384]{1,0:T(8,128)(2,1)S(1)}, u32[]{:S(2)}, u32[]{:S(2)}) collective-permute-start(bf16[256,384]{1,0:T(8,128)(2,1)S(1)} %copy-done.3), channel_id=1, source_target_pairs={{0,16},{8,24},{16,0},{24,8},{32,48},{40,56},{48,32},{56,40},{64,80... | collective-permute-start | bytes 589832 | tf_op jit(solution)/shard_map/ppermute | solution.py:280
  41.2 24.5 %collective-permute-start.9 = (bf16[512,384]{1,0:T(8,128)(2,1)S(1)}, bf16[512,384]{1,0:T(8,128)(2,1)S(1)}, u32[]{:S(2)}, u32[]{:S(2)}) collective-permute-start(bf16[512,384]{1,0:T(8,128)(2,1)S(1)} %copy-done.10), channel_id=1, source_target_pairs={{0,8},{8,0},{16,24},{24,16},{32,40},{40,32},{48,56},{56,48},{64,72... | collective-permute-start | bytes 1179656 | tf_op jit(solution)/shard_map/ppermute | solution.py:280
  43.0 18.1 %collective-permute-start.11 = (bf16[256,384]{1,0:T(8,128)(2,1)S(1)}, bf16[256,384]{1,0:T(8,128)(2,1)S(1)}, u32[]{:S(2)}, u32[]{:S(2)}) collective-permute-start(bf16[256,384]{1,0:T(8,128)(2,1)S(1)} %collective-permute-done.8.refs_3_), channel_id=1, source_target_pairs={{0,48},{8,56},{16,32},{24,40},{32,16},{40,24},{48,0},{56,8},{64,11... | collective-permute-start | bytes 589832 | tf_op jit(solution)/shard_map/ppermute | solution.py:280
  47.0 14.1 %all-to-all-start.1 = ((bf16[4,128,256]{2,1,0:T(8,128)(2,1)}), bf16[4,128,256]{2,1,0:T(8,128)(2,1)S(1)}, u32[]{:S(2)}, u32[]{:S(2)}) async-start(bf16[4,128,256]{2,1,0:T(8,128)(2,1)} %broadcast_in_dim.4), calls=%async_computation.1 | async-start | bytes 524288 | tf_op jit(solution)/shard_map/all_to_all | solution.py:222
  52.6 108.7 %reduce-scatter.2.cloned.1.call-start = ((), (), s32[]{:S(2)}) async-start(), calls=%async_computation.6 | async-start | bytes 6193152 | tf_op jit(solution)/shard_map/reduce_scatter | solution.py:393
  52.6 13.1 %collective-permute-start.12 = (bf16[256,384]{1,0:T(8,128)(2,1)S(1)}, bf16[256,384]{1,0:T(8,128)(2,1)S(1)}, u32[]{:S(2)}, u32[]{:S(2)}) collective-permute-start(bf16[256,384]{1,0:T(8,128)(2,1)S(1)} %collective-permute-done.10.refs_4_), channel_id=1, source_target_pairs={{0,48},{8,56},{16,32},{24,40},{32,16},{40,24},{48,0},{56,8},{64,11... | collective-permute-start | bytes 589832 | tf_op jit(solution)/shard_map/ppermute | solution.py:280
  83.7 12.1 %all-to-all-start.2 = ((bf16[4,128,256]{2,1,0:T(8,128)(2,1)}), bf16[4,128,256]{2,1,0:T(8,128)(2,1)S(1)}, u32[]{:S(2)}, u32[]{:S(2)}) async-start(bf16[4,128,256]{2,1,0:T(8,128)(2,1)} %bitcast.2), calls=%async_computation.2 | async-start | bytes 524288 | tf_op jit(solution)/shard_map/all_to_all | solution.py:222
  90.3 23.9 %collective-permute-start.15 = (bf16[256,384]{1,0:T(8,128)(2,1)S(1)}, bf16[256,384]{1,0:T(8,128)(2,1)S(1)}, u32[]{:S(2)}, u32[]{:S(2)}) collective-permute-start(bf16[256,384]{1,0:T(8,128)(2,1)S(1)} %copy-done.24), channel_id=1, source_target_pairs={{0,48},{8,56},{16,32},{24,40},{32,16},{40,24},{48,0},{56,8},{64,11... | collective-permute-start | bytes 589832 | tf_op jit(solution)/shard_map/ppermute | solution.py:280
  95.9 18.3 %collective-permute-start.13 = (bf16[512,384]{1,0:T(8,128)(2,1)S(1)}, bf16[512,384]{1,0:T(8,128)(2,1)S(1)}, u32[]{:S(2)}, u32[]{:S(2)}) collective-permute-start(bf16[512,384]{1,0:T(8,128)(2,1)S(1)} %copy-done.22), channel_id=1, source_target_pairs={{0,64},{8,72},{16,80},{24,88},{32,96},{40,104},{48,112},{56,120},{... | collective-permute-start | bytes 1179656 | tf_op jit(solution)/shard_map/ppermute | solution.py:280
  96.3 18.0 %collective-permute-start.14 = (bf16[512,384]{1,0:T(8,128)(2,1)S(1)}, bf16[512,384]{1,0:T(8,128)(2,1)S(1)}, u32[]{:S(2)}, u32[]{:S(2)}) collective-permute-start(bf16[512,384]{1,0:T(8,128)(2,1)S(1)} %copy-done.21), channel_id=1, source_target_pairs={{0,128},{8,136},{16,144},{24,152},{32,160},{40,168},{48,176},{56,1... | collective-permute-start | bytes 1179656 | tf_op jit(solution)/shard_map/ppermute | solution.py:280
  101.3 5.2 %collective-permute-start.4 = (bf16[128,256]{1,0:T(8,128)(2,1)S(1)}, bf16[128,256]{1,0:T(8,128)(2,1)S(1)}, u32[]{:S(2)}, u32[]{:S(2)}) collective-permute-start(bf16[128,256]{1,0:T(8,128)(2,1)S(1)} %add_convert_fusion.17), channel_id=1, source_target_pairs={{0,16},{8,24},{16,0},{24,8},{32,48},{40,56},{48,32},{56,40},{64,80... | collective-permute-start | bytes 196616 | tf_op jit(solution)/shard_map/while/body/ppermute | solution.py:239
  106.5 7.6 %collective-permute-start.5 = (bf16[128,256]{1,0:T(8,128)(2,1)S(1)}, bf16[128,256]{1,0:T(8,128)(2,1)S(1)}, u32[]{:S(2)}, u32[]{:S(2)}) collective-permute-start(bf16[128,256]{1,0:T(8,128)(2,1)S(1)} %add_convert_fusion.18), channel_id=1, source_target_pairs={{0,32},{8,40},{16,48},{24,56},{32,0},{40,8},{48,16},{56,24},{64,96... | collective-permute-start | bytes 196616 | tf_op jit(solution)/shard_map/while/body/ppermute | solution.py:239
  114.2 29.0 %collective-permute-start.18 = (bf16[256,384]{1,0:T(8,128)(2,1)S(1)}, bf16[256,384]{1,0:T(8,128)(2,1)S(1)}, u32[]{:S(2)}, u32[]{:S(2)}) collective-permute-start(bf16[256,384]{1,0:T(8,128)(2,1)S(1)} %copy-done.23), channel_id=1, source_target_pairs={{0,48},{8,56},{16,32},{24,40},{32,16},{40,24},{48,0},{56,8},{64,11... | collective-permute-start | bytes 589832 | tf_op jit(solution)/shard_map/ppermute | solution.py:280
  115.1 9.4 %all-to-all-start.3 = ((bf16[4,128,256]{2,1,0:T(8,128)(2,1)}), bf16[4,128,256]{2,1,0:T(8,128)(2,1)S(1)}, u32[]{:S(2)}, u32[]{:S(2)}) async-start(bf16[4,128,256]{2,1,0:T(8,128)(2,1)} %broadcast_in_dim.5), calls=%async_computation.3 | async-start | bytes 524288 | tf_op jit(solution)/shard_map/all_to_all | solution.py:222
  118.9 27.0 %collective-permute-start.17 = (bf16[256,384]{1,0:T(8,128)(2,1)S(1)}, bf16[256,384]{1,0:T(8,128)(2,1)S(1)}, u32[]{:S(2)}, u32[]{:S(2)}) collective-permute-start(bf16[256,384]{1,0:T(8,128)(2,1)S(1)} %add_convert_fusion.7), channel_id=1, source_target_pairs={{0,16},{8,24},{16,0},{24,8},{32,48},{40,56},{48,32},{56,40},{64,80... | collective-permute-start | bytes 589832 | tf_op jit(solution)/shard_map/ppermute | solution.py:280
  119.9 35.3 %collective-permute-start.16 = (bf16[512,384]{1,0:T(8,128)(2,1)S(1)}, bf16[512,384]{1,0:T(8,128)(2,1)S(1)}, u32[]{:S(2)}, u32[]{:S(2)}) collective-permute-start(bf16[512,384]{1,0:T(8,128)(2,1)S(1)} %copy-done.20), channel_id=1, source_target_pairs={{0,8},{8,0},{16,24},{24,16},{32,40},{40,32},{48,56},{56,48},{64,72... | collective-permute-start | bytes 1179656 | tf_op jit(solution)/shard_map/ppermute | solution.py:280
  127.3 31.5 %all-to-all-start.4 = ((bf16[8,192,128]{2,1,0:T(8,128)(2,1)}), bf16[8,192,128]{2,1,0:T(8,128)(2,1)S(1)}, u32[]{:S(2)}, u32[]{:S(2)}) async-start(bf16[8,192,128]{2,1,0:T(8,128)(2,1)} %late.1), calls=%async_computation.5 | async-start | bytes 786432 | tf_op jit(solution)/shard_map/all_to_all | solution.py:421
  143.3 12.0 %collective-permute-start.19 = (bf16[256,384]{1,0:T(8,128)(2,1)S(1)}, bf16[256,384]{1,0:T(8,128)(2,1)S(1)}, u32[]{:S(2)}, u32[]{:S(2)}) collective-permute-start(bf16[256,384]{1,0:T(8,128)(2,1)S(1)} %add_convert_fusion.6), channel_id=1, source_target_pairs={{0,16},{8,24},{16,0},{24,8},{32,48},{40,56},{48,32},{56,40},{64,80... | collective-permute-start | bytes 589832 | tf_op jit(solution)/shard_map/ppermute | solution.py:280
  (27 other events, 465.7 us)
Sparse Core Ops, SparseCore 0:
  83.8 44.1 reduce-scatter.1

commit v5 on v3

--- a/solution.py
+++ b/solution.py
@@ -58,14 +58,15 @@
 
 
 def middle_kernel(levels, index_ref, *refs):
+    rows = refs[0].shape[0] // 2
     fields = refs[:levels]
-    low_ref, up_ref, down_ref, up_right_ref, down_left_ref = refs[levels : levels + 5]
-    act_ref, grad_ref, lowp_ref = refs[levels + 5 : levels + 8]
-    parts = refs[levels + 8 : 2 * levels + 8]
-    out_acc, in_acc, low_acc = refs[2 * levels + 8 :]
+    refs = refs[levels:]
+    low_ref, up_ref, down_ref, up_right_ref, down_left_ref = refs[:5]
+    act_ref, grad_ref, lowp_ref = refs[5:8]
+    parts = refs[8 : 8 + levels]
+    out_acc, in_acc, low_acc = refs[8 + levels :]
     block = pl.program_id(0)
-    rows = low_ref.shape[0] // 2
-    sub = fields[0].shape[1] // 3
+    sub = refs[8].shape[1] // 3
 
     @pl.when(block == 0)
     def _():
@@ -98,21 +99,19 @@
         lowp_ref[...] = low_acc[...].astype(BF)
         for k in range(levels):
             for c in range(3):
-                cols = slice(c * sub, (c + 1) * sub)
-                parts[k][:rows, cols] = out_acc[3 * k + c].astype(BF)
-                parts[k][rows:, cols] = in_acc[3 * k + c].astype(BF)
+                columns = slice(c * sub, (c + 1) * sub)
+                parts[k][:rows, columns] = out_acc[3 * k + c].astype(BF)
+                parts[k][rows:, columns] = in_acc[3 * k + c].astype(BF)
 
 
 def grads_kernel(levels, groups, index_ref, *refs):
+    rows = refs[0].shape[0] // 2
     fields = refs[:levels]
     low_ref, act_ref, grad_ref, out_ref = refs[levels:]
     block = pl.program_id(0)
-    rows = low_ref.shape[0] // 2
-    sub = fields[0].shape[1] // 3
+    sub = refs[0].shape[1] // 3
     width = act_ref.shape[1]
     piece = width // groups
-    per = 3 * piece
-    up_base = (levels + 1) * per
     act_t = act_ref[...].T
     grad = grad_ref[...]
     for k in range(levels + 1):
@@ -127,10 +126,22 @@
         for m in range(groups):
             slot = block * groups + m
             group = slot // 3
-            row = pl.multiple_of(k * per + (slot - 3 * group) * piece, piece)
-            out_ref[group, pl.ds(row, piece), :] = down[m * piece : (m + 1) * piece]
-            row = pl.multiple_of(up_base + (block * (levels + 1) + k) * piece, piece)
-            out_ref[m, pl.ds(row, piece), :] = up[m * piece : (m + 1) * piece]
+            row = pl.multiple_of((slot - 3 * group) * piece, piece)
+            out_ref[group, k, 0, pl.ds(row, piece), :] = down[m * piece : (m + 1) * piece]
+            row = pl.multiple_of(block * piece, piece)
+            out_ref[m, k, 1, pl.ds(row, piece), :] = up[m * piece : (m + 1) * piece]
+
+
+def unpack_kernel(sum_ref, down_ref, left_ref, up_ref, right_ref):
+    levels = down_ref.shape[0]
+    piece = right_ref.shape[0]
+    width = sum_ref.shape[3]
+    down_ref[...] = sum_ref[:levels, 0]
+    left_ref[...] = sum_ref[levels, 0]
+    for b in range(right_ref.shape[1] // width):
+        columns = slice(b * width, (b + 1) * width)
+        up_ref[:, :, columns] = sum_ref[:levels, 1, b * piece : (b + 1) * piece]
+        right_ref[:, columns] = sum_ref[levels, 1, b * piece : (b + 1) * piece]
 
 
 def late_kernel(groups, both_ref, low_ref, out_ref):
@@ -149,18 +160,17 @@
             ]
 
 
-def final_kernel(levels, *refs):
-    parts = refs[:levels]
-    low_ref, down_right_ref, up_left_ref = refs[levels : levels + 3]
-    layer_ref, tokens_ref = refs[levels + 3 :]
+def final_kernel(count, *refs):
+    parts = refs[:count]
+    low_ref, down_right_ref, up_left_ref, layer_ref, tokens_ref = refs[count:]
     rows = low_ref.shape[0] // 2
-    out = parts[0][:rows].astype(F32)
-    back = parts[0][rows:].astype(F32)
-    for k in range(1, levels):
-        out += parts[k][:rows].astype(F32)
-        back += parts[k][rows:].astype(F32)
-    layer_ref[...] = (out + dot(low_ref[:rows], down_right_ref[...])).astype(BF)
-    tokens_ref[...] = (back + dot_nt(low_ref[rows:], up_left_ref[...])).astype(BF)
+    out = dot(low_ref[:rows], down_right_ref[...])
+    back = dot_nt(low_ref[rows:], up_left_ref[...])
+    for ref in parts:
+        out += ref[:rows].astype(F32)
+        back += ref[rows:].astype(F32)
+    layer_ref[...] = out.astype(BF)
+    tokens_ref[...] = back.astype(BF)
 
 
 def last_kernel(late_ref, right_ref, left_ref):
@@ -215,20 +225,23 @@
     return [list(range(i, lax.axis_size("hid"), inner)) for i in range(inner)]
 
 
-def finish_sum(held, distance):
-    trips = 1 + lax.shift_right_logical(lax.axis_index("hid"), 20)
-    outer = len(hid_columns()[0])
-
-    def once(_, carried):
-        value = carried[0]
-        step = distance
-        while step < hid_inner():
+def fence(body, *operands):
+    shapes = jax.eval_shape(body, *operands)
+
+    def skipped(*_):
+        return jax.tree.map(lambda leaf: jnp.zeros(leaf.shape, leaf.dtype), shapes)
+
+    taken = lax.shift_right_logical(lax.axis_index("hid"), 20) == 0
+    return lax.cond(taken, body, skipped, *operands)
+
+
+def line_sum(held, steps):
+    def body(value):
+        for step in steps:
             value = line_step(value, step)
-            step *= 2
-        return value, group_gather(value, hid_columns())
-
-    wide = jnp.zeros((outer * held.shape[0], held.shape[1]), held.dtype)
-    return lax.fori_loop(0, trips, once, (held, wide))[1]
+        return value
+
+    return fence(body, held)
 
 
 def on_device(
@@ -245,10 +258,11 @@
     sub = feat // 3
     sds = jax.ShapeDtypeStruct
 
-    def partner(value, level):
-        distance = 1 << (level - 1)
+    def swap(value, distance):
         return lax.ppermute(value, "hid", [(i, i ^ distance) for i in range(hid_count)])
 
+    tie = lax.optimization_barrier
+    columns = hid_columns()
     both, low_part = pl.pallas_call(
         head_kernel,
         out_shape=(sds((2 * rows, feat), BF), sds((2 * rows, rank), BF)),
@@ -258,13 +272,19 @@
         cost_estimate=cost(4 * rows * feat * rank, 4 * rows * feat * 2),
         name="head",
     )(tokens, cotangent, up_left, down_right)
-    order = [3, 2, 1, 5, 4]
-    fields = [both] + [None] * (levels - 1)
-    for level in order:
-        fields[level] = partner(both, level)
-    total = group_scatter(low_part, hid_columns())
-    total, fields[4] = lax.optimization_barrier((total, fields[4]))
-    low = finish_sum(total, 1)
+    z_two = swap(both, 2)
+    total = group_scatter(low_part, columns)
+    total, both_x = tie((total, both))
+    x_one = swap(both_x, 8)
+    x_two = swap(both_x, 16)
+    total, z_two, x_one, x_two, both_z = tie(
+        (line_sum(total, (6, 1, 2)), z_two, x_one, x_two, both)
+    )
+    z_four = swap(z_two, 6)
+    z_one = swap(both_z, 1)
+    low = group_gather(total, columns)
+    fields = [both, z_one, z_two, z_four, x_one, x_two]
+    part_shapes = [(2 * rows, feat)] * levels
 
     def whole(shape):
         return pl.BlockSpec(shape, lambda b, *_: (0,) * len(shape))
@@ -278,7 +298,7 @@
         grid_spec=pltpu.PrefetchScalarGridSpec(
             num_scalar_prefetch=1,
             grid=(blocks,),
-            in_specs=[whole((2 * rows, feat))] * levels
+            in_specs=[whole(field.shape) for field in fields]
             + [
                 whole((2 * rows, rank)),
                 pl.BlockSpec((levels, 2 * sub, width), lambda b, *_: (0, 0, b)),
@@ -291,7 +311,7 @@
                 pl.BlockSpec((rows, width), lambda b, *_: (0, b)),
                 whole((2 * rows, rank)),
             ]
-            + [whole((2 * rows, feat))] * levels,
+            + [whole(shape) for shape in part_shapes],
             scratch_shapes=[
                 pltpu.VMEM((3 * levels, rows, sub), F32),
                 pltpu.VMEM((3 * levels, rows, sub), F32),
@@ -303,7 +323,7 @@
             sds((rows, hidden), BF),
             sds((2 * rows, rank), BF),
         ]
-        + [sds((2 * rows, feat), BF)] * levels,
+        + [sds(shape, BF) for shape in part_shapes],
         compiler_params=grid_params,
         cost_estimate=cost(4 * flops, 10 * 1024 * 1024),
         name="middle",
@@ -312,42 +332,58 @@
     parts = list(middle[3:])
 
     piece = width // groups
-    chunk = 2 * (levels + 1) * 3 * piece
-    packed = pl.pallas_call(
+    packed_shape = (groups, levels + 1, 2, 3 * piece, width)
+    grads = pl.pallas_call(
         functools.partial(grads_kernel, levels, groups),
         grid_spec=pltpu.PrefetchScalarGridSpec(
             num_scalar_prefetch=1,
             grid=(blocks,),
-            in_specs=[whole((2 * rows, feat))] * levels
+            in_specs=[whole(field.shape) for field in fields]
             + [
                 whole((2 * rows, rank)),
                 pl.BlockSpec((rows, width), lambda b, *_: (0, b)),
                 pl.BlockSpec((rows, width), lambda b, *_: (0, b)),
             ],
-            out_specs=whole((groups, chunk, width)),
+            out_specs=whole(packed_shape),
         ),
-        out_shape=sds((groups, chunk, width), BF),
+        out_shape=sds(packed_shape, BF),
         compiler_params=grid_params,
         cost_estimate=cost(2 * flops, 10 * 1024 * 1024),
         name="grads",
-    )(block_index, *fields, low, act, grad_pre)
-
-    for level in order:
-        parts[level] = partner(parts[level], level)
-    total = group_scatter(lowp, hid_columns())
-    total, parts[4] = lax.optimization_barrier((total, parts[4]))
-    low2 = finish_sum(total, 1)
+    )
+
+
+    own, z_one, z_two, z_four, x_one, x_two = parts
+    z_four = swap(z_four, 6)
+
+    total = group_scatter(lowp, columns)
+    packed = grads(block_index, *fields, low, act, grad_pre)
+    total, packed = tie((total, packed))
+    total, z_four, x_one, x_two, z_one = tie(
+        (line_sum(total, (2, 1, 6)), z_four, x_one, x_two, z_one)
+    )
+    z_two = swap((z_two.astype(F32) + z_four.astype(F32)).astype(BF), 2)
+    low2 = group_gather(total, columns)
+    x_one = swap(x_one, 8)
+    x_two = swap(x_two, 16)
+    z_one = swap(z_one, 1)
     summed = lax.psum_scatter(
-        packed.reshape(groups * chunk, width), "tok", scatter_dimension=0, tiled=True
-    )
-    half = (levels + 1) * 3 * piece
-    down_sum = summed[:half].reshape(levels + 1, 3 * piece, width)
-    up_sum = summed[half:].reshape(blocks, levels + 1, piece, width)
-    grad_down_tiles = down_sum[:levels]
-    grad_down_left = down_sum[levels]
-    up_sum = up_sum.transpose(1, 2, 0, 3).reshape(levels + 1, piece, hidden)
-    grad_up_tiles = up_sum[:levels]
-    grad_up_right = up_sum[levels]
+        packed.reshape(-1, width), "tok", scatter_dimension=0, tiled=True
+    ).reshape(packed.shape[1:])
+    grad_down_tiles, grad_down_left, grad_up_tiles, grad_up_right = pl.pallas_call(
+        unpack_kernel,
+        out_shape=(
+            sds((levels, hidden // groups, 2 * sub), BF),
+            sds((hidden // groups, rank), BF),
+            sds((levels, 2 * sub // groups, hidden), BF),
+            sds((rank // groups, hidden), BF),
+        ),
+        in_specs=[vmem_spec()],
+        out_specs=(vmem_spec(),) * 4,
+        compiler_params=params(),
+        cost_estimate=cost(0, packed.size // 2),
+        name="unpack",
+    )(summed)
 
     late_rows = (rank // groups) * (feat // 128) + (feat // groups) * (rank // 128)
     late = pl.pallas_call(
@@ -358,13 +394,15 @@
         compiler_params=params(),
         cost_estimate=cost(4 * rows * feat * rank, 4 * rows * feat * 2),
         name="late",
-    )(both, low2)
-    late, parts = lax.optimization_barrier((late, parts))
-    late = lax.all_to_all(late, "tok", 0, 0, tiled=True)
+    )
+
+    moved = late(both, low2)
+    moved = lax.all_to_all(moved, "tok", 0, 0, tiled=True)
+    parts = (own, z_one, z_two, x_one, x_two)
     layer_out, grad_tokens = pl.pallas_call(
-        functools.partial(final_kernel, levels),
+        functools.partial(final_kernel, len(parts)),
         out_shape=(sds((rows, feat), BF), sds((rows, feat), BF)),
-        in_specs=[vmem_spec()] * (levels + 3),
+        in_specs=[vmem_spec()] * (len(parts) + 3),
         out_specs=(vmem_spec(),) * 2,
         compiler_params=params(),
         cost_estimate=cost(4 * rows * feat * rank, 16 * rows * feat * 2),
@@ -378,7 +416,7 @@
         compiler_params=params(),
         cost_estimate=cost(rows * feat, 3 * rows * feat),
         name="last",
-    )(late)
+    )(moved)
     return (
         layer_out,
         grad_tokens,

time: 199 us -> 154 us (0.77)
  waiting for transfers between devices: 84.1 us -> 35 us
  starting transfers between devices: 60.6 us -> 68.9 us
  local copies, waits for them, and re-layouts: 12.4 us -> 6.08 us
    ppermute x6, waiting for transfers between devices: 67.8 us -> 18.6 us  [line_step(): other = lax.ppermute(held, 'hid', [(i, i ^ distance) for i in range(count)])]
    ppermute x10, waiting for transfers between devices: 0.03 us -> 7.29 us  [swap(): lax.ppermute(value, 'hid', [(i, i ^ distance) for i in range(hid_count)])]
    ppermute x6, starting transfers between devices: 12.3 us -> 19.1 us  [line_step(): other = lax.ppermute(held, 'hid', [(i, i ^ distance) for i in range(count)])]
    all_to_all x4, waiting for transfers between devices: 11.2 us -> 7.37 us  [group_exchange(): lax.all_to_all(pieces, 'hid', 0, 0, axis_index_groups=groups, tiled=True)]
    slice x6 -> x0, local copies, waits for them, and re-layouts: 3.64 us -> none  [the longest x2 1.19 us: on_device(): grad_up_tiles = up_sum[:levels]]
    all_to_all x4, starting transfers between devices: 14.6 us -> 18.3 us  [group_exchange(): lax.all_to_all(pieces, 'hid', 0, 0, axis_index_groups=groups, tiled=True)]
    all_to_all x1, waiting for transfers between devices: 5.18 us -> 1.74 us  [on_device(): moved = lax.all_to_all(moved, 'tok', 0, 0, tiled=True)]
    pallas_call x3 -> x4, Pallas kernels: 12.5 us -> 14.3 us  [the longest x1 7.47 us: on_device(): packed = grads(block_index, *fields, low, act, grad_pre)]
  transfers between devices with their start and end apart: 22 -> 22, of which waited for: 10 -> 13; matrix products, arithmetic and copies ran while one was open for 2% -> 2% of each run, Pallas kernels for 3% -> 9%
where the time goes in v5:
time: 154 us; the launch traced here: 152 us
  starting transfers between devices  68.9 us (45%)
  waiting for transfers between devices  35 us (23%)
  Pallas kernels  27.8 us (18%)
  between operations  14.2 us (9%)
  local copies, waits for them, and re-layouts  6.08 us (4%)
    ppermute x10, starting transfers between devices, swap(): lax.ppermute(value, 'hid', [(i, i ^ distance) for i in range(hid_count)])  21.6 us
    ppermute x6, starting transfers between devices, line_step(): other = lax.ppermute(held, 'hid', [(i, i ^ distance) for i in range(count)])  19.1 us
    ppermute x6, waiting for transfers between devices, line_step(): other = lax.ppermute(held, 'hid', [(i, i ^ distance) for i in range(count)])  18.6 us
    all_to_all x4, starting transfers between devices, group_exchange(): lax.all_to_all(pieces, 'hid', 0, 0, axis_index_groups=groups, tiled=True)  18.3 us
    all_to_all x1, starting transfers between devices, on_device(): moved = lax.all_to_all(moved, 'tok', 0, 0, tiled=True)  9.91 us
    pallas_call x1, Pallas kernels, on_device(): pl.pallas_call(functools.partial(middle_kernel, levels), grid_spec=pltpu....  9.61 us
    pallas_call x1, Pallas kernels, on_device(): packed = grads(block_index, *fields, low, act, grad_pre)  7.47 us
    all_to_all x4, waiting for transfers between devices, group_exchange(): lax.all_to_all(pieces, 'hid', 0, 0, axis_index_groups=groups, tiled=True)  7.37 us
  transfers between devices with their start and end apart: 22, of which 13 were waited for; matrix products, arithmetic and copies ran while one was open for 2% of the time, Pallas kernels for 9%

profile of v5, /device:TPU:1, one launch (start us, length us, event | category | flops | bytes accessed | tf_op | source)
XLA Modules:
  0.0 152.3 jit_solution(5031487458480316142)
XLA Ops:
  9.4 4.8 %all-to-all-start = ((bf16[4,128,256]{2,1,0:T(8,128)(2,1)}), bf16[4,128,256]{2,1,0:T(8,128)(2,1)S(1)}, u32[]{:S(2)}, u32[]{:S(2)}) async-start(bf16[4,128,256]{2,1,0:T(8,128)(2,1)} %bitcast.13), calls=%async_computation | async-start | bytes 524288 | tf_op jit(solution)/shard_map/all_to_all | solution.py:198
  14.3 3.0 %collective-permute-start.6 = (bf16[512,384]{1,0:T(8,128)(2,1)}, bf16[512,384]{1,0:T(8,128)(2,1)S(1)}, u32[]{:S(2)}, u32[]{:S(2)}) collective-permute-start(bf16[512,384]{1,0:T(8,128)(2,1)} %get-tuple-element.53.refs_0_.both_ref), channel_id=1, source_target_pairs={{0,16},{8,24},{16,0},{24,8},{32,48},{40,56},{48,32},{56,40},{64,80... | collective-permute-start | bytes 1179656 | tf_op jit(solution)/shard_map/ppermute | solution.py:262
  17.2 2.5 %all-to-all-done = bf16[4,128,256]{2,1,0:T(8,128)(2,1)S(1)} async-done(((bf16[4,128,256]{2,1,0:T(8,128)(2,1)}), bf16[4,128,256]{2,1,0:T(8,128)(2,1)S(1)}, u32[]{:S(2)}, u32[]{:S(2)}) %all-to-all-start) | async-done | bytes 262176 | tf_op jit(solution)/shard_map/all_to_all | solution.py:198
  21.4 22.8 %conditional.2 = (bf16[128,256]{1,0:T(8,128)(2,1)S(1)}) conditional(s32[]{:T(128)} %convert_element_type.71, () %tuple.24, bf16[128,256]{1,0:T(8,128)(2,1)S(1)} %reduce_sum.24), branch_computations={%region_1.0_spmd, %region_2.0_spmd} | conditional | flops 393216 | bytes 1376384 | solution.py:235
  21.4 6.0 %collective-permute-start = (bf16[128,256]{1,0:T(8,128)(2,1)S(1)}, bf16[128,256]{1,0:T(8,128)(2,1)S(1)}, u32[]{:S(2)}, u32[]{:S(2)}) collective-permute-start(bf16[128,256]{1,0:T(8,128)(2,1)S(1)} %param.1), channel_id=1, source_target_pairs={{0,48},{8,56},{16,32},{24,40},{32,16},{40,24},{48,0},{56,8},{64,11... | collective-permute-start | bytes 196616 | tf_op jit(solution)/shard_map/cond/branch_1_fun/ppermute | solution.py:215
  29.4 6.9 %collective-permute-start.1 = (bf16[128,256]{1,0:T(8,128)(2,1)S(1)}, bf16[128,256]{1,0:T(8,128)(2,1)S(1)}, u32[]{:S(2)}, u32[]{:S(2)}) collective-permute-start(bf16[128,256]{1,0:T(8,128)(2,1)S(1)} %add_convert_fusion.2), channel_id=1, source_target_pairs={{0,8},{8,0},{16,24},{24,16},{32,40},{40,32},{48,56},{56,48},{64,72... | collective-permute-start | bytes 196616 | tf_op jit(solution)/shard_map/cond/branch_1_fun/ppermute | solution.py:215
  38.3 3.5 %collective-permute-start.2 = (bf16[128,256]{1,0:T(8,128)(2,1)S(1)}, bf16[128,256]{1,0:T(8,128)(2,1)S(1)}, u32[]{:S(2)}, u32[]{:S(2)}) collective-permute-start(bf16[128,256]{1,0:T(8,128)(2,1)S(1)} %add_convert_fusion.1), channel_id=1, source_target_pairs={{0,16},{8,24},{16,0},{24,8},{32,48},{40,56},{48,32},{56,40},{64,80... | collective-permute-start | bytes 196616 | tf_op jit(solution)/shard_map/cond/branch_1_fun/ppermute | solution.py:215
  44.4 3.9 %collective-permute-start.10 = (bf16[512,384]{1,0:T(8,128)(2,1)S(1)}, bf16[512,384]{1,0:T(8,128)(2,1)S(1)}, u32[]{:S(2)}, u32[]{:S(2)}) collective-permute-start(bf16[512,384]{1,0:T(8,128)(2,1)S(1)} %collective-permute-done.6.refs_2_), channel_id=1, source_target_pairs={{0,48},{8,56},{16,32},{24,40},{32,16},{40,24},{48,0},{56,8},{64,11... | collective-permute-start | bytes 1179656 | tf_op jit(solution)/shard_map/ppermute | solution.py:262
  49.0 4.5 %all-to-all-start.1 = ((bf16[4,128,256]{2,1,0:T(8,128)(2,1)}), bf16[4,128,256]{2,1,0:T(8,128)(2,1)S(1)}, u32[]{:S(2)}, u32[]{:S(2)}) async-start(bf16[4,128,256]{2,1,0:T(8,128)(2,1)} %broadcast_in_dim.4), calls=%async_computation.1 | async-start | bytes 524288 | tf_op jit(solution)/shard_map/all_to_all | solution.py:198
  54.2 4.8 %all-to-all-done.1 = bf16[4,128,256]{2,1,0:T(8,128)(2,1)S(1)} async-done(((bf16[4,128,256]{2,1,0:T(8,128)(2,1)}), bf16[4,128,256]{2,1,0:T(8,128)(2,1)S(1)}, u32[]{:S(2)}, u32[]{:S(2)}) %all-to-all-start.1) | async-done | bytes 262176 | tf_op jit(solution)/shard_map/all_to_all | solution.py:198
  59.0 4.5 %collective-permute-done.10.refs_3_ = bf16[512,384]{1,0:T(8,128)(2,1)S(1)} collective-permute-done((bf16[512,384]{1,0:T(8,128)(2,1)S(1)}, bf16[512,384]{1,0:T(8,128)(2,1)S(1)}, u32[]{:S(2)}, u32[]{:S(2)}) %collective-permute-start.10) | collective-permute-done | bytes 393248 | tf_op jit(solution)/shard_map/ppermute | solution.py:262
  64.3 9.6 %middle.1 = (bf16[256,768]{1,0:T(8,128)(2,1)}, bf16[256,768]{1,0:T(8,128)(2,1)}, bf16[512,256]{1,0:T(8,128)(2,1)}, bf16[512,384]{1,0:T(8,128)(2,1)}, bf16[512,38...) custom-call(s32[6,3,2]{2,1,0:T(4,128)} %copy.17.index_ref, ...), custom_call_target="tpu_custom_call" | custom-call | flops 2818572288 | bytes 10485760 | tf_op jit(solution)/shard_map/middle/pallas_call | solution.py:296
  73.9 4.8 %all-to-all-start.2 = ((bf16[4,128,256]{2,1,0:T(8,128)(2,1)}), bf16[4,128,256]{2,1,0:T(8,128)(2,1)S(1)}, u32[]{:S(2)}, u32[]{:S(2)}) async-start(bf16[4,128,256]{2,1,0:T(8,128)(2,1)} %bitcast.12), calls=%async_computation.2 | async-start | bytes 524288 | tf_op jit(solution)/shard_map/all_to_all | solution.py:198
  78.7 7.5 %grads.1 = bf16[8,7,2,96,256]{4,3,2,1,0:T(8,128)(2,1)} custom-call(s32[6,3,2]{2,1,0:T(4,128)} %copy.17.index_ref, bf16[512,384]{1,0:T(8,128)(2,1)} %get-tuple-element.53.refs_0_.both_ref, bf16[512,384]{1,0:T(8,128)(2,1)} %copy-done.6, bf16[512,384]{1,0:T(8,128)(2,1)} %copy-done.3, bf16[512,384]{1,0:T(8,128)(2,1)} %copy-done.7, bf16[512,384]{1,0:T(8,128)(2,1)} %copy-done.5, ...), custom_call_target="tpu_custom_call" | custom-call | flops 1409286144 | bytes 10485760 | tf_op jit(solution)/shard_map/grads/pallas_call | solution.py:360
  87.2 4.3 %collective-permute-start.11 = (bf16[512,384]{1,0:T(8,128)(2,1)S(1)}, bf16[512,384]{1,0:T(8,128)(2,1)S(1)}, u32[]{:S(2)}, u32[]{:S(2)}) collective-permute-start(bf16[512,384]{1,0:T(8,128)(2,1)S(1)} %copy-done.17), channel_id=1, source_target_pairs={{0,48},{8,56},{16,32},{24,40},{32,16},{40,24},{48,0},{56,8},{64,11... | collective-permute-start | bytes 1179656 | tf_op jit(solution)/shard_map/ppermute | solution.py:262
  91.5 15.1 %conditional.3 = (bf16[128,256]{1,0:T(8,128)(2,1)S(1)}) conditional(s32[]{:T(128)} %convert_element_type.71, () %tuple.27, bf16[128,256]{1,0:T(8,128)(2,1)S(1)} %reduce_sum.25), branch_computations={%region_4.0_spmd, %region_5.0_spmd} | conditional | flops 393216 | bytes 1376384 | solution.py:235
  91.5 4.1 %collective-permute-done.3 = bf16[128,256]{1,0:T(8,128)(2,1)S(1)} collective-permute-done((bf16[128,256]{1,0:T(8,128)(2,1)S(1)}, bf16[128,256]{1,0:T(8,128)(2,1)S(1)}, u32[]{:S(2)}, u32[]{:S(2)}) %collective-permute-start.3) | collective-permute-done | bytes 65568 | tf_op jit(solution)/shard_map/cond/branch_1_fun/ppermute | solution.py:215
  95.7 2.6 %collective-permute-start.4 = (bf16[128,256]{1,0:T(8,128)(2,1)S(1)}, bf16[128,256]{1,0:T(8,128)(2,1)S(1)}, u32[]{:S(2)}, u32[]{:S(2)}) collective-permute-start(bf16[128,256]{1,0:T(8,128)(2,1)S(1)} %add_convert_fusion.5), channel_id=1, source_target_pairs={{0,8},{8,0},{16,24},{24,16},{32,40},{40,32},{48,56},{56,48},{64,72... | collective-permute-start | bytes 196616 | tf_op jit(solution)/shard_map/cond/branch_1_fun/ppermute | solution.py:215
  100.4 6.2 %collective-permute-done.5 = bf16[128,256]{1,0:T(8,128)(2,1)S(1)} collective-permute-done((bf16[128,256]{1,0:T(8,128)(2,1)S(1)}, bf16[128,256]{1,0:T(8,128)(2,1)S(1)}, u32[]{:S(2)}, u32[]{:S(2)}) %collective-permute-start.5) | collective-permute-done | bytes 65568 | tf_op jit(solution)/shard_map/cond/branch_1_fun/ppermute | solution.py:215
  107.4 4.1 %all-to-all-start.3 = ((bf16[4,128,256]{2,1,0:T(8,128)(2,1)}), bf16[4,128,256]{2,1,0:T(8,128)(2,1)S(1)}, u32[]{:S(2)}, u32[]{:S(2)}) async-start(bf16[4,128,256]{2,1,0:T(8,128)(2,1)} %broadcast_in_dim.5), calls=%async_computation.3 | async-start | bytes 524288 | tf_op jit(solution)/shard_map/all_to_all | solution.py:198
  111.6 4.7 %collective-permute-start.13 = (bf16[512,384]{1,0:T(8,128)(2,1)S(1)}, bf16[512,384]{1,0:T(8,128)(2,1)S(1)}, u32[]{:S(2)}, u32[]{:S(2)}) collective-permute-start(bf16[512,384]{1,0:T(8,128)(2,1)S(1)} %add_convert_fusion.6), channel_id=1, source_target_pairs={{0,16},{8,24},{16,0},{24,8},{32,48},{40,56},{48,32},{56,40},{64,80... | collective-permute-start | bytes 1179656 | tf_op jit(solution)/shard_map/ppermute | solution.py:262
  117.9 2.4 %collective-permute-start.15 = (bf16[512,384]{1,0:T(8,128)(2,1)S(1)}, bf16[512,384]{1,0:T(8,128)(2,1)S(1)}, u32[]{:S(2)}, u32[]{:S(2)}) collective-permute-start(bf16[512,384]{1,0:T(8,128)(2,1)S(1)} %copy-done.14), channel_id=1, source_target_pairs={{0,128},{8,136},{16,144},{24,152},{32,160},{40,168},{48,176},{56,1... | collective-permute-start | bytes 1179656 | tf_op jit(solution)/shard_map/ppermute | solution.py:262
  123.1 9.9 %all-to-all-start.4 = ((bf16[8,192,128]{2,1,0:T(8,128)(2,1)}), bf16[8,192,128]{2,1,0:T(8,128)(2,1)S(1)}, u32[]{:S(2)}, u32[]{:S(2)}) async-start(bf16[8,192,128]{2,1,0:T(8,128)(2,1)} %late.1), calls=%async_computation.5 | async-start | bytes 786432 | tf_op jit(solution)/shard_map/all_to_all | solution.py:400
  136.6 2.8 %final.1 = (bf16[256,384]{1,0:T(8,128)(2,1)}, bf16[256,384]{1,0:T(8,128)(2,1)}) custom-call(bf16[512,384]{1,0:T(8,128)(2,1)} %get-tuple-element.58.refs_0_, bf16[512,384]{1,0:T(8,128)(2,1)} %copy-done.9, bf16[512,384]{1,0:T(8,128)(2,1)} %copy-done.8, bf16[512,384]{1,0:T(8,128)(2,1)} %copy-done.10, bf16[512,384]{1,0:T(8,128)(2,1)} %copy-done.11, ...), custom_call_target="tpu_custom_call" | custom-call | flops 100663296 | bytes 3145728 | tf_op jit(solution)/shard_map/final/pallas_call | solution.py:402
  (78 shorter events, 30.6 us)
Async XLA Ops:
  7.2 46.3 %copy-start.13 = (s32[6,3,2]{0,2,1:T(2,128)S(1)}, s32[6,3,2]{0,2,1:T(2,128)}, u32[]{:S(2)}) copy-start(s32[6,3,2]{0,2,1:T(2,128)} %param.17) | copy-start | bytes 436
  9.4 10.4 %all-to-all-start = ((bf16[4,128,256]{2,1,0:T(8,128)(2,1)}), bf16[4,128,256]{2,1,0:T(8,128)(2,1)S(1)}, u32[]{:S(2)}, u32[]{:S(2)}) async-start(bf16[4,128,256]{2,1,0:T(8,128)(2,1)} %bitcast.13), calls=%async_computation | async-start | bytes 524288 | tf_op jit(solution)/shard_map/all_to_all | solution.py:198
  14.3 30.0 %collective-permute-start.6 = (bf16[512,384]{1,0:T(8,128)(2,1)}, bf16[512,384]{1,0:T(8,128)(2,1)S(1)}, u32[]{:S(2)}, u32[]{:S(2)}) collective-permute-start(bf16[512,384]{1,0:T(8,128)(2,1)} %get-tuple-element.53.refs_0_.both_ref), channel_id=1, source_target_pairs={{0,16},{8,24},{16,0},{24,8},{32,48},{40,56},{48,32},{56,40},{64,80... | collective-permute-start | bytes 1179656 | tf_op jit(solution)/shard_map/ppermute | solution.py:262
  19.8 24.4 %collective-permute-start.8 = (bf16[512,384]{1,0:T(8,128)(2,1)}, bf16[512,384]{1,0:T(8,128)(2,1)S(1)}, u32[]{:S(2)}, u32[]{:S(2)}) collective-permute-start(bf16[512,384]{1,0:T(8,128)(2,1)} %get-tuple-element.53.refs_0_.both_ref), channel_id=1, source_target_pairs={{0,128},{8,136},{16,144},{24,152},{32,160},{40,168},{48,176},{56,1... | collective-permute-start | bytes 1179656 | tf_op jit(solution)/shard_map/ppermute | solution.py:262
  20.3 23.9 %collective-permute-start.7 = (bf16[512,384]{1,0:T(8,128)(2,1)}, bf16[512,384]{1,0:T(8,128)(2,1)S(1)}, u32[]{:S(2)}, u32[]{:S(2)}) collective-permute-start(bf16[512,384]{1,0:T(8,128)(2,1)} %get-tuple-element.53.refs_0_.both_ref), channel_id=1, source_target_pairs={{0,64},{8,72},{16,80},{24,88},{32,96},{40,104},{48,112},{56,120},{... | collective-permute-start | bytes 1179656 | tf_op jit(solution)/shard_map/ppermute | solution.py:262
  21.4 7.9 %collective-permute-start = (bf16[128,256]{1,0:T(8,128)(2,1)S(1)}, bf16[128,256]{1,0:T(8,128)(2,1)S(1)}, u32[]{:S(2)}, u32[]{:S(2)}) collective-permute-start(bf16[128,256]{1,0:T(8,128)(2,1)S(1)} %param.1), channel_id=1, source_target_pairs={{0,48},{8,56},{16,32},{24,40},{32,16},{40,24},{48,0},{56,8},{64,11... | collective-permute-start | bytes 196616 | tf_op jit(solution)/shard_map/cond/branch_1_fun/ppermute | solution.py:215
  29.4 8.9 %collective-permute-start.1 = (bf16[128,256]{1,0:T(8,128)(2,1)S(1)}, bf16[128,256]{1,0:T(8,128)(2,1)S(1)}, u32[]{:S(2)}, u32[]{:S(2)}) collective-permute-start(bf16[128,256]{1,0:T(8,128)(2,1)S(1)} %add_convert_fusion.2), channel_id=1, source_target_pairs={{0,8},{8,0},{16,24},{24,16},{32,40},{40,32},{48,56},{56,48},{64,72... | collective-permute-start | bytes 196616 | tf_op jit(solution)/shard_map/cond/branch_1_fun/ppermute | solution.py:215
  38.3 5.9 %collective-permute-start.2 = (bf16[128,256]{1,0:T(8,128)(2,1)S(1)}, bf16[128,256]{1,0:T(8,128)(2,1)S(1)}, u32[]{:S(2)}, u32[]{:S(2)}) collective-permute-start(bf16[128,256]{1,0:T(8,128)(2,1)S(1)} %add_convert_fusion.1), channel_id=1, source_target_pairs={{0,16},{8,24},{16,0},{24,8},{32,48},{40,56},{48,32},{56,40},{64,80... | collective-permute-start | bytes 196616 | tf_op jit(solution)/shard_map/cond/branch_1_fun/ppermute | solution.py:215
  44.3 14.8 %collective-permute-start.9 = (bf16[512,384]{1,0:T(8,128)(2,1)}, bf16[512,384]{1,0:T(8,128)(2,1)S(1)}, u32[]{:S(2)}, u32[]{:S(2)}) collective-permute-start(bf16[512,384]{1,0:T(8,128)(2,1)} %get-tuple-element.53.refs_0_.both_ref), channel_id=1, source_target_pairs={{0,8},{8,0},{16,24},{24,16},{32,40},{40,32},{48,56},{56,48},{64,72... | collective-permute-start | bytes 1179656 | tf_op jit(solution)/shard_map/ppermute | solution.py:262
  44.4 19.2 %collective-permute-start.10 = (bf16[512,384]{1,0:T(8,128)(2,1)S(1)}, bf16[512,384]{1,0:T(8,128)(2,1)S(1)}, u32[]{:S(2)}, u32[]{:S(2)}) collective-permute-start(bf16[512,384]{1,0:T(8,128)(2,1)S(1)} %collective-permute-done.6.refs_2_), channel_id=1, source_target_pairs={{0,48},{8,56},{16,32},{24,40},{32,16},{40,24},{48,0},{56,8},{64,11... | collective-permute-start | bytes 1179656 | tf_op jit(solution)/shard_map/ppermute | solution.py:262
  49.0 10.1 %all-to-all-start.1 = ((bf16[4,128,256]{2,1,0:T(8,128)(2,1)}), bf16[4,128,256]{2,1,0:T(8,128)(2,1)S(1)}, u32[]{:S(2)}, u32[]{:S(2)}) async-start(bf16[4,128,256]{2,1,0:T(8,128)(2,1)} %broadcast_in_dim.4), calls=%async_computation.1 | async-start | bytes 524288 | tf_op jit(solution)/shard_map/all_to_all | solution.py:198
  73.9 12.2 %all-to-all-start.2 = ((bf16[4,128,256]{2,1,0:T(8,128)(2,1)}), bf16[4,128,256]{2,1,0:T(8,128)(2,1)S(1)}, u32[]{:S(2)}, u32[]{:S(2)}) async-start(bf16[4,128,256]{2,1,0:T(8,128)(2,1)} %bitcast.12), calls=%async_computation.2 | async-start | bytes 524288 | tf_op jit(solution)/shard_map/all_to_all | solution.py:198
  78.7 64.8 %reduce-scatter.2.cloned.1.call-start = ((), (), s32[]{:S(2)}) async-start(), calls=%async_computation.6 | async-start | bytes 6193152 | tf_op jit(solution)/shard_map/reduce_scatter | solution.py:370
  86.3 31.6 %copy-start.14 = (bf16[512,384]{1,0:T(8,128)(2,1)S(1)}, bf16[512,384]{1,0:T(8,128)(2,1)}, u32[]{:S(2)}) copy-start(bf16[512,384]{1,0:T(8,128)(2,1)} %get-tuple-element.71) | copy-start | bytes 1179652
  87.2 19.4 %collective-permute-start.11 = (bf16[512,384]{1,0:T(8,128)(2,1)S(1)}, bf16[512,384]{1,0:T(8,128)(2,1)S(1)}, u32[]{:S(2)}, u32[]{:S(2)}) collective-permute-start(bf16[512,384]{1,0:T(8,128)(2,1)S(1)} %copy-done.17), channel_id=1, source_target_pairs={{0,48},{8,56},{16,32},{24,40},{32,16},{40,24},{48,0},{56,8},{64,11... | collective-permute-start | bytes 1179656 | tf_op jit(solution)/shard_map/ppermute | solution.py:262
  91.5 4.1 %collective-permute-start.3 = (bf16[128,256]{1,0:T(8,128)(2,1)S(1)}, bf16[128,256]{1,0:T(8,128)(2,1)S(1)}, u32[]{:S(2)}, u32[]{:S(2)}) collective-permute-start(bf16[128,256]{1,0:T(8,128)(2,1)S(1)} %param.3), channel_id=1, source_target_pairs={{0,16},{8,24},{16,0},{24,8},{32,48},{40,56},{48,32},{56,40},{64,80... | collective-permute-start | bytes 196616 | tf_op jit(solution)/shard_map/cond/branch_1_fun/ppermute | solution.py:215
  95.7 4.6 %collective-permute-start.4 = (bf16[128,256]{1,0:T(8,128)(2,1)S(1)}, bf16[128,256]{1,0:T(8,128)(2,1)S(1)}, u32[]{:S(2)}, u32[]{:S(2)}) collective-permute-start(bf16[128,256]{1,0:T(8,128)(2,1)S(1)} %add_convert_fusion.5), channel_id=1, source_target_pairs={{0,8},{8,0},{16,24},{24,16},{32,40},{40,32},{48,56},{56,48},{64,72... | collective-permute-start | bytes 196616 | tf_op jit(solution)/shard_map/cond/branch_1_fun/ppermute | solution.py:215
  100.3 6.3 %collective-permute-start.5 = (bf16[128,256]{1,0:T(8,128)(2,1)S(1)}, bf16[128,256]{1,0:T(8,128)(2,1)S(1)}, u32[]{:S(2)}, u32[]{:S(2)}) collective-permute-start(bf16[128,256]{1,0:T(8,128)(2,1)S(1)} %add_convert_fusion.4), channel_id=1, source_target_pairs={{0,48},{8,56},{16,32},{24,40},{32,16},{40,24},{48,0},{56,8},{64,11... | collective-permute-start | bytes 196616 | tf_op jit(solution)/shard_map/cond/branch_1_fun/ppermute | solution.py:215
  107.4 12.9 %all-to-all-start.3 = ((bf16[4,128,256]{2,1,0:T(8,128)(2,1)}), bf16[4,128,256]{2,1,0:T(8,128)(2,1)S(1)}, u32[]{:S(2)}, u32[]{:S(2)}) async-start(bf16[4,128,256]{2,1,0:T(8,128)(2,1)} %broadcast_in_dim.5), calls=%async_computation.3 | async-start | bytes 524288 | tf_op jit(solution)/shard_map/all_to_all | solution.py:198
  111.6 21.8 %collective-permute-start.13 = (bf16[512,384]{1,0:T(8,128)(2,1)S(1)}, bf16[512,384]{1,0:T(8,128)(2,1)S(1)}, u32[]{:S(2)}, u32[]{:S(2)}) collective-permute-start(bf16[512,384]{1,0:T(8,128)(2,1)S(1)} %add_convert_fusion.6), channel_id=1, source_target_pairs={{0,16},{8,24},{16,0},{24,8},{32,48},{40,56},{48,32},{56,40},{64,80... | collective-permute-start | bytes 1179656 | tf_op jit(solution)/shard_map/ppermute | solution.py:262
  116.3 17.5 %collective-permute-start.12 = (bf16[512,384]{1,0:T(8,128)(2,1)S(1)}, bf16[512,384]{1,0:T(8,128)(2,1)S(1)}, u32[]{:S(2)}, u32[]{:S(2)}) collective-permute-start(bf16[512,384]{1,0:T(8,128)(2,1)S(1)} %copy-done.16), channel_id=1, source_target_pairs={{0,8},{8,0},{16,24},{24,16},{32,40},{40,32},{48,56},{56,48},{64,72... | collective-permute-start | bytes 1179656 | tf_op jit(solution)/shard_map/ppermute | solution.py:262
  116.3 17.5 %collective-permute-start.14 = (bf16[512,384]{1,0:T(8,128)(2,1)S(1)}, bf16[512,384]{1,0:T(8,128)(2,1)S(1)}, u32[]{:S(2)}, u32[]{:S(2)}) collective-permute-start(bf16[512,384]{1,0:T(8,128)(2,1)S(1)} %copy-done.15), channel_id=1, source_target_pairs={{0,64},{8,72},{16,80},{24,88},{32,96},{40,104},{48,112},{56,120},{... | collective-permute-start | bytes 1179656 | tf_op jit(solution)/shard_map/ppermute | solution.py:262
  117.9 17.9 %collective-permute-start.15 = (bf16[512,384]{1,0:T(8,128)(2,1)S(1)}, bf16[512,384]{1,0:T(8,128)(2,1)S(1)}, u32[]{:S(2)}, u32[]{:S(2)}) collective-permute-start(bf16[512,384]{1,0:T(8,128)(2,1)S(1)} %copy-done.14), channel_id=1, source_target_pairs={{0,128},{8,136},{16,144},{24,152},{32,160},{40,168},{48,176},{56,1... | collective-permute-start | bytes 1179656 | tf_op jit(solution)/shard_map/ppermute | solution.py:262
  123.1 18.0 %all-to-all-start.4 = ((bf16[8,192,128]{2,1,0:T(8,128)(2,1)}), bf16[8,192,128]{2,1,0:T(8,128)(2,1)S(1)}, u32[]{:S(2)}, u32[]{:S(2)}) async-start(bf16[8,192,128]{2,1,0:T(8,128)(2,1)} %late.1), calls=%async_computation.5 | async-start | bytes 786432 | tf_op jit(solution)/shard_map/all_to_all | solution.py:400
  (16 other events, 162.8 us)
Sparse Core Ops, SparseCore 0:
  86.4 45.8 reduce-scatter.1

commit v6 on v5

--- a/solution.py
+++ b/solution.py
@@ -11,7 +11,7 @@
 GELU_CUBIC = 0.044715
 BF = jnp.bfloat16
 F32 = jnp.float32
-VMEM_LIMIT = 56 * 1024 * 1024
+VMEM_LIMIT = 16 * 1024 * 1024
 
 
 def gelu_parts(pre_act):
@@ -223,6 +223,10 @@
 def hid_columns():
     inner = hid_inner()
     return [list(range(i, lax.axis_size("hid"), inner)) for i in range(inner)]
+
+
+def in_hbm(value):
+    return pltpu.with_memory_space_constraint(value, pltpu.HBM)
 
 
 def fence(body, *operands):
@@ -321,13 +325,13 @@
         out_shape=[
             sds((rows, hidden), BF),
             sds((rows, hidden), BF),
-            sds((2 * rows, rank), BF),
+            pltpu.HBM((2 * rows, rank), BF),
         ]
-        + [sds(shape, BF) for shape in part_shapes],
+        + [pltpu.HBM(shape, BF) for shape in part_shapes],
         compiler_params=grid_params,
         cost_estimate=cost(4 * flops, 10 * 1024 * 1024),
         name="middle",
-    )(block_index, *fields, low, up_tiles, down_tiles, up_right, down_left)
+    )(block_index, *fields, low, *map(in_hbm, (up_tiles, down_tiles, up_right, down_left)))
     act, grad_pre, lowp = middle[:3]
     parts = list(middle[3:])
 
@@ -398,6 +402,7 @@
 
     moved = late(both, low2)
     moved = lax.all_to_all(moved, "tok", 0, 0, tiled=True)
+    x_two, grad_down_tiles, grad_up_tiles = tie((x_two, grad_down_tiles, grad_up_tiles))
     parts = (own, z_one, z_two, x_one, x_two)
     layer_out, grad_tokens = pl.pallas_call(
         functools.partial(final_kernel, len(parts)),
@@ -408,6 +413,7 @@
         cost_estimate=cost(4 * rows * feat * rank, 16 * rows * feat * 2),
         name="final",
     )(*parts, low2, down_right, up_left)
+    moved, layer_out = tie((moved, layer_out))
     grad_down_right, grad_up_left = pl.pallas_call(
         last_kernel,
         out_shape=(sds((rank // groups, feat), BF), sds((feat // groups, rank), BF)),

time: 154 us -> 149 us (0.968)
  Pallas kernels: 27.8 us -> 16.3 us
  local copies, waits for them, and re-layouts: 6.08 us -> 9.73 us
    pallas_call x1, Pallas kernels: 7.47 us -> 3.01 us  [on_device(): packed = grads(block_index, *fields, low, act, grad_pre)]
    unnamed x37 -> x25, local copies, waits for them, and re-layouts: 4.64 us -> 8.29 us
    all_to_all x1, waiting for transfers between devices: 1.74 us -> 4.76 us  [on_device(): moved = lax.all_to_all(moved, 'tok', 0, 0, tiled=True)]
    ppermute x10, waiting for transfers between devices: 7.29 us -> 4.63 us  [swap(): lax.ppermute(value, 'hid', [(i, i ^ distance) for i in range(hid_count)])]
    ppermute x6, starting transfers between devices: 19.1 us -> 21.4 us  [line_step(): other = lax.ppermute(held, 'hid', [(i, i ^ distance) for i in range(count)])]
    pallas_call x1, Pallas kernels: 2.77 us -> 1.12 us  [on_device(): pl.pallas_call(functools.partial(final_kernel, len(parts)), out_shape=(sd...]
  transfers between devices with their start and end apart: 22 -> 22, of which waited for: 13 -> 12; matrix products, arithmetic and copies ran while one was open for 2% -> 1% of each run, Pallas kernels for 9% -> 4%
where the time goes in v6:
time: 149 us; the launch traced here: 147 us
  starting transfers between devices  70.4 us (47%)
  waiting for transfers between devices  34.9 us (23%)
  Pallas kernels  16.3 us (11%)
  between operations  14.2 us (10%)
  local copies, waits for them, and re-layouts  9.73 us (7%)
    ppermute x6, starting transfers between devices, line_step(): other = lax.ppermute(held, 'hid', [(i, i ^ distance) for i in range(count)])  21.4 us
    ppermute x10, starting transfers between devices, swap(): lax.ppermute(value, 'hid', [(i, i ^ distance) for i in range(hid_count)])  20.9 us
    all_to_all x4, starting transfers between devices, group_exchange(): lax.all_to_all(pieces, 'hid', 0, 0, axis_index_groups=groups, tiled=True)  17.3 us
    ppermute x6, waiting for transfers between devices, line_step(): other = lax.ppermute(held, 'hid', [(i, i ^ distance) for i in range(count)])  17.2 us
    all_to_all x1, starting transfers between devices, on_device(): moved = lax.all_to_all(moved, 'tok', 0, 0, tiled=True)  10.8 us
    pallas_call x1, Pallas kernels, on_device(): pl.pallas_call(functools.partial(middle_kernel, levels), grid_spec=pltpu....  8.53 us
    unnamed x25, local copies, waits for them, and re-layouts  8.29 us
    all_to_all x4, waiting for transfers between devices, group_exchange(): lax.all_to_all(pieces, 'hid', 0, 0, axis_index_groups=groups, tiled=True)  8.16 us
  transfers between devices with their start and end apart: 22, of which 12 were waited for; matrix products, arithmetic and copies ran while one was open for 1% of the time, Pallas kernels for 4%

profile of v6, /device:TPU:1, one launch (start us, length us, event | category | flops | bytes accessed | tf_op | source)
XLA Modules:
  0.0 146.9 jit_solution(4961298257432406564)
XLA Ops:
  11.9 4.8 %all-to-all-start = ((bf16[4,128,256]{2,1,0:T(8,128)(2,1)}), bf16[4,128,256]{2,1,0:T(8,128)(2,1)S(1)}, u32[]{:S(2)}, u32[]{:S(2)}) async-start(bf16[4,128,256]{2,1,0:T(8,128)(2,1)} %bitcast), calls=%async_computation | async-start | bytes 524288 | tf_op jit(solution)/shard_map/all_to_all | solution.py:198
  16.7 3.0 %collective-permute-start.6 = (bf16[512,384]{1,0:T(8,128)(2,1)S(1)}, bf16[512,384]{1,0:T(8,128)(2,1)S(1)}, u32[]{:S(2)}, u32[]{:S(2)}) collective-permute-start(bf16[512,384]{1,0:T(8,128)(2,1)S(1)} %get-tuple-element.58.refs_0_.both_ref), channel_id=1, source_target_pairs={{0,16},{8,24},{16,0},{24,8},{32,48},{40,56},{48,32},{56,40},{64,80... | collective-permute-start | bytes 1179656 | tf_op jit(solution)/shard_map/ppermute | solution.py:266
  19.7 2.5 %all-to-all-done = bf16[4,128,256]{2,1,0:T(8,128)(2,1)S(1)} async-done(((bf16[4,128,256]{2,1,0:T(8,128)(2,1)}), bf16[4,128,256]{2,1,0:T(8,128)(2,1)S(1)}, u32[]{:S(2)}, u32[]{:S(2)}) %all-to-all-start) | async-done | bytes 262176 | tf_op jit(solution)/shard_map/all_to_all | solution.py:198
  23.9 22.6 %conditional.2 = (bf16[128,256]{1,0:T(8,128)(2,1)S(1)}) conditional(s32[]{:T(128)} %convert_element_type.71, () %tuple.27, bf16[128,256]{1,0:T(8,128)(2,1)S(1)} %reduce_sum.24), branch_computations={%region_1.0_spmd, %region_2.0_spmd} | conditional | flops 393216 | bytes 1376384 | solution.py:239
  23.9 6.0 %collective-permute-start = (bf16[128,256]{1,0:T(8,128)(2,1)S(1)}, bf16[128,256]{1,0:T(8,128)(2,1)S(1)}, u32[]{:S(2)}, u32[]{:S(2)}) collective-permute-start(bf16[128,256]{1,0:T(8,128)(2,1)S(1)} %param.1), channel_id=1, source_target_pairs={{0,48},{8,56},{16,32},{24,40},{32,16},{40,24},{48,0},{56,8},{64,11... | collective-permute-start | bytes 196616 | tf_op jit(solution)/shard_map/cond/branch_1_fun/ppermute | solution.py:215
  31.9 6.7 %collective-permute-start.1 = (bf16[128,256]{1,0:T(8,128)(2,1)S(1)}, bf16[128,256]{1,0:T(8,128)(2,1)S(1)}, u32[]{:S(2)}, u32[]{:S(2)}) collective-permute-start(bf16[128,256]{1,0:T(8,128)(2,1)S(1)} %add_convert_fusion.2), channel_id=1, source_target_pairs={{0,8},{8,0},{16,24},{24,16},{32,40},{40,32},{48,56},{56,48},{64,72... | collective-permute-start | bytes 196616 | tf_op jit(solution)/shard_map/cond/branch_1_fun/ppermute | solution.py:215
  40.6 3.5 %collective-permute-start.2 = (bf16[128,256]{1,0:T(8,128)(2,1)S(1)}, bf16[128,256]{1,0:T(8,128)(2,1)S(1)}, u32[]{:S(2)}, u32[]{:S(2)}) collective-permute-start(bf16[128,256]{1,0:T(8,128)(2,1)S(1)} %add_convert_fusion.1), channel_id=1, source_target_pairs={{0,16},{8,24},{16,0},{24,8},{32,48},{40,56},{48,32},{56,40},{64,80... | collective-permute-start | bytes 196616 | tf_op jit(solution)/shard_map/cond/branch_1_fun/ppermute | solution.py:215
  46.6 3.9 %collective-permute-start.10 = (bf16[512,384]{1,0:T(8,128)(2,1)S(1)}, bf16[512,384]{1,0:T(8,128)(2,1)S(1)}, u32[]{:S(2)}, u32[]{:S(2)}) collective-permute-start(bf16[512,384]{1,0:T(8,128)(2,1)S(1)} %collective-permute-done.6.refs_2_), channel_id=1, source_target_pairs={{0,48},{8,56},{16,32},{24,40},{32,16},{40,24},{48,0},{56,8},{64,11... | collective-permute-start | bytes 1179656 | tf_op jit(solution)/shard_map/ppermute | solution.py:266
  51.2 4.2 %all-to-all-start.1 = ((bf16[4,128,256]{2,1,0:T(8,128)(2,1)}), bf16[4,128,256]{2,1,0:T(8,128)(2,1)S(1)}, u32[]{:S(2)}, u32[]{:S(2)}) async-start(bf16[4,128,256]{2,1,0:T(8,128)(2,1)} %broadcast_in_dim.4), calls=%async_computation.1 | async-start | bytes 524288 | tf_op jit(solution)/shard_map/all_to_all | solution.py:198
  55.6 5.4 %all-to-all-done.1 = bf16[4,128,256]{2,1,0:T(8,128)(2,1)S(1)} async-done(((bf16[4,128,256]{2,1,0:T(8,128)(2,1)}), bf16[4,128,256]{2,1,0:T(8,128)(2,1)S(1)}, u32[]{:S(2)}, u32[]{:S(2)}) %all-to-all-start.1) | async-done | bytes 262176 | tf_op jit(solution)/shard_map/all_to_all | solution.py:198
  61.0 4.6 %collective-permute-done.10.refs_3_ = bf16[512,384]{1,0:T(8,128)(2,1)S(1)} collective-permute-done((bf16[512,384]{1,0:T(8,128)(2,1)S(1)}, bf16[512,384]{1,0:T(8,128)(2,1)S(1)}, u32[]{:S(2)}, u32[]{:S(2)}) %collective-permute-start.10) | collective-permute-done | bytes 393248 | tf_op jit(solution)/shard_map/ppermute | solution.py:266
  65.6 8.5 %middle.1 = (bf16[256,768]{1,0:T(8,128)(2,1)S(1)}, bf16[256,768]{1,0:T(8,128)(2,1)S(1)}, bf16[512,256]{1,0:T(8,128)(2,1)}, bf16[512,384]{1,0:T(8,128)(2,1)}, bf1...) custom-call(s32[6,3,2]{2,1,0:T(4,128)S(1)} %copy.17.index_ref, ...), custom_call_target="tpu_custom_call" | custom-call | flops 2818572288 | bytes 10485760 | tf_op jit(solution)/shard_map/middle/pallas_call | solution.py:300
  74.1 4.2 %all-to-all-start.2 = ((bf16[4,128,256]{2,1,0:T(8,128)(2,1)}), bf16[4,128,256]{2,1,0:T(8,128)(2,1)}, u32[]{:S(2)}, u32[]{:S(2)}) async-start(bf16[4,128,256]{2,1,0:T(8,128)(2,1)} %bitcast.12), calls=%async_computation.2 | async-start | bytes 524288 | tf_op jit(solution)/shard_map/all_to_all | solution.py:198
  78.4 3.0 %grads.1 = bf16[8,7,2,96,256]{4,3,2,1,0:T(8,128)(2,1)S(1)} custom-call(s32[6,3,2]{2,1,0:T(4,128)S(1)} %copy.17.index_ref, bf16[512,384]{1,0:T(8,128)(2,1)S(1)} %get-tuple-element.58.refs_0_.both_ref, bf16[512,384]{1,0:T(8,128)(2,1)S(1)} %collective-permute-done.9.refs_1_, bf16[512,384]{1,0:T(8,128)(2,1)S(1)} %collective-permute-done.6.refs_2_, ...), custom_call_target="tpu_custom_call" | custom-call | flops 1409286144 | bytes 10485760 | tf_op jit(solution)/shard_map/grads/pallas_call | solution.py:364
  86.0 3.5 %collective-permute-start.11 = (bf16[512,384]{1,0:T(8,128)(2,1)S(1)}, bf16[512,384]{1,0:T(8,128)(2,1)S(1)}, u32[]{:S(2)}, u32[]{:S(2)}) collective-permute-start(bf16[512,384]{1,0:T(8,128)(2,1)S(1)} %copy-done.11), channel_id=1, source_target_pairs={{0,48},{8,56},{16,32},{24,40},{32,16},{40,24},{48,0},{56,8},{64,11... | collective-permute-start | bytes 1179656 | tf_op jit(solution)/shard_map/ppermute | solution.py:266
  89.5 16.2 %conditional.3 = (bf16[128,256]{1,0:T(8,128)(2,1)S(1)}) conditional(s32[]{:T(128)} %convert_element_type.71, () %tuple.26, bf16[128,256]{1,0:T(8,128)(2,1)S(1)} %reduce_sum.25), branch_computations={%region_4.0_spmd, %region_5.0_spmd} | conditional | flops 393216 | bytes 1376384 | solution.py:239
  89.5 4.0 %collective-permute-done.3 = bf16[128,256]{1,0:T(8,128)(2,1)S(1)} collective-permute-done((bf16[128,256]{1,0:T(8,128)(2,1)S(1)}, bf16[128,256]{1,0:T(8,128)(2,1)S(1)}, u32[]{:S(2)}, u32[]{:S(2)}) %collective-permute-start.3) | collective-permute-done | bytes 65568 | tf_op jit(solution)/shard_map/cond/branch_1_fun/ppermute | solution.py:215
  93.6 4.5 %collective-permute-start.4 = (bf16[128,256]{1,0:T(8,128)(2,1)S(1)}, bf16[128,256]{1,0:T(8,128)(2,1)S(1)}, u32[]{:S(2)}, u32[]{:S(2)}) collective-permute-start(bf16[128,256]{1,0:T(8,128)(2,1)S(1)} %add_convert_fusion.5), channel_id=1, source_target_pairs={{0,8},{8,0},{16,24},{24,16},{32,40},{40,32},{48,56},{56,48},{64,72... | collective-permute-start | bytes 196616 | tf_op jit(solution)/shard_map/cond/branch_1_fun/ppermute | solution.py:215
  101.1 4.5 %collective-permute-done.5 = bf16[128,256]{1,0:T(8,128)(2,1)S(1)} collective-permute-done((bf16[128,256]{1,0:T(8,128)(2,1)S(1)}, bf16[128,256]{1,0:T(8,128)(2,1)S(1)}, u32[]{:S(2)}, u32[]{:S(2)}) %collective-permute-start.5) | collective-permute-done | bytes 65568 | tf_op jit(solution)/shard_map/cond/branch_1_fun/ppermute | solution.py:215
  106.5 4.0 %all-to-all-start.3 = ((bf16[4,128,256]{2,1,0:T(8,128)(2,1)}), bf16[4,128,256]{2,1,0:T(8,128)(2,1)S(1)}, u32[]{:S(2)}, u32[]{:S(2)}) async-start(bf16[4,128,256]{2,1,0:T(8,128)(2,1)} %broadcast_in_dim.5), calls=%async_computation.3 | async-start | bytes 524288 | tf_op jit(solution)/shard_map/all_to_all | solution.py:198
  112.5 3.0 %collective-permute-start.15 = (bf16[512,384]{1,0:T(8,128)(2,1)}, bf16[512,384]{1,0:T(8,128)(2,1)S(1)}, u32[]{:S(2)}, u32[]{:S(2)}) collective-permute-start(bf16[512,384]{1,0:T(8,128)(2,1)} %get-tuple-element.77), channel_id=1, source_target_pairs={{0,128},{8,136},{16,144},{24,152},{32,160},{40,168},{48,176},{56,1... | collective-permute-start | bytes 1179656 | tf_op jit(solution)/shard_map/ppermute | solution.py:266
  115.6 3.5 %collective-permute-start.13 = (bf16[512,384]{1,0:T(8,128)(2,1)S(1)}, bf16[512,384]{1,0:T(8,128)(2,1)S(1)}, u32[]{:S(2)}, u32[]{:S(2)}) collective-permute-start(bf16[512,384]{1,0:T(8,128)(2,1)S(1)} %add_convert_fusion.6), channel_id=1, source_target_pairs={{0,16},{8,24},{16,0},{24,8},{32,48},{40,56},{48,32},{56,40},{64,80... | collective-permute-start | bytes 1179656 | tf_op jit(solution)/shard_map/ppermute | solution.py:266
  120.4 10.8 %all-to-all-start.4 = ((bf16[8,192,128]{2,1,0:T(8,128)(2,1)}), bf16[8,192,128]{2,1,0:T(8,128)(2,1)S(1)}, u32[]{:S(2)}, u32[]{:S(2)}) async-start(bf16[8,192,128]{2,1,0:T(8,128)(2,1)} %late.1), calls=%async_computation.4 | async-start | bytes 786432 | tf_op jit(solution)/shard_map/all_to_all | solution.py:404
  134.6 4.8 %all-to-all-done.4.late_ref = bf16[8,192,128]{2,1,0:T(8,128)(2,1)S(1)} async-done(((bf16[8,192,128]{2,1,0:T(8,128)(2,1)}), bf16[8,192,128]{2,1,0:T(8,128)(2,1)S(1)}, u32[]{:S(2)}, u32[]{:S(2)}) %all-to-all-start.4) | async-done | bytes 393248 | tf_op jit(solution)/shard_map/all_to_all | solution.py:404
  (66 shorter events, 29.6 us)
Async XLA Ops:
  10.9 44.6 %copy-start.10 = (s32[6,3,2]{0,2,1:T(2,128)S(1)}, s32[6,3,2]{0,2,1:T(2,128)}, u32[]{:S(2)}) copy-start(s32[6,3,2]{0,2,1:T(2,128)} %param.17) | copy-start | bytes 436
  11.9 10.4 %all-to-all-start = ((bf16[4,128,256]{2,1,0:T(8,128)(2,1)}), bf16[4,128,256]{2,1,0:T(8,128)(2,1)S(1)}, u32[]{:S(2)}, u32[]{:S(2)}) async-start(bf16[4,128,256]{2,1,0:T(8,128)(2,1)} %bitcast), calls=%async_computation | async-start | bytes 524288 | tf_op jit(solution)/shard_map/all_to_all | solution.py:198
  16.7 29.7 %collective-permute-start.6 = (bf16[512,384]{1,0:T(8,128)(2,1)S(1)}, bf16[512,384]{1,0:T(8,128)(2,1)S(1)}, u32[]{:S(2)}, u32[]{:S(2)}) collective-permute-start(bf16[512,384]{1,0:T(8,128)(2,1)S(1)} %get-tuple-element.58.refs_0_.both_ref), channel_id=1, source_target_pairs={{0,16},{8,24},{16,0},{24,8},{32,48},{40,56},{48,32},{56,40},{64,80... | collective-permute-start | bytes 1179656 | tf_op jit(solution)/shard_map/ppermute | solution.py:266
  22.3 24.2 %collective-permute-start.8 = (bf16[512,384]{1,0:T(8,128)(2,1)S(1)}, bf16[512,384]{1,0:T(8,128)(2,1)S(1)}, u32[]{:S(2)}, u32[]{:S(2)}) collective-permute-start(bf16[512,384]{1,0:T(8,128)(2,1)S(1)} %get-tuple-element.58.refs_0_.both_ref), channel_id=1, source_target_pairs={{0,128},{8,136},{16,144},{24,152},{32,160},{40,168},{48,176},{56,1... | collective-permute-start | bytes 1179656 | tf_op jit(solution)/shard_map/ppermute | solution.py:266
  22.8 23.7 %collective-permute-start.7 = (bf16[512,384]{1,0:T(8,128)(2,1)S(1)}, bf16[512,384]{1,0:T(8,128)(2,1)S(1)}, u32[]{:S(2)}, u32[]{:S(2)}) collective-permute-start(bf16[512,384]{1,0:T(8,128)(2,1)S(1)} %get-tuple-element.58.refs_0_.both_ref), channel_id=1, source_target_pairs={{0,64},{8,72},{16,80},{24,88},{32,96},{40,104},{48,112},{56,120},{... | collective-permute-start | bytes 1179656 | tf_op jit(solution)/shard_map/ppermute | solution.py:266
  23.9 7.9 %collective-permute-start = (bf16[128,256]{1,0:T(8,128)(2,1)S(1)}, bf16[128,256]{1,0:T(8,128)(2,1)S(1)}, u32[]{:S(2)}, u32[]{:S(2)}) collective-permute-start(bf16[128,256]{1,0:T(8,128)(2,1)S(1)} %param.1), channel_id=1, source_target_pairs={{0,48},{8,56},{16,32},{24,40},{32,16},{40,24},{48,0},{56,8},{64,11... | collective-permute-start | bytes 196616 | tf_op jit(solution)/shard_map/cond/branch_1_fun/ppermute | solution.py:215
  31.9 8.7 %collective-permute-start.1 = (bf16[128,256]{1,0:T(8,128)(2,1)S(1)}, bf16[128,256]{1,0:T(8,128)(2,1)S(1)}, u32[]{:S(2)}, u32[]{:S(2)}) collective-permute-start(bf16[128,256]{1,0:T(8,128)(2,1)S(1)} %add_convert_fusion.2), channel_id=1, source_target_pairs={{0,8},{8,0},{16,24},{24,16},{32,40},{40,32},{48,56},{56,48},{64,72... | collective-permute-start | bytes 196616 | tf_op jit(solution)/shard_map/cond/branch_1_fun/ppermute | solution.py:215
  40.6 5.9 %collective-permute-start.2 = (bf16[128,256]{1,0:T(8,128)(2,1)S(1)}, bf16[128,256]{1,0:T(8,128)(2,1)S(1)}, u32[]{:S(2)}, u32[]{:S(2)}) collective-permute-start(bf16[128,256]{1,0:T(8,128)(2,1)S(1)} %add_convert_fusion.1), channel_id=1, source_target_pairs={{0,16},{8,24},{16,0},{24,8},{32,48},{40,56},{48,32},{56,40},{64,80... | collective-permute-start | bytes 196616 | tf_op jit(solution)/shard_map/cond/branch_1_fun/ppermute | solution.py:215
  46.5 14.5 %collective-permute-start.9 = (bf16[512,384]{1,0:T(8,128)(2,1)S(1)}, bf16[512,384]{1,0:T(8,128)(2,1)S(1)}, u32[]{:S(2)}, u32[]{:S(2)}) collective-permute-start(bf16[512,384]{1,0:T(8,128)(2,1)S(1)} %get-tuple-element.58.refs_0_.both_ref), channel_id=1, source_target_pairs={{0,8},{8,0},{16,24},{24,16},{32,40},{40,32},{48,56},{56,48},{64,72... | collective-permute-start | bytes 1179656 | tf_op jit(solution)/shard_map/ppermute | solution.py:266
  46.6 19.0 %collective-permute-start.10 = (bf16[512,384]{1,0:T(8,128)(2,1)S(1)}, bf16[512,384]{1,0:T(8,128)(2,1)S(1)}, u32[]{:S(2)}, u32[]{:S(2)}) collective-permute-start(bf16[512,384]{1,0:T(8,128)(2,1)S(1)} %collective-permute-done.6.refs_2_), channel_id=1, source_target_pairs={{0,48},{8,56},{16,32},{24,40},{32,16},{40,24},{48,0},{56,8},{64,11... | collective-permute-start | bytes 1179656 | tf_op jit(solution)/shard_map/ppermute | solution.py:266
  51.2 9.8 %all-to-all-start.1 = ((bf16[4,128,256]{2,1,0:T(8,128)(2,1)}), bf16[4,128,256]{2,1,0:T(8,128)(2,1)S(1)}, u32[]{:S(2)}, u32[]{:S(2)}) async-start(bf16[4,128,256]{2,1,0:T(8,128)(2,1)} %broadcast_in_dim.4), calls=%async_computation.1 | async-start | bytes 524288 | tf_op jit(solution)/shard_map/all_to_all | solution.py:198
  74.1 9.9 %all-to-all-start.2 = ((bf16[4,128,256]{2,1,0:T(8,128)(2,1)}), bf16[4,128,256]{2,1,0:T(8,128)(2,1)}, u32[]{:S(2)}, u32[]{:S(2)}) async-start(bf16[4,128,256]{2,1,0:T(8,128)(2,1)} %bitcast.12), calls=%async_computation.2 | async-start | bytes 524288 | tf_op jit(solution)/shard_map/all_to_all | solution.py:198
  78.4 53.1 %reduce-scatter.2.cloned.1.call-start = ((), (), s32[]{:S(2)}) async-start(), calls=%async_computation.6 | async-start | bytes 6193152 | tf_op jit(solution)/shard_map/reduce_scatter | solution.py:374
  85.0 30.5 %copy-start.9 = (bf16[512,384]{1,0:T(8,128)(2,1)S(1)}, bf16[512,384]{1,0:T(8,128)(2,1)}, u32[]{:S(2)}) copy-start(bf16[512,384]{1,0:T(8,128)(2,1)} %get-tuple-element.74) | copy-start | bytes 1179652
  86.0 19.8 %collective-permute-start.11 = (bf16[512,384]{1,0:T(8,128)(2,1)S(1)}, bf16[512,384]{1,0:T(8,128)(2,1)S(1)}, u32[]{:S(2)}, u32[]{:S(2)}) collective-permute-start(bf16[512,384]{1,0:T(8,128)(2,1)S(1)} %copy-done.11), channel_id=1, source_target_pairs={{0,48},{8,56},{16,32},{24,40},{32,16},{40,24},{48,0},{56,8},{64,11... | collective-permute-start | bytes 1179656 | tf_op jit(solution)/shard_map/ppermute | solution.py:266
  89.5 4.0 %collective-permute-start.3 = (bf16[128,256]{1,0:T(8,128)(2,1)S(1)}, bf16[128,256]{1,0:T(8,128)(2,1)S(1)}, u32[]{:S(2)}, u32[]{:S(2)}) collective-permute-start(bf16[128,256]{1,0:T(8,128)(2,1)S(1)} %param.3), channel_id=1, source_target_pairs={{0,16},{8,24},{16,0},{24,8},{32,48},{40,56},{48,32},{56,40},{64,80... | collective-permute-start | bytes 196616 | tf_op jit(solution)/shard_map/cond/branch_1_fun/ppermute | solution.py:215
  93.6 6.8 %collective-permute-start.4 = (bf16[128,256]{1,0:T(8,128)(2,1)S(1)}, bf16[128,256]{1,0:T(8,128)(2,1)S(1)}, u32[]{:S(2)}, u32[]{:S(2)}) collective-permute-start(bf16[128,256]{1,0:T(8,128)(2,1)S(1)} %add_convert_fusion.5), channel_id=1, source_target_pairs={{0,8},{8,0},{16,24},{24,16},{32,40},{40,32},{48,56},{56,48},{64,72... | collective-permute-start | bytes 196616 | tf_op jit(solution)/shard_map/cond/branch_1_fun/ppermute | solution.py:215
  100.4 5.3 %collective-permute-start.5 = (bf16[128,256]{1,0:T(8,128)(2,1)S(1)}, bf16[128,256]{1,0:T(8,128)(2,1)S(1)}, u32[]{:S(2)}, u32[]{:S(2)}) collective-permute-start(bf16[128,256]{1,0:T(8,128)(2,1)S(1)} %add_convert_fusion.4), channel_id=1, source_target_pairs={{0,48},{8,56},{16,32},{24,40},{32,16},{40,24},{48,0},{56,8},{64,11... | collective-permute-start | bytes 196616 | tf_op jit(solution)/shard_map/cond/branch_1_fun/ppermute | solution.py:215
  106.5 12.9 %all-to-all-start.3 = ((bf16[4,128,256]{2,1,0:T(8,128)(2,1)}), bf16[4,128,256]{2,1,0:T(8,128)(2,1)S(1)}, u32[]{:S(2)}, u32[]{:S(2)}) async-start(bf16[4,128,256]{2,1,0:T(8,128)(2,1)} %broadcast_in_dim.5), calls=%async_computation.3 | async-start | bytes 524288 | tf_op jit(solution)/shard_map/all_to_all | solution.py:198
  110.4 23.0 %collective-permute-start.12 = (bf16[512,384]{1,0:T(8,128)(2,1)}, bf16[512,384]{1,0:T(8,128)(2,1)S(1)}, u32[]{:S(2)}, u32[]{:S(2)}) collective-permute-start(bf16[512,384]{1,0:T(8,128)(2,1)} %get-tuple-element.73), channel_id=1, source_target_pairs={{0,8},{8,0},{16,24},{24,16},{32,40},{40,32},{48,56},{56,48},{64,72... | collective-permute-start | bytes 1179656 | tf_op jit(solution)/shard_map/ppermute | solution.py:266
  112.5 20.9 %collective-permute-start.15 = (bf16[512,384]{1,0:T(8,128)(2,1)}, bf16[512,384]{1,0:T(8,128)(2,1)S(1)}, u32[]{:S(2)}, u32[]{:S(2)}) collective-permute-start(bf16[512,384]{1,0:T(8,128)(2,1)} %get-tuple-element.77), channel_id=1, source_target_pairs={{0,128},{8,136},{16,144},{24,152},{32,160},{40,168},{48,176},{56,1... | collective-permute-start | bytes 1179656 | tf_op jit(solution)/shard_map/ppermute | solution.py:266
  115.6 17.9 %collective-permute-start.13 = (bf16[512,384]{1,0:T(8,128)(2,1)S(1)}, bf16[512,384]{1,0:T(8,128)(2,1)S(1)}, u32[]{:S(2)}, u32[]{:S(2)}) collective-permute-start(bf16[512,384]{1,0:T(8,128)(2,1)S(1)} %add_convert_fusion.6), channel_id=1, source_target_pairs={{0,16},{8,24},{16,0},{24,8},{32,48},{40,56},{48,32},{56,40},{64,80... | collective-permute-start | bytes 1179656 | tf_op jit(solution)/shard_map/ppermute | solution.py:266
  119.0 14.4 %collective-permute-start.14 = (bf16[512,384]{1,0:T(8,128)(2,1)}, bf16[512,384]{1,0:T(8,128)(2,1)S(1)}, u32[]{:S(2)}, u32[]{:S(2)}) collective-permute-start(bf16[512,384]{1,0:T(8,128)(2,1)} %get-tuple-element.76), channel_id=1, source_target_pairs={{0,64},{8,72},{16,80},{24,88},{32,96},{40,104},{48,112},{56,120},{... | collective-permute-start | bytes 1179656 | tf_op jit(solution)/shard_map/ppermute | solution.py:266
  120.4 18.9 %all-to-all-start.4 = ((bf16[8,192,128]{2,1,0:T(8,128)(2,1)}), bf16[8,192,128]{2,1,0:T(8,128)(2,1)S(1)}, u32[]{:S(2)}, u32[]{:S(2)}) async-start(bf16[8,192,128]{2,1,0:T(8,128)(2,1)} %late.1), calls=%async_computation.4 | async-start | bytes 786432 | tf_op jit(solution)/shard_map/all_to_all | solution.py:404
  (10 other events, 91.4 us)
Sparse Core Ops, SparseCore 0:
  85.1 46.2 reduce-scatter.1

commit v7 on v6

--- a/solution.py
+++ b/solution.py
@@ -144,7 +144,9 @@
         right_ref[:, columns] = sum_ref[levels, 1, b * piece : (b + 1) * piece]
 
 
-def late_kernel(groups, both_ref, low_ref, out_ref):
+def late_kernel(groups, both_ref, *refs):
+    *pieces, out_ref, low_ref = refs
+    assemble(low_ref, pieces)
     rows = low_ref.shape[0] // 2
     right = dot_tn(low_ref[:rows], both_ref[rows:]).astype(BF)
     left = dot_tn(both_ref[:rows], low_ref[rows:]).astype(BF)
@@ -198,16 +200,36 @@
     return lax.all_to_all(pieces, "hid", 0, 0, axis_index_groups=groups, tiled=True)
 
 
-def group_scatter(value, groups):
+def group_scatter(value, groups, beside=None):
     count = len(groups[0])
     pieces = value.reshape(count, value.shape[0] // count, value.shape[1])
-    return jnp.sum(group_exchange(pieces, groups).astype(F32), axis=0).astype(BF)
+    pieces = group_exchange(pieces, groups)
+    if beside is not None:
+        pieces, beside = lax.optimization_barrier((pieces, beside))
+    return jnp.sum(pieces.astype(F32), axis=0).astype(BF), beside
 
 
 def group_gather(value, groups):
     count = len(groups[0])
     pieces = jnp.broadcast_to(value[None], (count,) + value.shape)
     return group_exchange(pieces, groups).reshape(count * value.shape[0], value.shape[1])
+
+
+def outer_shift(value, step):
+    count, inner = lax.axis_size("hid"), hid_inner()
+    return lax.ppermute(value, "hid", [(i, (i + step * inner) % count) for i in range(count)])
+
+
+def outer_pieces(value):
+    return [value] + [outer_shift(value, d) for d in range(1, len(hid_columns()[0]))]
+
+
+def assemble(out_ref, piece_refs):
+    count, tall = len(piece_refs), piece_refs[0].shape[0]
+    place = lax.axis_index("hid") // hid_inner()
+    for d, ref in enumerate(piece_refs):
+        first = pl.multiple_of(lax.rem(place + count - d, count) * tall, tall)
+        out_ref[pl.ds(first, tall), :] = ref[...]
 
 
 def line_step(held, distance):
@@ -277,12 +299,12 @@
         name="head",
     )(tokens, cotangent, up_left, down_right)
     z_two = swap(both, 2)
-    total = group_scatter(low_part, columns)
+    total, _ = group_scatter(low_part, columns)
     total, both_x = tie((total, both))
     x_one = swap(both_x, 8)
     x_two = swap(both_x, 16)
     total, z_two, x_one, x_two, both_z = tie(
-        (line_sum(total, (6, 1, 2)), z_two, x_one, x_two, both)
+        (line_sum(total, (1, 6, 2)), z_two, x_one, x_two, both)
     )
     z_four = swap(z_two, 6)
     z_one = swap(both_z, 1)
@@ -360,14 +382,13 @@
     own, z_one, z_two, z_four, x_one, x_two = parts
     z_four = swap(z_four, 6)
 
-    total = group_scatter(lowp, columns)
     packed = grads(block_index, *fields, low, act, grad_pre)
-    total, packed = tie((total, packed))
+    total, packed = group_scatter(lowp, columns, packed)
     total, z_four, x_one, x_two, z_one = tie(
         (line_sum(total, (2, 1, 6)), z_four, x_one, x_two, z_one)
     )
     z_two = swap((z_two.astype(F32) + z_four.astype(F32)).astype(BF), 2)
-    low2 = group_gather(total, columns)
+    low_pieces = outer_pieces(total)
     x_one = swap(x_one, 8)
     x_two = swap(x_two, 16)
     z_one = swap(z_one, 1)
@@ -392,15 +413,15 @@
     late_rows = (rank // groups) * (feat // 128) + (feat // groups) * (rank // 128)
     late = pl.pallas_call(
         functools.partial(late_kernel, groups),
-        out_shape=sds((groups, late_rows, 128), BF),
-        in_specs=[vmem_spec()] * 2,
-        out_specs=vmem_spec(),
+        out_shape=(sds((groups, late_rows, 128), BF), sds((2 * rows, rank), BF)),
+        in_specs=[vmem_spec()] * (1 + len(low_pieces)),
+        out_specs=(vmem_spec(),) * 2,
         compiler_params=params(),
         cost_estimate=cost(4 * rows * feat * rank, 4 * rows * feat * 2),
         name="late",
     )
 
-    moved = late(both, low2)
+    moved, low2 = late(both, *low_pieces)
     moved = lax.all_to_all(moved, "tok", 0, 0, tiled=True)
     x_two, grad_down_tiles, grad_up_tiles = tie((x_two, grad_down_tiles, grad_up_tiles))
     parts = (own, z_one, z_two, x_one, x_two)

time: 149 us -> 146 us (0.980)
  starting transfers between devices: 70.4 us -> 60.1 us
  waiting for transfers between devices: 34.9 us -> 43.4 us
    ppermute x6, waiting for transfers between devices: 17.2 us -> 26.2 us  [line_step(): other = lax.ppermute(held, 'hid', [(i, i ^ distance) for i in range(count)])]
    ppermute x10, starting transfers between devices: 20.9 us -> 13.1 us  [swap(): lax.ppermute(value, 'hid', [(i, i ^ distance) for i in range(hid_count)])]
    ppermute x6, starting transfers between devices: 21.4 us -> 16.4 us  [line_step(): other = lax.ppermute(held, 'hid', [(i, i ^ distance) for i in range(count)])]
    ppermute x10, waiting for transfers between devices: 4.63 us -> 0.03 us  [swap(): lax.ppermute(value, 'hid', [(i, i ^ distance) for i in range(hid_count)])]
    ppermute x0 -> x3, starting transfers between devices: none -> 4.41 us  [outer_shift(): lax.ppermute(value, 'hid', [(i, (i + step * inner) % count) for i in rang...]
    ppermute x0 -> x3, waiting for transfers between devices: none -> 4.02 us  [outer_shift(): lax.ppermute(value, 'hid', [(i, (i + step * inner) % count) for i in rang...]
    all_to_all x1, starting transfers between devices: 10.8 us -> 9.13 us  [on_device(): moved = lax.all_to_all(moved, 'tok', 0, 0, tiled=True)]
    all_to_all x4 -> x3, starting transfers between devices: 17.3 us -> 17 us  [group_exchange(): lax.all_to_all(pieces, 'hid', 0, 0, axis_index_groups=groups, tiled=True)]
  transfers between devices with their start and end apart: 22 -> 24, of which waited for: 12 -> 12; matrix products, arithmetic and copies ran while one was open for 1% -> 1% of each run, Pallas kernels for 4% -> 4%
where the time goes in v7:
time: 146 us; the launch traced here: 144 us
  starting transfers between devices  60.1 us (41%)
  waiting for transfers between devices  43.4 us (30%)
  Pallas kernels  16.4 us (11%)
  between operations  14.2 us (10%)
  local copies, waits for them, and re-layouts  8.98 us (6%)
    ppermute x6, waiting for transfers between devices, line_step(): other = lax.ppermute(held, 'hid', [(i, i ^ distance) for i in range(count)])  26.2 us
    all_to_all x3, starting transfers between devices, group_exchange(): lax.all_to_all(pieces, 'hid', 0, 0, axis_index_groups=groups, tiled=True)  17 us
    ppermute x6, starting transfers between devices, line_step(): other = lax.ppermute(held, 'hid', [(i, i ^ distance) for i in range(count)])  16.4 us
    ppermute x10, starting transfers between devices, swap(): lax.ppermute(value, 'hid', [(i, i ^ distance) for i in range(hid_count)])  13.1 us
    all_to_all x1, starting transfers between devices, on_device(): moved = lax.all_to_all(moved, 'tok', 0, 0, tiled=True)  9.13 us
    pallas_call x1, Pallas kernels, on_device(): pl.pallas_call(functools.partial(middle_kernel, levels), grid_spec=pltpu....  8.56 us
    unnamed x25, local copies, waits for them, and re-layouts  8.26 us
    all_to_all x3, waiting for transfers between devices, group_exchange(): lax.all_to_all(pieces, 'hid', 0, 0, axis_index_groups=groups, tiled=True)  8.2 us
  transfers between devices with their start and end apart: 24, of which 12 were waited for; matrix products, arithmetic and copies ran while one was open for 1% of the time, Pallas kernels for 4%

profile of v7, /device:TPU:1, one launch (start us, length us, event | category | flops | bytes accessed | tf_op | source)
XLA Modules:
  0.0 144.3 jit_solution(7503835245961899128)
XLA Ops:
  11.9 4.8 %all-to-all-start = ((bf16[4,128,256]{2,1,0:T(8,128)(2,1)}), bf16[4,128,256]{2,1,0:T(8,128)(2,1)S(1)}, u32[]{:S(2)}, u32[]{:S(2)}) async-start(bf16[4,128,256]{2,1,0:T(8,128)(2,1)} %bitcast), calls=%async_computation | async-start | bytes 524288 | tf_op jit(solution)/shard_map/all_to_all | solution.py:200
  16.7 3.0 %collective-permute-start.6 = (bf16[512,384]{1,0:T(8,128)(2,1)S(1)}, bf16[512,384]{1,0:T(8,128)(2,1)S(1)}, u32[]{:S(2)}, u32[]{:S(2)}) collective-permute-start(bf16[512,384]{1,0:T(8,128)(2,1)S(1)} %get-tuple-element.62.refs_0_.both_ref), channel_id=1, source_target_pairs={{0,16},{8,24},{16,0},{24,8},{32,48},{40,56},{48,32},{56,40},{64,80... | collective-permute-start | bytes 1179656 | tf_op jit(solution)/shard_map/ppermute | solution.py:288
  19.7 2.5 %all-to-all-done = bf16[4,128,256]{2,1,0:T(8,128)(2,1)S(1)} async-done(((bf16[4,128,256]{2,1,0:T(8,128)(2,1)}), bf16[4,128,256]{2,1,0:T(8,128)(2,1)S(1)}, u32[]{:S(2)}, u32[]{:S(2)}) %all-to-all-start) | async-done | bytes 262176 | tf_op jit(solution)/shard_map/all_to_all | solution.py:200
  23.9 23.7 %conditional.2 = (bf16[128,256]{1,0:T(8,128)(2,1)S(1)}) conditional(s32[]{:T(128)} %convert_element_type.73, () %tuple.27, bf16[128,256]{1,0:T(8,128)(2,1)S(1)} %reduce_sum.24), branch_computations={%region_1.0_spmd, %region_2.0_spmd} | conditional | flops 393216 | bytes 1376384 | solution.py:261
  25.5 3.1 %collective-permute-done = bf16[128,256]{1,0:T(8,128)(2,1)S(1)} collective-permute-done((bf16[128,256]{1,0:T(8,128)(2,1)S(1)}, bf16[128,256]{1,0:T(8,128)(2,1)S(1)}, u32[]{:S(2)}, u32[]{:S(2)}) %collective-permute-start) | collective-permute-done | bytes 65568 | tf_op jit(solution)/shard_map/cond/branch_1_fun/ppermute | solution.py:237
  28.7 5.8 %collective-permute-start.1 = (bf16[128,256]{1,0:T(8,128)(2,1)S(1)}, bf16[128,256]{1,0:T(8,128)(2,1)S(1)}, u32[]{:S(2)}, u32[]{:S(2)}) collective-permute-start(bf16[128,256]{1,0:T(8,128)(2,1)S(1)} %add_convert_fusion.2), channel_id=1, source_target_pairs={{0,48},{8,56},{16,32},{24,40},{32,16},{40,24},{48,0},{56,8},{64,11... | collective-permute-start | bytes 196616 | tf_op jit(solution)/shard_map/cond/branch_1_fun/ppermute | solution.py:237
  34.5 8.9 %collective-permute-done.1 = bf16[128,256]{1,0:T(8,128)(2,1)S(1)} collective-permute-done((bf16[128,256]{1,0:T(8,128)(2,1)S(1)}, bf16[128,256]{1,0:T(8,128)(2,1)S(1)}, u32[]{:S(2)}, u32[]{:S(2)}) %collective-permute-start.1) | collective-permute-done | bytes 65568 | tf_op jit(solution)/shard_map/cond/branch_1_fun/ppermute | solution.py:237
  43.5 4.1 %collective-permute-done.2 = bf16[128,256]{1,0:T(8,128)(2,1)S(1)} collective-permute-done((bf16[128,256]{1,0:T(8,128)(2,1)S(1)}, bf16[128,256]{1,0:T(8,128)(2,1)S(1)}, u32[]{:S(2)}, u32[]{:S(2)}) %collective-permute-start.2) | collective-permute-done | bytes 65568 | tf_op jit(solution)/shard_map/cond/branch_1_fun/ppermute | solution.py:237
  48.7 4.5 %all-to-all-start.1 = ((bf16[4,128,256]{2,1,0:T(8,128)(2,1)}), bf16[4,128,256]{2,1,0:T(8,128)(2,1)S(1)}, u32[]{:S(2)}, u32[]{:S(2)}) async-start(bf16[4,128,256]{2,1,0:T(8,128)(2,1)} %broadcast_in_dim.2), calls=%async_computation.1 | async-start | bytes 524288 | tf_op jit(solution)/shard_map/all_to_all | solution.py:200
  53.2 5.4 %all-to-all-done.1 = bf16[4,128,256]{2,1,0:T(8,128)(2,1)S(1)} async-done(((bf16[4,128,256]{2,1,0:T(8,128)(2,1)}), bf16[4,128,256]{2,1,0:T(8,128)(2,1)S(1)}, u32[]{:S(2)}, u32[]{:S(2)}) %all-to-all-start.1) | async-done | bytes 262176 | tf_op jit(solution)/shard_map/all_to_all | solution.py:200
  58.7 8.6 %middle.1 = (bf16[256,768]{1,0:T(8,128)(2,1)S(1)}, bf16[256,768]{1,0:T(8,128)(2,1)S(1)}, bf16[512,256]{1,0:T(8,128)(2,1)}, bf16[512,384]{1,0:T(8,128)(2,1)}, bf1...) custom-call(s32[6,3,2]{2,1,0:T(4,128)S(1)} %copy.17.index_ref, ...), custom_call_target="tpu_custom_call" | custom-call | flops 2818572288 | bytes 10485760 | tf_op jit(solution)/shard_map/middle/pallas_call | solution.py:322
  67.2 7.7 %all-to-all-start.2 = ((bf16[4,128,256]{2,1,0:T(8,128)(2,1)}), bf16[4,128,256]{2,1,0:T(8,128)(2,1)}, u32[]{:S(2)}, u32[]{:S(2)}) async-start(bf16[4,128,256]{2,1,0:T(8,128)(2,1)} %bitcast.9), calls=%async_computation.2 | async-start | bytes 524288 | tf_op jit(solution)/shard_map/all_to_all | solution.py:200
  74.9 3.0 %grads.1 = bf16[8,7,2,96,256]{4,3,2,1,0:T(8,128)(2,1)S(1)} custom-call(s32[6,3,2]{2,1,0:T(4,128)S(1)} %copy.17.index_ref, bf16[512,384]{1,0:T(8,128)(2,1)S(1)} %get-tuple-element.62.refs_0_.both_ref, bf16[512,384]{1,0:T(8,128)(2,1)S(1)} %collective-permute-done.9.refs_1_, bf16[512,384]{1,0:T(8,128)(2,1)S(1)} %collective-permute-done.6.refs_2_, ...), custom_call_target="tpu_custom_call" | custom-call | flops 1409286144 | bytes 10485760 | tf_op jit(solution)/shard_map/grads/pallas_call | solution.py:385
  77.9 2.4 %copy-done = bf16[8,7,2,96,256]{4,3,2,1,0:T(8,128)(2,1)} copy-done((bf16[8,7,2,96,256]{4,3,2,1,0:T(8,128)(2,1)}, bf16[8,7,2,96,256]{4,3,2,1,0:T(8,128)(2,1)S(1)}, u32[]{:S(2)}) %copy-start) | copy-done | bytes 5505048
  81.5 3.4 %collective-permute-start.11 = (bf16[512,384]{1,0:T(8,128)(2,1)S(1)}, bf16[512,384]{1,0:T(8,128)(2,1)S(1)}, u32[]{:S(2)}, u32[]{:S(2)}) collective-permute-start(bf16[512,384]{1,0:T(8,128)(2,1)S(1)} %copy-done.11), channel_id=1, source_target_pairs={{0,48},{8,56},{16,32},{24,40},{32,16},{40,24},{48,0},{56,8},{64,11... | collective-permute-start | bytes 1179656 | tf_op jit(solution)/shard_map/ppermute | solution.py:288
  85.0 20.1 %conditional.3 = (bf16[128,256]{1,0:T(8,128)(2,1)S(1)}) conditional(s32[]{:T(128)} %convert_element_type.73, () %tuple.26, bf16[4,128,256]{2,1,0:T(8,128)(2,1)} %all-to-all-done.2), branch_computations={%region_3.0_spmd, %region_4.6_spmd} | conditional | flops 491520 | bytes 1704066 | solution.py:261
  86.0 2.4 %collective-permute-start.3 = (bf16[128,256]{1,0:T(8,128)(2,1)S(1)}, bf16[128,256]{1,0:T(8,128)(2,1)S(1)}, u32[]{:S(2)}, u32[]{:S(2)}) collective-permute-start(bf16[128,256]{1,0:T(8,128)(2,1)S(1)} %reduce_sum.22), channel_id=1, source_target_pairs={{0,16},{8,24},{16,0},{24,8},{32,48},{40,56},{48,32},{56,40},{64,80... | collective-permute-start | bytes 196616 | tf_op jit(solution)/shard_map/cond/branch_1_fun/ppermute | solution.py:237
  90.5 6.4 %collective-permute-start.4 = (bf16[128,256]{1,0:T(8,128)(2,1)S(1)}, bf16[128,256]{1,0:T(8,128)(2,1)S(1)}, u32[]{:S(2)}, u32[]{:S(2)}) collective-permute-start(bf16[128,256]{1,0:T(8,128)(2,1)S(1)} %add_convert_fusion.5), channel_id=1, source_target_pairs={{0,8},{8,0},{16,24},{24,16},{32,40},{40,32},{48,56},{56,48},{64,72... | collective-permute-start | bytes 196616 | tf_op jit(solution)/shard_map/cond/branch_1_fun/ppermute | solution.py:237
  96.9 2.7 %collective-permute-done.4 = bf16[128,256]{1,0:T(8,128)(2,1)S(1)} collective-permute-done((bf16[128,256]{1,0:T(8,128)(2,1)S(1)}, bf16[128,256]{1,0:T(8,128)(2,1)S(1)}, u32[]{:S(2)}, u32[]{:S(2)}) %collective-permute-start.4) | collective-permute-done | bytes 65568 | tf_op jit(solution)/shard_map/cond/branch_1_fun/ppermute | solution.py:237
  99.7 5.3 %collective-permute-done.5 = bf16[128,256]{1,0:T(8,128)(2,1)S(1)} collective-permute-done((bf16[128,256]{1,0:T(8,128)(2,1)S(1)}, bf16[128,256]{1,0:T(8,128)(2,1)S(1)}, u32[]{:S(2)}, u32[]{:S(2)}) %collective-permute-start.5) | collective-permute-done | bytes 65568 | tf_op jit(solution)/shard_map/cond/branch_1_fun/ppermute | solution.py:237
  105.1 2.6 %collective-permute-start.14 = (bf16[128,256]{1,0:T(8,128)(2,1)S(1)}, bf16[128,256]{1,0:T(8,128)(2,1)S(1)}, u32[]{:S(2)}, u32[]{:S(2)}) collective-permute-start(bf16[128,256]{1,0:T(8,128)(2,1)S(1)} %get-tuple-element.99.refs_0_), channel_id=1, source_target_pairs={{0,192},{8,200},{16,208},{24,216},{32,224},{40,232},{48,240},{56,2... | collective-permute-start | bytes 196616 | tf_op jit(solution)/shard_map/ppermute | solution.py:220
  114.4 4.0 %collective-permute-done.12.refs_1_ = bf16[128,256]{1,0:T(8,128)(2,1)S(1)} collective-permute-done((bf16[128,256]{1,0:T(8,128)(2,1)S(1)}, bf16[128,256]{1,0:T(8,128)(2,1)S(1)}, u32[]{:S(2)}, u32[]{:S(2)}) %collective-permute-start.12) | collective-permute-done | bytes 65568 | tf_op jit(solution)/shard_map/ppermute | solution.py:220
  119.6 9.1 %all-to-all-start.3 = ((bf16[8,192,128]{2,1,0:T(8,128)(2,1)}), bf16[8,192,128]{2,1,0:T(8,128)(2,1)S(1)}, u32[]{:S(2)}, u32[]{:S(2)}) async-start(bf16[8,192,128]{2,1,0:T(8,128)(2,1)} %get-tuple-element.76), calls=%async_computation.3 | async-start | bytes 786432 | tf_op jit(solution)/shard_map/all_to_all | solution.py:425
  133.1 3.7 %all-to-all-done.3.late_ref = bf16[8,192,128]{2,1,0:T(8,128)(2,1)S(1)} async-done(((bf16[8,192,128]{2,1,0:T(8,128)(2,1)}), bf16[8,192,128]{2,1,0:T(8,128)(2,1)S(1)}, u32[]{:S(2)}, u32[]{:S(2)}) %all-to-all-start.3) | async-done | bytes 393248 | tf_op jit(solution)/shard_map/all_to_all | solution.py:425
  (69 shorter events, 26.5 us)
Async XLA Ops:
  11.9 10.4 %all-to-all-start = ((bf16[4,128,256]{2,1,0:T(8,128)(2,1)}), bf16[4,128,256]{2,1,0:T(8,128)(2,1)S(1)}, u32[]{:S(2)}, u32[]{:S(2)}) async-start(bf16[4,128,256]{2,1,0:T(8,128)(2,1)} %bitcast), calls=%async_computation | async-start | bytes 524288 | tf_op jit(solution)/shard_map/all_to_all | solution.py:200
  16.7 30.9 %collective-permute-start.6 = (bf16[512,384]{1,0:T(8,128)(2,1)S(1)}, bf16[512,384]{1,0:T(8,128)(2,1)S(1)}, u32[]{:S(2)}, u32[]{:S(2)}) collective-permute-start(bf16[512,384]{1,0:T(8,128)(2,1)S(1)} %get-tuple-element.62.refs_0_.both_ref), channel_id=1, source_target_pairs={{0,16},{8,24},{16,0},{24,8},{32,48},{40,56},{48,32},{56,40},{64,80... | collective-permute-start | bytes 1179656 | tf_op jit(solution)/shard_map/ppermute | solution.py:288
  22.3 25.3 %collective-permute-start.8 = (bf16[512,384]{1,0:T(8,128)(2,1)S(1)}, bf16[512,384]{1,0:T(8,128)(2,1)S(1)}, u32[]{:S(2)}, u32[]{:S(2)}) collective-permute-start(bf16[512,384]{1,0:T(8,128)(2,1)S(1)} %get-tuple-element.62.refs_0_.both_ref), channel_id=1, source_target_pairs={{0,128},{8,136},{16,144},{24,152},{32,160},{40,168},{48,176},{56,1... | collective-permute-start | bytes 1179656 | tf_op jit(solution)/shard_map/ppermute | solution.py:288
  22.8 24.8 %collective-permute-start.7 = (bf16[512,384]{1,0:T(8,128)(2,1)S(1)}, bf16[512,384]{1,0:T(8,128)(2,1)S(1)}, u32[]{:S(2)}, u32[]{:S(2)}) collective-permute-start(bf16[512,384]{1,0:T(8,128)(2,1)S(1)} %get-tuple-element.62.refs_0_.both_ref), channel_id=1, source_target_pairs={{0,64},{8,72},{16,80},{24,88},{32,96},{40,104},{48,112},{56,120},{... | collective-permute-start | bytes 1179656 | tf_op jit(solution)/shard_map/ppermute | solution.py:288
  23.9 4.7 %collective-permute-start = (bf16[128,256]{1,0:T(8,128)(2,1)S(1)}, bf16[128,256]{1,0:T(8,128)(2,1)S(1)}, u32[]{:S(2)}, u32[]{:S(2)}) collective-permute-start(bf16[128,256]{1,0:T(8,128)(2,1)S(1)} %param.1), channel_id=1, source_target_pairs={{0,8},{8,0},{16,24},{24,16},{32,40},{40,32},{48,56},{56,48},{64,72... | collective-permute-start | bytes 196616 | tf_op jit(solution)/shard_map/cond/branch_1_fun/ppermute | solution.py:237
  28.7 14.7 %collective-permute-start.1 = (bf16[128,256]{1,0:T(8,128)(2,1)S(1)}, bf16[128,256]{1,0:T(8,128)(2,1)S(1)}, u32[]{:S(2)}, u32[]{:S(2)}) collective-permute-start(bf16[128,256]{1,0:T(8,128)(2,1)S(1)} %add_convert_fusion.2), channel_id=1, source_target_pairs={{0,48},{8,56},{16,32},{24,40},{32,16},{40,24},{48,0},{56,8},{64,11... | collective-permute-start | bytes 196616 | tf_op jit(solution)/shard_map/cond/branch_1_fun/ppermute | solution.py:237
  43.4 4.2 %collective-permute-start.2 = (bf16[128,256]{1,0:T(8,128)(2,1)S(1)}, bf16[128,256]{1,0:T(8,128)(2,1)S(1)}, u32[]{:S(2)}, u32[]{:S(2)}) collective-permute-start(bf16[128,256]{1,0:T(8,128)(2,1)S(1)} %add_convert_fusion.1), channel_id=1, source_target_pairs={{0,16},{8,24},{16,0},{24,8},{32,48},{40,56},{48,32},{56,40},{64,80... | collective-permute-start | bytes 196616 | tf_op jit(solution)/shard_map/cond/branch_1_fun/ppermute | solution.py:237
  47.6 11.1 %collective-permute-start.9 = (bf16[512,384]{1,0:T(8,128)(2,1)S(1)}, bf16[512,384]{1,0:T(8,128)(2,1)S(1)}, u32[]{:S(2)}, u32[]{:S(2)}) collective-permute-start(bf16[512,384]{1,0:T(8,128)(2,1)S(1)} %get-tuple-element.62.refs_0_.both_ref), channel_id=1, source_target_pairs={{0,8},{8,0},{16,24},{24,16},{32,40},{40,32},{48,56},{56,48},{64,72... | collective-permute-start | bytes 1179656 | tf_op jit(solution)/shard_map/ppermute | solution.py:288
  47.9 10.7 %collective-permute-start.10 = (bf16[512,384]{1,0:T(8,128)(2,1)S(1)}, bf16[512,384]{1,0:T(8,128)(2,1)S(1)}, u32[]{:S(2)}, u32[]{:S(2)}) collective-permute-start(bf16[512,384]{1,0:T(8,128)(2,1)S(1)} %collective-permute-done.6.refs_2_), channel_id=1, source_target_pairs={{0,48},{8,56},{16,32},{24,40},{32,16},{40,24},{48,0},{56,8},{64,11... | collective-permute-start | bytes 1179656 | tf_op jit(solution)/shard_map/ppermute | solution.py:288
  48.7 10.0 %all-to-all-start.1 = ((bf16[4,128,256]{2,1,0:T(8,128)(2,1)}), bf16[4,128,256]{2,1,0:T(8,128)(2,1)S(1)}, u32[]{:S(2)}, u32[]{:S(2)}) async-start(bf16[4,128,256]{2,1,0:T(8,128)(2,1)} %broadcast_in_dim.2), calls=%async_computation.1 | async-start | bytes 524288 | tf_op jit(solution)/shard_map/all_to_all | solution.py:200
  67.2 13.3 %all-to-all-start.2 = ((bf16[4,128,256]{2,1,0:T(8,128)(2,1)}), bf16[4,128,256]{2,1,0:T(8,128)(2,1)}, u32[]{:S(2)}, u32[]{:S(2)}) async-start(bf16[4,128,256]{2,1,0:T(8,128)(2,1)} %bitcast.9), calls=%async_computation.2 | async-start | bytes 524288 | tf_op jit(solution)/shard_map/all_to_all | solution.py:200
  74.9 55.0 %reduce-scatter.2.cloned.1.call-start = ((), (), s32[]{:S(2)}) async-start(), calls=%async_computation.5 | async-start | bytes 6193152 | tf_op jit(solution)/shard_map/reduce_scatter | solution.py:395
  81.5 23.5 %collective-permute-start.11 = (bf16[512,384]{1,0:T(8,128)(2,1)S(1)}, bf16[512,384]{1,0:T(8,128)(2,1)S(1)}, u32[]{:S(2)}, u32[]{:S(2)}) collective-permute-start(bf16[512,384]{1,0:T(8,128)(2,1)S(1)} %copy-done.11), channel_id=1, source_target_pairs={{0,48},{8,56},{16,32},{24,40},{32,16},{40,24},{48,0},{56,8},{64,11... | collective-permute-start | bytes 1179656 | tf_op jit(solution)/shard_map/ppermute | solution.py:288
  86.0 4.5 %collective-permute-start.3 = (bf16[128,256]{1,0:T(8,128)(2,1)S(1)}, bf16[128,256]{1,0:T(8,128)(2,1)S(1)}, u32[]{:S(2)}, u32[]{:S(2)}) collective-permute-start(bf16[128,256]{1,0:T(8,128)(2,1)S(1)} %reduce_sum.22), channel_id=1, source_target_pairs={{0,16},{8,24},{16,0},{24,8},{32,48},{40,56},{48,32},{56,40},{64,80... | collective-permute-start | bytes 196616 | tf_op jit(solution)/shard_map/cond/branch_1_fun/ppermute | solution.py:237
  90.5 9.1 %collective-permute-start.4 = (bf16[128,256]{1,0:T(8,128)(2,1)S(1)}, bf16[128,256]{1,0:T(8,128)(2,1)S(1)}, u32[]{:S(2)}, u32[]{:S(2)}) collective-permute-start(bf16[128,256]{1,0:T(8,128)(2,1)S(1)} %add_convert_fusion.5), channel_id=1, source_target_pairs={{0,8},{8,0},{16,24},{24,16},{32,40},{40,32},{48,56},{56,48},{64,72... | collective-permute-start | bytes 196616 | tf_op jit(solution)/shard_map/cond/branch_1_fun/ppermute | solution.py:237
  99.6 5.4 %collective-permute-start.5 = (bf16[128,256]{1,0:T(8,128)(2,1)S(1)}, bf16[128,256]{1,0:T(8,128)(2,1)S(1)}, u32[]{:S(2)}, u32[]{:S(2)}) collective-permute-start(bf16[128,256]{1,0:T(8,128)(2,1)S(1)} %add_convert_fusion.4), channel_id=1, source_target_pairs={{0,48},{8,56},{16,32},{24,40},{32,16},{40,24},{48,0},{56,8},{64,11... | collective-permute-start | bytes 196616 | tf_op jit(solution)/shard_map/cond/branch_1_fun/ppermute | solution.py:237
  105.1 6.5 %collective-permute-start.14 = (bf16[128,256]{1,0:T(8,128)(2,1)S(1)}, bf16[128,256]{1,0:T(8,128)(2,1)S(1)}, u32[]{:S(2)}, u32[]{:S(2)}) collective-permute-start(bf16[128,256]{1,0:T(8,128)(2,1)S(1)} %get-tuple-element.99.refs_0_), channel_id=1, source_target_pairs={{0,192},{8,200},{16,208},{24,216},{32,224},{40,232},{48,240},{56,2... | collective-permute-start | bytes 196616 | tf_op jit(solution)/shard_map/ppermute | solution.py:220
  107.7 5.8 %collective-permute-start.13 = (bf16[128,256]{1,0:T(8,128)(2,1)S(1)}, bf16[128,256]{1,0:T(8,128)(2,1)S(1)}, u32[]{:S(2)}, u32[]{:S(2)}) collective-permute-start(bf16[128,256]{1,0:T(8,128)(2,1)S(1)} %get-tuple-element.99.refs_0_), channel_id=1, source_target_pairs={{0,128},{8,136},{16,144},{24,152},{32,160},{40,168},{48,176},{56,1... | collective-permute-start | bytes 196616 | tf_op jit(solution)/shard_map/ppermute | solution.py:220
  109.5 8.9 %collective-permute-start.12 = (bf16[128,256]{1,0:T(8,128)(2,1)S(1)}, bf16[128,256]{1,0:T(8,128)(2,1)S(1)}, u32[]{:S(2)}, u32[]{:S(2)}) collective-permute-start(bf16[128,256]{1,0:T(8,128)(2,1)S(1)} %get-tuple-element.99.refs_0_), channel_id=1, source_target_pairs={{0,64},{8,72},{16,80},{24,88},{32,96},{40,104},{48,112},{56,120},{... | collective-permute-start | bytes 196616 | tf_op jit(solution)/shard_map/ppermute | solution.py:220
  109.5 22.5 %collective-permute-start.18 = (bf16[512,384]{1,0:T(8,128)(2,1)}, bf16[512,384]{1,0:T(8,128)(2,1)S(1)}, u32[]{:S(2)}, u32[]{:S(2)}) collective-permute-start(bf16[512,384]{1,0:T(8,128)(2,1)} %get-tuple-element.82), channel_id=1, source_target_pairs={{0,128},{8,136},{16,144},{24,152},{32,160},{40,168},{48,176},{56,1... | collective-permute-start | bytes 1179656 | tf_op jit(solution)/shard_map/ppermute | solution.py:288
  111.5 20.5 %collective-permute-start.16 = (bf16[512,384]{1,0:T(8,128)(2,1)S(1)}, bf16[512,384]{1,0:T(8,128)(2,1)S(1)}, u32[]{:S(2)}, u32[]{:S(2)}) collective-permute-start(bf16[512,384]{1,0:T(8,128)(2,1)S(1)} %add_convert_fusion.6), channel_id=1, source_target_pairs={{0,16},{8,24},{16,0},{24,8},{32,48},{40,56},{48,32},{56,40},{64,80... | collective-permute-start | bytes 1179656 | tf_op jit(solution)/shard_map/ppermute | solution.py:288
  111.6 20.4 %collective-permute-start.15 = (bf16[512,384]{1,0:T(8,128)(2,1)}, bf16[512,384]{1,0:T(8,128)(2,1)S(1)}, u32[]{:S(2)}, u32[]{:S(2)}) collective-permute-start(bf16[512,384]{1,0:T(8,128)(2,1)} %get-tuple-element.78), channel_id=1, source_target_pairs={{0,8},{8,0},{16,24},{24,16},{32,40},{40,32},{48,56},{56,48},{64,72... | collective-permute-start | bytes 1179656 | tf_op jit(solution)/shard_map/ppermute | solution.py:288
  113.4 18.5 %collective-permute-start.17 = (bf16[512,384]{1,0:T(8,128)(2,1)}, bf16[512,384]{1,0:T(8,128)(2,1)S(1)}, u32[]{:S(2)}, u32[]{:S(2)}) collective-permute-start(bf16[512,384]{1,0:T(8,128)(2,1)} %get-tuple-element.81), channel_id=1, source_target_pairs={{0,64},{8,72},{16,80},{24,88},{32,96},{40,104},{48,112},{56,120},{... | collective-permute-start | bytes 1179656 | tf_op jit(solution)/shard_map/ppermute | solution.py:288
  119.6 17.2 %all-to-all-start.3 = ((bf16[8,192,128]{2,1,0:T(8,128)(2,1)}), bf16[8,192,128]{2,1,0:T(8,128)(2,1)S(1)}, u32[]{:S(2)}, u32[]{:S(2)}) async-start(bf16[8,192,128]{2,1,0:T(8,128)(2,1)} %get-tuple-element.76), calls=%async_computation.3 | async-start | bytes 786432 | tf_op jit(solution)/shard_map/all_to_all | solution.py:425
  (12 other events, 235.4 us)
Sparse Core Ops, SparseCore 0:
  80.7 49.2 reduce-scatter.1

commit v8 on v7

--- a/solution.py
+++ b/solution.py
@@ -304,7 +304,7 @@
     x_one = swap(both_x, 8)
     x_two = swap(both_x, 16)
     total, z_two, x_one, x_two, both_z = tie(
-        (line_sum(total, (1, 6, 2)), z_two, x_one, x_two, both)
+        (line_sum(total, (6, 1, 2)), z_two, x_one, x_two, both)
     )
     z_four = swap(z_two, 6)
     z_one = swap(both_z, 1)

time: 146 us -> 148 us (1.014)
  starting transfers between devices: 60.1 us -> 68 us
  waiting for transfers between devices: 43.4 us -> 37.9 us
    ppermute x6, waiting for transfers between devices: 26.2 us -> 20.2 us  [line_step(): other = lax.ppermute(held, 'hid', [(i, i ^ distance) for i in range(count)])]
    ppermute x6, starting transfers between devices: 16.4 us -> 21.1 us  [line_step(): other = lax.ppermute(held, 'hid', [(i, i ^ distance) for i in range(count)])]
    ppermute x10, waiting for transfers between devices: 0.03 us -> 4.63 us  [swap(): lax.ppermute(value, 'hid', [(i, i ^ distance) for i in range(hid_count)])]
    ppermute x10, starting transfers between devices: 13.1 us -> 17.5 us  [swap(): lax.ppermute(value, 'hid', [(i, i ^ distance) for i in range(hid_count)])]
    ppermute x3, waiting for transfers between devices: 4.02 us -> 0.01 us  [outer_shift(): lax.ppermute(value, 'hid', [(i, (i + step * inner) % count) for i in rang...]
    all_to_all x3, starting transfers between devices: 17 us -> 13.3 us  [group_exchange(): lax.all_to_all(pieces, 'hid', 0, 0, axis_index_groups=groups, tiled=True)]
    all_to_all x1, starting transfers between devices: 9.13 us -> 12.7 us  [on_device(): moved = lax.all_to_all(moved, 'tok', 0, 0, tiled=True)]
  transfers between devices with their start and end apart: 24 -> 24, of which waited for: 12 -> 11; matrix products, arithmetic and copies ran while one was open for 1% -> 1% of each run, Pallas kernels for 4% -> 4%
where the time goes in v8:
time: 148 us; the launch traced here: 147 us
  starting transfers between devices  68 us (46%)
  waiting for transfers between devices  37.9 us (26%)
  Pallas kernels  16.4 us (11%)
  between operations  14.2 us (10%)
  local copies, waits for them, and re-layouts  8.98 us (6%)
    ppermute x6, starting transfers between devices, line_step(): other = lax.ppermute(held, 'hid', [(i, i ^ distance) for i in range(count)])  21.1 us
    ppermute x6, waiting for transfers between devices, line_step(): other = lax.ppermute(held, 'hid', [(i, i ^ distance) for i in range(count)])  20.2 us
    ppermute x10, starting transfers between devices, swap(): lax.ppermute(value, 'hid', [(i, i ^ distance) for i in range(hid_count)])  17.5 us
    all_to_all x3, starting transfers between devices, group_exchange(): lax.all_to_all(pieces, 'hid', 0, 0, axis_index_groups=groups, tiled=True)  13.3 us
    all_to_all x1, starting transfers between devices, on_device(): moved = lax.all_to_all(moved, 'tok', 0, 0, tiled=True)  12.7 us
    pallas_call x1, Pallas kernels, on_device(): pl.pallas_call(functools.partial(middle_kernel, levels), grid_spec=pltpu....  8.56 us
    unnamed x25, local copies, waits for them, and re-layouts  8.26 us
    all_to_all x3, waiting for transfers between devices, group_exchange(): lax.all_to_all(pieces, 'hid', 0, 0, axis_index_groups=groups, tiled=True)  8.17 us
  transfers between devices with their start and end apart: 24, of which 11 were waited for; matrix products, arithmetic and copies ran while one was open for 1% of the time, Pallas kernels for 4%

profile of v8, /device:TPU:1, one launch (start us, length us, event | category | flops | bytes accessed | tf_op | source)
XLA Modules:
  0.0 146.8 jit_solution(16856119841074653905)
XLA Ops:
  11.9 4.8 %all-to-all-start = ((bf16[4,128,256]{2,1,0:T(8,128)(2,1)}), bf16[4,128,256]{2,1,0:T(8,128)(2,1)S(1)}, u32[]{:S(2)}, u32[]{:S(2)}) async-start(bf16[4,128,256]{2,1,0:T(8,128)(2,1)} %bitcast), calls=%async_computation | async-start | bytes 524288 | tf_op jit(solution)/shard_map/all_to_all | solution.py:200
  16.7 3.0 %collective-permute-start.6 = (bf16[512,384]{1,0:T(8,128)(2,1)S(1)}, bf16[512,384]{1,0:T(8,128)(2,1)S(1)}, u32[]{:S(2)}, u32[]{:S(2)}) collective-permute-start(bf16[512,384]{1,0:T(8,128)(2,1)S(1)} %get-tuple-element.62.refs_0_.both_ref), channel_id=1, source_target_pairs={{0,16},{8,24},{16,0},{24,8},{32,48},{40,56},{48,32},{56,40},{64,80... | collective-permute-start | bytes 1179656 | tf_op jit(solution)/shard_map/ppermute | solution.py:288
  19.7 2.5 %all-to-all-done = bf16[4,128,256]{2,1,0:T(8,128)(2,1)S(1)} async-done(((bf16[4,128,256]{2,1,0:T(8,128)(2,1)}), bf16[4,128,256]{2,1,0:T(8,128)(2,1)S(1)}, u32[]{:S(2)}, u32[]{:S(2)}) %all-to-all-start) | async-done | bytes 262176 | tf_op jit(solution)/shard_map/all_to_all | solution.py:200
  23.9 22.6 %conditional.2 = (bf16[128,256]{1,0:T(8,128)(2,1)S(1)}) conditional(s32[]{:T(128)} %convert_element_type.73, () %tuple.27, bf16[128,256]{1,0:T(8,128)(2,1)S(1)} %reduce_sum.24), branch_computations={%region_1.0_spmd, %region_2.0_spmd} | conditional | flops 393216 | bytes 1376384 | solution.py:261
  23.9 6.0 %collective-permute-start = (bf16[128,256]{1,0:T(8,128)(2,1)S(1)}, bf16[128,256]{1,0:T(8,128)(2,1)S(1)}, u32[]{:S(2)}, u32[]{:S(2)}) collective-permute-start(bf16[128,256]{1,0:T(8,128)(2,1)S(1)} %param.1), channel_id=1, source_target_pairs={{0,48},{8,56},{16,32},{24,40},{32,16},{40,24},{48,0},{56,8},{64,11... | collective-permute-start | bytes 196616 | tf_op jit(solution)/shard_map/cond/branch_1_fun/ppermute | solution.py:237
  31.9 6.7 %collective-permute-start.1 = (bf16[128,256]{1,0:T(8,128)(2,1)S(1)}, bf16[128,256]{1,0:T(8,128)(2,1)S(1)}, u32[]{:S(2)}, u32[]{:S(2)}) collective-permute-start(bf16[128,256]{1,0:T(8,128)(2,1)S(1)} %add_convert_fusion.2), channel_id=1, source_target_pairs={{0,8},{8,0},{16,24},{24,16},{32,40},{40,32},{48,56},{56,48},{64,72... | collective-permute-start | bytes 196616 | tf_op jit(solution)/shard_map/cond/branch_1_fun/ppermute | solution.py:237
  40.6 3.5 %collective-permute-start.2 = (bf16[128,256]{1,0:T(8,128)(2,1)S(1)}, bf16[128,256]{1,0:T(8,128)(2,1)S(1)}, u32[]{:S(2)}, u32[]{:S(2)}) collective-permute-start(bf16[128,256]{1,0:T(8,128)(2,1)S(1)} %add_convert_fusion.1), channel_id=1, source_target_pairs={{0,16},{8,24},{16,0},{24,8},{32,48},{40,56},{48,32},{56,40},{64,80... | collective-permute-start | bytes 196616 | tf_op jit(solution)/shard_map/cond/branch_1_fun/ppermute | solution.py:237
  46.6 3.9 %collective-permute-start.10 = (bf16[512,384]{1,0:T(8,128)(2,1)S(1)}, bf16[512,384]{1,0:T(8,128)(2,1)S(1)}, u32[]{:S(2)}, u32[]{:S(2)}) collective-permute-start(bf16[512,384]{1,0:T(8,128)(2,1)S(1)} %collective-permute-done.6.refs_2_), channel_id=1, source_target_pairs={{0,48},{8,56},{16,32},{24,40},{32,16},{40,24},{48,0},{56,8},{64,11... | collective-permute-start | bytes 1179656 | tf_op jit(solution)/shard_map/ppermute | solution.py:288
  51.2 4.2 %all-to-all-start.1 = ((bf16[4,128,256]{2,1,0:T(8,128)(2,1)}), bf16[4,128,256]{2,1,0:T(8,128)(2,1)S(1)}, u32[]{:S(2)}, u32[]{:S(2)}) async-start(bf16[4,128,256]{2,1,0:T(8,128)(2,1)} %broadcast_in_dim.2), calls=%async_computation.1 | async-start | bytes 524288 | tf_op jit(solution)/shard_map/all_to_all | solution.py:200
  55.6 5.4 %all-to-all-done.1 = bf16[4,128,256]{2,1,0:T(8,128)(2,1)S(1)} async-done(((bf16[4,128,256]{2,1,0:T(8,128)(2,1)}), bf16[4,128,256]{2,1,0:T(8,128)(2,1)S(1)}, u32[]{:S(2)}, u32[]{:S(2)}) %all-to-all-start.1) | async-done | bytes 262176 | tf_op jit(solution)/shard_map/all_to_all | solution.py:200
  61.0 4.6 %collective-permute-done.10.refs_3_ = bf16[512,384]{1,0:T(8,128)(2,1)S(1)} collective-permute-done((bf16[512,384]{1,0:T(8,128)(2,1)S(1)}, bf16[512,384]{1,0:T(8,128)(2,1)S(1)}, u32[]{:S(2)}, u32[]{:S(2)}) %collective-permute-start.10) | collective-permute-done | bytes 393248 | tf_op jit(solution)/shard_map/ppermute | solution.py:288
  65.6 8.6 %middle.1 = (bf16[256,768]{1,0:T(8,128)(2,1)S(1)}, bf16[256,768]{1,0:T(8,128)(2,1)S(1)}, bf16[512,256]{1,0:T(8,128)(2,1)}, bf16[512,384]{1,0:T(8,128)(2,1)}, bf1...) custom-call(s32[6,3,2]{2,1,0:T(4,128)S(1)} %copy.17.index_ref, ...), custom_call_target="tpu_custom_call" | custom-call | flops 2818572288 | bytes 10485760 | tf_op jit(solution)/shard_map/middle/pallas_call | solution.py:322
  74.1 4.2 %all-to-all-start.2 = ((bf16[4,128,256]{2,1,0:T(8,128)(2,1)}), bf16[4,128,256]{2,1,0:T(8,128)(2,1)}, u32[]{:S(2)}, u32[]{:S(2)}) async-start(bf16[4,128,256]{2,1,0:T(8,128)(2,1)} %bitcast.9), calls=%async_computation.2 | async-start | bytes 524288 | tf_op jit(solution)/shard_map/all_to_all | solution.py:200
  78.4 3.0 %grads.1 = bf16[8,7,2,96,256]{4,3,2,1,0:T(8,128)(2,1)S(1)} custom-call(s32[6,3,2]{2,1,0:T(4,128)S(1)} %copy.17.index_ref, bf16[512,384]{1,0:T(8,128)(2,1)S(1)} %get-tuple-element.62.refs_0_.both_ref, bf16[512,384]{1,0:T(8,128)(2,1)S(1)} %collective-permute-done.9.refs_1_, bf16[512,384]{1,0:T(8,128)(2,1)S(1)} %collective-permute-done.6.refs_2_, ...), custom_call_target="tpu_custom_call" | custom-call | flops 1409286144 | bytes 10485760 | tf_op jit(solution)/shard_map/grads/pallas_call | solution.py:385
  81.4 2.4 %copy-done = bf16[8,7,2,96,256]{4,3,2,1,0:T(8,128)(2,1)} copy-done((bf16[8,7,2,96,256]{4,3,2,1,0:T(8,128)(2,1)}, bf16[8,7,2,96,256]{4,3,2,1,0:T(8,128)(2,1)S(1)}, u32[]{:S(2)}) %copy-start) | copy-done | bytes 5505048
  85.0 3.5 %collective-permute-start.11 = (bf16[512,384]{1,0:T(8,128)(2,1)S(1)}, bf16[512,384]{1,0:T(8,128)(2,1)S(1)}, u32[]{:S(2)}, u32[]{:S(2)}) collective-permute-start(bf16[512,384]{1,0:T(8,128)(2,1)S(1)} %copy-done.11), channel_id=1, source_target_pairs={{0,48},{8,56},{16,32},{24,40},{32,16},{40,24},{48,0},{56,8},{64,11... | collective-permute-start | bytes 1179656 | tf_op jit(solution)/shard_map/ppermute | solution.py:288
  88.5 19.9 %conditional.3 = (bf16[128,256]{1,0:T(8,128)(2,1)S(1)}) conditional(s32[]{:T(128)} %convert_element_type.73, () %tuple.26, bf16[4,128,256]{2,1,0:T(8,128)(2,1)} %all-to-all-done.2), branch_computations={%region_3.0_spmd, %region_4.6_spmd} | conditional | flops 491520 | bytes 1704066 | solution.py:261
  89.6 4.0 %collective-permute-done.3 = bf16[128,256]{1,0:T(8,128)(2,1)S(1)} collective-permute-done((bf16[128,256]{1,0:T(8,128)(2,1)S(1)}, bf16[128,256]{1,0:T(8,128)(2,1)S(1)}, u32[]{:S(2)}, u32[]{:S(2)}) %collective-permute-start.3) | collective-permute-done | bytes 65568 | tf_op jit(solution)/shard_map/cond/branch_1_fun/ppermute | solution.py:237
  93.7 4.8 %collective-permute-start.4 = (bf16[128,256]{1,0:T(8,128)(2,1)S(1)}, bf16[128,256]{1,0:T(8,128)(2,1)S(1)}, u32[]{:S(2)}, u32[]{:S(2)}) collective-permute-start(bf16[128,256]{1,0:T(8,128)(2,1)S(1)} %add_convert_fusion.5), channel_id=1, source_target_pairs={{0,8},{8,0},{16,24},{24,16},{32,40},{40,32},{48,56},{56,48},{64,72... | collective-permute-start | bytes 196616 | tf_op jit(solution)/shard_map/cond/branch_1_fun/ppermute | solution.py:237
  98.5 4.6 %collective-permute-done.4 = bf16[128,256]{1,0:T(8,128)(2,1)S(1)} collective-permute-done((bf16[128,256]{1,0:T(8,128)(2,1)S(1)}, bf16[128,256]{1,0:T(8,128)(2,1)S(1)}, u32[]{:S(2)}, u32[]{:S(2)}) %collective-permute-start.4) | collective-permute-done | bytes 65568 | tf_op jit(solution)/shard_map/cond/branch_1_fun/ppermute | solution.py:237
  103.2 5.2 %collective-permute-done.5 = bf16[128,256]{1,0:T(8,128)(2,1)S(1)} collective-permute-done((bf16[128,256]{1,0:T(8,128)(2,1)S(1)}, bf16[128,256]{1,0:T(8,128)(2,1)S(1)}, u32[]{:S(2)}, u32[]{:S(2)}) %collective-permute-start.5) | collective-permute-done | bytes 65568 | tf_op jit(solution)/shard_map/cond/branch_1_fun/ppermute | solution.py:237
  113.9 2.5 %collective-permute-start.16 = (bf16[512,384]{1,0:T(8,128)(2,1)S(1)}, bf16[512,384]{1,0:T(8,128)(2,1)S(1)}, u32[]{:S(2)}, u32[]{:S(2)}) collective-permute-start(bf16[512,384]{1,0:T(8,128)(2,1)S(1)} %add_convert_fusion.6), channel_id=1, source_target_pairs={{0,16},{8,24},{16,0},{24,8},{32,48},{40,56},{48,32},{56,40},{64,80... | collective-permute-start | bytes 1179656 | tf_op jit(solution)/shard_map/ppermute | solution.py:288
  118.5 12.7 %all-to-all-start.3 = ((bf16[8,192,128]{2,1,0:T(8,128)(2,1)}), bf16[8,192,128]{2,1,0:T(8,128)(2,1)S(1)}, u32[]{:S(2)}, u32[]{:S(2)}) async-start(bf16[8,192,128]{2,1,0:T(8,128)(2,1)} %get-tuple-element.76), calls=%async_computation.3 | async-start | bytes 786432 | tf_op jit(solution)/shard_map/all_to_all | solution.py:425
  134.3 4.9 %all-to-all-done.3.late_ref = bf16[8,192,128]{2,1,0:T(8,128)(2,1)S(1)} async-done(((bf16[8,192,128]{2,1,0:T(8,128)(2,1)}), bf16[8,192,128]{2,1,0:T(8,128)(2,1)S(1)}, u32[]{:S(2)}, u32[]{:S(2)}) %all-to-all-start.3) | async-done | bytes 393248 | tf_op jit(solution)/shard_map/all_to_all | solution.py:425
  (69 shorter events, 27.4 us)
Async XLA Ops:
  11.9 10.4 %all-to-all-start = ((bf16[4,128,256]{2,1,0:T(8,128)(2,1)}), bf16[4,128,256]{2,1,0:T(8,128)(2,1)S(1)}, u32[]{:S(2)}, u32[]{:S(2)}) async-start(bf16[4,128,256]{2,1,0:T(8,128)(2,1)} %bitcast), calls=%async_computation | async-start | bytes 524288 | tf_op jit(solution)/shard_map/all_to_all | solution.py:200
  16.7 29.7 %collective-permute-start.6 = (bf16[512,384]{1,0:T(8,128)(2,1)S(1)}, bf16[512,384]{1,0:T(8,128)(2,1)S(1)}, u32[]{:S(2)}, u32[]{:S(2)}) collective-permute-start(bf16[512,384]{1,0:T(8,128)(2,1)S(1)} %get-tuple-element.62.refs_0_.both_ref), channel_id=1, source_target_pairs={{0,16},{8,24},{16,0},{24,8},{32,48},{40,56},{48,32},{56,40},{64,80... | collective-permute-start | bytes 1179656 | tf_op jit(solution)/shard_map/ppermute | solution.py:288
  22.3 24.2 %collective-permute-start.8 = (bf16[512,384]{1,0:T(8,128)(2,1)S(1)}, bf16[512,384]{1,0:T(8,128)(2,1)S(1)}, u32[]{:S(2)}, u32[]{:S(2)}) collective-permute-start(bf16[512,384]{1,0:T(8,128)(2,1)S(1)} %get-tuple-element.62.refs_0_.both_ref), channel_id=1, source_target_pairs={{0,128},{8,136},{16,144},{24,152},{32,160},{40,168},{48,176},{56,1... | collective-permute-start | bytes 1179656 | tf_op jit(solution)/shard_map/ppermute | solution.py:288
  22.8 23.7 %collective-permute-start.7 = (bf16[512,384]{1,0:T(8,128)(2,1)S(1)}, bf16[512,384]{1,0:T(8,128)(2,1)S(1)}, u32[]{:S(2)}, u32[]{:S(2)}) collective-permute-start(bf16[512,384]{1,0:T(8,128)(2,1)S(1)} %get-tuple-element.62.refs_0_.both_ref), channel_id=1, source_target_pairs={{0,64},{8,72},{16,80},{24,88},{32,96},{40,104},{48,112},{56,120},{... | collective-permute-start | bytes 1179656 | tf_op jit(solution)/shard_map/ppermute | solution.py:288
  23.9 7.9 %collective-permute-start = (bf16[128,256]{1,0:T(8,128)(2,1)S(1)}, bf16[128,256]{1,0:T(8,128)(2,1)S(1)}, u32[]{:S(2)}, u32[]{:S(2)}) collective-permute-start(bf16[128,256]{1,0:T(8,128)(2,1)S(1)} %param.1), channel_id=1, source_target_pairs={{0,48},{8,56},{16,32},{24,40},{32,16},{40,24},{48,0},{56,8},{64,11... | collective-permute-start | bytes 196616 | tf_op jit(solution)/shard_map/cond/branch_1_fun/ppermute | solution.py:237
  31.9 8.7 %collective-permute-start.1 = (bf16[128,256]{1,0:T(8,128)(2,1)S(1)}, bf16[128,256]{1,0:T(8,128)(2,1)S(1)}, u32[]{:S(2)}, u32[]{:S(2)}) collective-permute-start(bf16[128,256]{1,0:T(8,128)(2,1)S(1)} %add_convert_fusion.2), channel_id=1, source_target_pairs={{0,8},{8,0},{16,24},{24,16},{32,40},{40,32},{48,56},{56,48},{64,72... | collective-permute-start | bytes 196616 | tf_op jit(solution)/shard_map/cond/branch_1_fun/ppermute | solution.py:237
  40.6 5.9 %collective-permute-start.2 = (bf16[128,256]{1,0:T(8,128)(2,1)S(1)}, bf16[128,256]{1,0:T(8,128)(2,1)S(1)}, u32[]{:S(2)}, u32[]{:S(2)}) collective-permute-start(bf16[128,256]{1,0:T(8,128)(2,1)S(1)} %add_convert_fusion.1), channel_id=1, source_target_pairs={{0,16},{8,24},{16,0},{24,8},{32,48},{40,56},{48,32},{56,40},{64,80... | collective-permute-start | bytes 196616 | tf_op jit(solution)/shard_map/cond/branch_1_fun/ppermute | solution.py:237
  46.5 14.5 %collective-permute-start.9 = (bf16[512,384]{1,0:T(8,128)(2,1)S(1)}, bf16[512,384]{1,0:T(8,128)(2,1)S(1)}, u32[]{:S(2)}, u32[]{:S(2)}) collective-permute-start(bf16[512,384]{1,0:T(8,128)(2,1)S(1)} %get-tuple-element.62.refs_0_.both_ref), channel_id=1, source_target_pairs={{0,8},{8,0},{16,24},{24,16},{32,40},{40,32},{48,56},{56,48},{64,72... | collective-permute-start | bytes 1179656 | tf_op jit(solution)/shard_map/ppermute | solution.py:288
  46.6 19.0 %collective-permute-start.10 = (bf16[512,384]{1,0:T(8,128)(2,1)S(1)}, bf16[512,384]{1,0:T(8,128)(2,1)S(1)}, u32[]{:S(2)}, u32[]{:S(2)}) collective-permute-start(bf16[512,384]{1,0:T(8,128)(2,1)S(1)} %collective-permute-done.6.refs_2_), channel_id=1, source_target_pairs={{0,48},{8,56},{16,32},{24,40},{32,16},{40,24},{48,0},{56,8},{64,11... | collective-permute-start | bytes 1179656 | tf_op jit(solution)/shard_map/ppermute | solution.py:288
  51.2 9.8 %all-to-all-start.1 = ((bf16[4,128,256]{2,1,0:T(8,128)(2,1)}), bf16[4,128,256]{2,1,0:T(8,128)(2,1)S(1)}, u32[]{:S(2)}, u32[]{:S(2)}) async-start(bf16[4,128,256]{2,1,0:T(8,128)(2,1)} %broadcast_in_dim.2), calls=%async_computation.1 | async-start | bytes 524288 | tf_op jit(solution)/shard_map/all_to_all | solution.py:200
  74.1 9.9 %all-to-all-start.2 = ((bf16[4,128,256]{2,1,0:T(8,128)(2,1)}), bf16[4,128,256]{2,1,0:T(8,128)(2,1)}, u32[]{:S(2)}, u32[]{:S(2)}) async-start(bf16[4,128,256]{2,1,0:T(8,128)(2,1)} %bitcast.9), calls=%async_computation.2 | async-start | bytes 524288 | tf_op jit(solution)/shard_map/all_to_all | solution.py:200
  78.4 52.8 %reduce-scatter.2.cloned.1.call-start = ((), (), s32[]{:S(2)}) async-start(), calls=%async_computation.5 | async-start | bytes 6193152 | tf_op jit(solution)/shard_map/reduce_scatter | solution.py:395
  85.0 23.4 %collective-permute-start.11 = (bf16[512,384]{1,0:T(8,128)(2,1)S(1)}, bf16[512,384]{1,0:T(8,128)(2,1)S(1)}, u32[]{:S(2)}, u32[]{:S(2)}) collective-permute-start(bf16[512,384]{1,0:T(8,128)(2,1)S(1)} %copy-done.11), channel_id=1, source_target_pairs={{0,48},{8,56},{16,32},{24,40},{32,16},{40,24},{48,0},{56,8},{64,11... | collective-permute-start | bytes 1179656 | tf_op jit(solution)/shard_map/ppermute | solution.py:288
  89.5 4.1 %collective-permute-start.3 = (bf16[128,256]{1,0:T(8,128)(2,1)S(1)}, bf16[128,256]{1,0:T(8,128)(2,1)S(1)}, u32[]{:S(2)}, u32[]{:S(2)}) collective-permute-start(bf16[128,256]{1,0:T(8,128)(2,1)S(1)} %reduce_sum.22), channel_id=1, source_target_pairs={{0,16},{8,24},{16,0},{24,8},{32,48},{40,56},{48,32},{56,40},{64,80... | collective-permute-start | bytes 196616 | tf_op jit(solution)/shard_map/cond/branch_1_fun/ppermute | solution.py:237
  93.7 9.4 %collective-permute-start.4 = (bf16[128,256]{1,0:T(8,128)(2,1)S(1)}, bf16[128,256]{1,0:T(8,128)(2,1)S(1)}, u32[]{:S(2)}, u32[]{:S(2)}) collective-permute-start(bf16[128,256]{1,0:T(8,128)(2,1)S(1)} %add_convert_fusion.5), channel_id=1, source_target_pairs={{0,8},{8,0},{16,24},{24,16},{32,40},{40,32},{48,56},{56,48},{64,72... | collective-permute-start | bytes 196616 | tf_op jit(solution)/shard_map/cond/branch_1_fun/ppermute | solution.py:237
  103.1 5.3 %collective-permute-start.5 = (bf16[128,256]{1,0:T(8,128)(2,1)S(1)}, bf16[128,256]{1,0:T(8,128)(2,1)S(1)}, u32[]{:S(2)}, u32[]{:S(2)}) collective-permute-start(bf16[128,256]{1,0:T(8,128)(2,1)S(1)} %add_convert_fusion.4), channel_id=1, source_target_pairs={{0,48},{8,56},{16,32},{24,40},{32,16},{40,24},{48,0},{56,8},{64,11... | collective-permute-start | bytes 196616 | tf_op jit(solution)/shard_map/cond/branch_1_fun/ppermute | solution.py:237
  108.4 8.0 %collective-permute-start.14 = (bf16[128,256]{1,0:T(8,128)(2,1)S(1)}, bf16[128,256]{1,0:T(8,128)(2,1)S(1)}, u32[]{:S(2)}, u32[]{:S(2)}) collective-permute-start(bf16[128,256]{1,0:T(8,128)(2,1)S(1)} %get-tuple-element.99.refs_0_), channel_id=1, source_target_pairs={{0,192},{8,200},{16,208},{24,216},{32,224},{40,232},{48,240},{56,2... | collective-permute-start | bytes 196616 | tf_op jit(solution)/shard_map/ppermute | solution.py:220
  110.8 5.6 %collective-permute-start.13 = (bf16[128,256]{1,0:T(8,128)(2,1)S(1)}, bf16[128,256]{1,0:T(8,128)(2,1)S(1)}, u32[]{:S(2)}, u32[]{:S(2)}) collective-permute-start(bf16[128,256]{1,0:T(8,128)(2,1)S(1)} %get-tuple-element.99.refs_0_), channel_id=1, source_target_pairs={{0,128},{8,136},{16,144},{24,152},{32,160},{40,168},{48,176},{56,1... | collective-permute-start | bytes 196616 | tf_op jit(solution)/shard_map/ppermute | solution.py:220
  111.1 6.3 %collective-permute-start.12 = (bf16[128,256]{1,0:T(8,128)(2,1)S(1)}, bf16[128,256]{1,0:T(8,128)(2,1)S(1)}, u32[]{:S(2)}, u32[]{:S(2)}) collective-permute-start(bf16[128,256]{1,0:T(8,128)(2,1)S(1)} %get-tuple-element.99.refs_0_), channel_id=1, source_target_pairs={{0,64},{8,72},{16,80},{24,88},{32,96},{40,104},{48,112},{56,120},{... | collective-permute-start | bytes 196616 | tf_op jit(solution)/shard_map/ppermute | solution.py:220
  111.9 21.3 %collective-permute-start.18 = (bf16[512,384]{1,0:T(8,128)(2,1)}, bf16[512,384]{1,0:T(8,128)(2,1)S(1)}, u32[]{:S(2)}, u32[]{:S(2)}) collective-permute-start(bf16[512,384]{1,0:T(8,128)(2,1)} %get-tuple-element.82), channel_id=1, source_target_pairs={{0,128},{8,136},{16,144},{24,152},{32,160},{40,168},{48,176},{56,1... | collective-permute-start | bytes 1179656 | tf_op jit(solution)/shard_map/ppermute | solution.py:288
  113.9 19.3 %collective-permute-start.16 = (bf16[512,384]{1,0:T(8,128)(2,1)S(1)}, bf16[512,384]{1,0:T(8,128)(2,1)S(1)}, u32[]{:S(2)}, u32[]{:S(2)}) collective-permute-start(bf16[512,384]{1,0:T(8,128)(2,1)S(1)} %add_convert_fusion.6), channel_id=1, source_target_pairs={{0,16},{8,24},{16,0},{24,8},{32,48},{40,56},{48,32},{56,40},{64,80... | collective-permute-start | bytes 1179656 | tf_op jit(solution)/shard_map/ppermute | solution.py:288
  116.4 16.8 %collective-permute-start.15 = (bf16[512,384]{1,0:T(8,128)(2,1)}, bf16[512,384]{1,0:T(8,128)(2,1)S(1)}, u32[]{:S(2)}, u32[]{:S(2)}) collective-permute-start(bf16[512,384]{1,0:T(8,128)(2,1)} %get-tuple-element.78), channel_id=1, source_target_pairs={{0,8},{8,0},{16,24},{24,16},{32,40},{40,32},{48,56},{56,48},{64,72... | collective-permute-start | bytes 1179656 | tf_op jit(solution)/shard_map/ppermute | solution.py:288
  116.4 16.8 %collective-permute-start.17 = (bf16[512,384]{1,0:T(8,128)(2,1)}, bf16[512,384]{1,0:T(8,128)(2,1)S(1)}, u32[]{:S(2)}, u32[]{:S(2)}) collective-permute-start(bf16[512,384]{1,0:T(8,128)(2,1)} %get-tuple-element.81), channel_id=1, source_target_pairs={{0,64},{8,72},{16,80},{24,88},{32,96},{40,104},{48,112},{56,120},{... | collective-permute-start | bytes 1179656 | tf_op jit(solution)/shard_map/ppermute | solution.py:288
  118.5 20.7 %all-to-all-start.3 = ((bf16[8,192,128]{2,1,0:T(8,128)(2,1)}), bf16[8,192,128]{2,1,0:T(8,128)(2,1)S(1)}, u32[]{:S(2)}, u32[]{:S(2)}) async-start(bf16[8,192,128]{2,1,0:T(8,128)(2,1)} %get-tuple-element.76), calls=%async_computation.3 | async-start | bytes 786432 | tf_op jit(solution)/shard_map/all_to_all | solution.py:425
  (12 other events, 229.9 us)
Sparse Core Ops, SparseCore 0:
  84.2 46.2 reduce-scatter.1
